TPU v7x, 32 devices: a whole 2x2x4 slice. The times are simulated.
32 devices in a mesh: orb: 8 (over y, x, core), grid: 4 (over z).
Axes of the slice: x: 2, y: 2, z: 4, core: 2. Of those that a mesh axis runs over, the one named last changes fastest.
Arguments:
- orbitals: float32 [128, 32, 4096], P('orb', 'grid'), may hold values from -6 to 6
- rotation: float32 [128, 128], replicated, may hold values from -0.5 to 0.5
- tile_list: int32 [4, 2], replicated, may hold values from 0 to 31, as said below
- pair_mask: int32 [128, 128], replicated, may hold values from 0 to 1, as said below
Outputs:
- exchange_term: float32 [128, 32, 4096], P('orb', 'grid')
Inputs may be any that keep to these rules, and one draw needn't show every extreme that they name: `tile_list`: row t names one tile: its target block and its source block of 4 orbitals each; no tile is named twice. `pair_mask`: among the 64 orbital pairs that lie in listed tiles, exactly 32 are 1.
All inputs are finite; a program needn't handle non-finite values.
Results may differ from a plain program's by a relative error of at most 0.0003.
Values sent between devices are 32-bit elements; how exact they have to be, the bound alone decides.
No kernel may reach another device: no remote copies, remote signals or barrier semaphores. Data moves between devices by JAX's collectives and lax.ppermute only.
A program may use at most 64 MiB of HBM per device.

v0:
```python
import functools
import itertools

import jax
import jax.numpy as jnp
import numpy as np
from jax import lax
from jax.experimental import pallas as pl
from jax.experimental.pallas import tpu as pltpu
from jax.sharding import PartitionSpec as P

BLK = 4
NY = 64
NZ = 64
LANES = 128
SUB = 8
CHUNKS = 2
COUPLING = 0.25
SCREENING = 0.1

precise = lax.Precision.HIGHEST
f32 = jnp.float32
bf16 = jnp.bfloat16

VM = pl.BlockSpec(memory_space=pltpu.VMEM)
SM = pl.BlockSpec(memory_space=pltpu.SMEM)
ANY = pl.BlockSpec(memory_space=pl.ANY)
HBM = pl.BlockSpec(memory_space=pltpu.HBM)
DMA = pltpu.SemaphoreType.DMA


def grant(mib):
    return pltpu.CompilerParams(vmem_limit_bytes=mib << 20)


def sine_np(n):
    k = np.arange(1, n + 1, dtype=np.float64)
    return np.sqrt(2.0 / (n + 1)) * np.sin(np.pi * k[:, None] * k[None, :] / (n + 1))


def eigen_np(n):
    k = np.arange(1, n + 1, dtype=np.float64)
    return 2.0 - 2.0 * np.cos(np.pi * k / (n + 1))


def halves_np(table):
    high = np.asarray(table, np.float32).astype(jnp.bfloat16)
    low = (np.asarray(table, np.float64) - high.astype(np.float64)).astype(jnp.bfloat16)
    return jnp.asarray(high), jnp.asarray(low)


def y_order():
    rows = LANES // NZ
    return np.arange(NY).reshape(NY // rows, rows).T.reshape(-1)


def y_table():
    order = y_order()
    return np.kron(sine_np(NY)[order][:, order], sine_np(SUB))


def z_table():
    half = LANES // NZ
    sine = sine_np(NZ)
    table = np.zeros((2, half, NZ, half, 2, NZ))
    for pair in range(2):
        for h in range(half):
            table[pair, h, :, h, pair, :] = sine
    return table.reshape(2 * half * NZ, half * 2 * NZ)


def line_np():
    c = eigen_np(NY)[y_order()][:, None] + eigen_np(NZ)[None, :] + SCREENING
    c = np.concatenate([c, c], axis=1)
    return c, 2.0 / (2.0 + c + np.sqrt(c * (c + 4.0)))


def host_np(chips):
    table = np.zeros((chips**chips, chips), np.int32)
    for owners in itertools.product(range(chips), repeat=chips):
        best = None
        for tiles in itertools.permutations(range(chips)):
            hops = [bin(chip ^ owners[tile]).count("1") for chip, tile in enumerate(tiles)]
            cost = (max(hops), sum(hops))
            if best is None or cost < best[0]:
                best = (cost, tiles)
        table[sum(own * chips**t for t, own in enumerate(owners))] = best[1]
    return table


def dot(a, b):
    return jnp.dot(a, b, preferred_element_type=f32)


def split(x):
    high = x.astype(bf16)
    return high, (x - high.astype(f32)).astype(bf16)


def dot3(a, b):
    return dot(a[0], b[0]) + dot(a[0], b[1]) + dot(a[1], b[0])


def my_core():
    return lax.rem(lax.axis_index("orb"), 2)


def my_place():
    o = lax.axis_index("orb")
    return o, lax.rem(o, 2), lax.div(o, 2)


def take_kernel(flip, start, source, *rest):
    out, sem = rest[-2:]
    core = my_core()
    side = 1 - core if flip else core
    at = pl.multiple_of(side * (source.shape[2] // 2) + start, LANES)
    copy = pltpu.make_async_copy(source.at[:, :, pl.ds(at, out.shape[2])], out, sem)
    copy.start()
    copy.wait()


def setup_kernel(per_device, tiles, host, rotation, mask, high, low, flags, match, alone):
    o, core, chip = my_place()
    chips = tiles.shape[0] // 2
    owners = [lax.div(tiles[2 * t] * BLK, 2 * per_device) for t in range(chips)]
    key = 0
    for t in range(chips):
        key = key + owners[t] * chips**t
    same = owners[0] == owners[1]
    for t in range(2, chips):
        same = same & (owners[t] == owners[0])
    alone[0] = same.astype(jnp.int32)
    bit_1 = jnp.where(core == 0, 1, 2)
    bit_2 = 3 - bit_1
    pair = BLK // 2
    order = [chip ^ 3, chip ^ bit_1, chip ^ bit_2, chip]
    heads = []
    for where in order:
        tile = host[key * chips + where]
        heads.append((BLK * tiles[2 * tile], BLK * tiles[2 * tile + 1]))
    wanted = []
    for a, b in heads:
        wanted += [a + (1 - core) * pair] + [b + w for w in range(BLK)] + [a + core * pair]
    for u in range(1, pair):
        for a, b in heads:
            wanted += [a + (1 - core) * pair + u, a + core * pair + u]
    lane = lax.broadcasted_iota(jnp.int32, (SUB, LANES), 1)
    chosen = jnp.concatenate([jnp.where(lane == n, 1.0, 0.0) for n in wanted]).astype(bf16)
    count = chosen.shape[0]
    row = lax.broadcasted_iota(jnp.int32, (LANES, LANES), 0)
    column = lax.broadcasted_iota(jnp.int32, (LANES, LANES), 1)
    columns = [
        jnp.where(row - (o ^ e) * per_device == jnp.right_shift(column, 3), 1.0, 0.0).astype(bf16)
        for e in range(2)
    ]
    keep = (lax.broadcasted_iota(jnp.int32, (count, LANES), 0) & (SUB - 1)) == (
        lax.broadcasted_iota(jnp.int32, (count, LANES), 1) & (SUB - 1)
    )
    for out, values in zip((high, low), split(rotation[...])):
        picked = lax.dot_general(chosen, values, (((1,), (1,)), ((), ())), preferred_element_type=f32).astype(bf16)
        for e in range(2):
            out[:, e * LANES:(e + 1) * LANES] = jnp.where(keep, dot(picked, columns[e]), 0.0).astype(bf16)
    a, b = heads[-1]
    live = mask[...].astype(f32)
    for u in range(pair):
        line = jnp.sum(jnp.where(row == a + core * pair + u, live, 0.0), axis=0, keepdims=True)
        for w in range(BLK):
            flags[u * BLK + w] = jnp.sum(jnp.where(column[:1] == b + w, line, 0.0))
    blocks = per_device // BLK
    parts = [chip, chip ^ bit_1, chip ^ bit_2, chip ^ 3, chip, chip ^ bit_2, chip ^ bit_1, chip ^ 3]
    for n, where in enumerate(parts):
        home = tiles[2 * host[key * chips + where]]
        for block in range(blocks):
            hit = home == o * blocks + block
            if n % 4 == 3:
                hit = hit & same
            match[block * len(parts) + n] = hit.astype(jnp.int32)


def rotate_kernel(first, high, low, *rest):
    send, keep = rest[-2:]
    rows = send.shape[0] * SUB
    part = pl.ds(first, 2 * rows)
    table = (high[part, :], low[part, :])
    at = 0
    step = 2 * LANES
    while at < send.shape[2]:
        width = rest[0].shape[2]
        n, inner = at // width, at % width
        lanes = slice(inner, inner + step)
        mine, theirs = rest[2 * n], rest[2 * n + 1]
        depth = mine.shape[0] * SUB
        cells = jnp.concatenate([mine[:, :, lanes].reshape(depth, step), theirs[:, :, lanes].reshape(depth, step)])
        total = dot3(table, split(cells))
        lanes = slice(at, at + step)
        send[:, :, lanes] = total[:rows].reshape(send.shape[0], SUB, step)
        keep[:, :, lanes] = total[rows:].reshape(keep.shape[0], SUB, step)
        at += step


def pass_kernel(keep, got, *rest):
    out = rest[-1]
    count = out.shape[0]
    out[...] = keep[:count] + got[:count]


def finish_kernel(keep, got, passed, *rest):
    out = rest[-1]
    count = out.shape[0]
    out[...] = keep[count:] + got[count:] + passed[...]


def clear_kernel(*refs):
    out, zeros, sem = refs[-3:]
    zeros[...] = jnp.zeros(zeros.shape, f32)
    step = zeros.shape[0]
    copies = [
        pltpu.make_async_copy(zeros, out.at[pl.ds(n * step, step)], sem.at[n]) for n in range(out.shape[0] // step)
    ]
    for copy in copies:
        copy.start()
    for copy in copies:
        copy.wait()


def sub_sums(values):
    row = lax.broadcasted_iota(jnp.int32, values[0].shape, 0)
    for s in (4, 2):
        low = (row & s) == 0
        paired = []
        for n in range(s):
            a, b = values[n], values[n + s]
            paired.append(jnp.where(low, a, pltpu.roll(b, s, 0)) + jnp.where(low, pltpu.roll(a, SUB - s, 0), b))
        values = paired
    even = (row & 1) == 0
    a, b = values
    return jnp.where(even, a, pltpu.roll(b, 1, 0)), jnp.where(even, pltpu.roll(a, SUB - 1, 0), b)


def fields(u, own, other, first_own, first_other):
    table = []
    for side, sources, targets in ((0, first_own, own), (1, first_other, other)):
        for n, ref in enumerate(sources):
            if u == 0:
                table.append((side, n, ref, targets[n], BLK + 1 if side == 0 else 0, 0))
            else:
                table.append((side, n, ref, targets[0], 1 if side == 0 else 0, n * ref.shape[2]))
    return table


def forward_kernel(u, counts, *refs):
    groups = []
    for count in counts[:-1]:
        groups.append(refs[:count])
        refs = refs[count:]
    first_own, first_other, own, other = groups[:4]
    y_hi, y_lo, z_hi, z_lo, ends, powers = refs[:6]
    messages, (spectrum, a_out, b_out, dens) = refs[-4 - counts[-1]:-4], refs[-4:]
    if u == 0:
        own, other = first_own, first_other
    core, g = my_core(), lax.axis_index("grid")
    tiles = first_own[0].shape[2] // LANES
    for side, n, source, target, slot, offset in fields(u, own, other, first_own, first_other):
        half = (core if side == 0 else 1 - core) * (len(first_own) * tiles * SUB)
        for t in range(tiles):
            lanes = pl.ds(t * LANES, LANES)
            value = target[slot, :, pl.ds(offset + t * LANES, LANES)]
            rows = pl.ds(pl.multiple_of(half + (n * tiles + t) * SUB, SUB), SUB)
            for w in range(BLK):
                dens[rows, w * LANES:(w + 1) * LANES] = value * source[1 + w, :, lanes]
    z = (z_hi[...], z_lo[...])
    half = dens.shape[0]
    for q in range(BLK // 2):
        out = dot3(split(dens[:, q * 2 * LANES:(q + 1) * 2 * LANES]), z)
        spectrum[:half, q * LANES:(q + 1) * LANES] = out[:, :LANES]
        spectrum[half:, q * LANES:(q + 1) * LANES] = out[:, LANES:]
    spectrum[...] = dot3((y_hi[...], y_lo[...]), split(spectrum[...]))

    def reduce(group, carry):
        lines = pl.ds(pl.multiple_of(group * SUB, SUB), SUB)
        near, far = powers[0, lines, :], powers[1, lines, :]
        for q in range(BLK // 2):
            lanes = slice(q * LANES, (q + 1) * LANES)
            values = []
            for k in range(SUB):
                rows = pl.ds(pl.multiple_of((group * SUB + k) * SUB, SUB), SUB)
                values.append(ends[rows, :] * spectrum[rows, lanes])
            even, odd = sub_sums(values)
            rightward = (even + odd) - near * (even - odd)
            leftward = (even - odd) - far * (even + odd)
            a_out[lines, lanes] = rightward
            b_out[lines, lanes] = leftward
            for k, out in enumerate(messages, 1):
                out[lines, lanes] = jnp.where((g ^ k) > g, rightward, leftward)
        return carry

    lax.fori_loop(0, NY // SUB, reduce, 0)


def backward_kernel(u, counts, flags, *refs):
    groups = []
    for count in counts:
        groups.append(refs[:count])
        refs = refs[count:]
    own, other, received = groups
    (y_hi, y_lo, z_hi, z_lo, inverse, basis, powers, steady, spectrum, a_in, b_in) = refs[:11]
    out, work, pot = refs[-3:]
    core, g = my_core(), lax.axis_index("grid")
    tiles = own[0].shape[2] // LANES
    first, last = basis[0], basis[1]

    def ends(group, carry):
        lines = pl.ds(pl.multiple_of(group * SUB, SUB), SUB)
        scale, r, slab = steady[0, lines, :], steady[1, lines, :], steady[2, lines, :]
        decays = [None, jnp.ones((SUB, LANES), f32), slab]
        while len(decays) <= len(received):
            decays.append(decays[-1] * slab)
        for q in range(BLK // 2):
            lanes = slice(q * LANES, (q + 1) * LANES)
            from_left = from_right = jnp.zeros((SUB, LANES), f32)
            for n, ref in enumerate(received, 1):
                distance = jnp.abs((g ^ n) - g)
                factor = decays[n]
                for d in range(1, n):
                    factor = jnp.where(distance == d, decays[d], factor)
                value = factor * ref[lines, lanes]
                is_left = (g ^ n) < g
                from_left = from_left + jnp.where(is_left, value, 0.0)
                from_right = from_right + jnp.where(is_left, 0.0, value)
            before = scale * (powers[2, lines, :] * from_left
                              + r * powers[3, lines, :] * (b_in[lines, lanes] + slab * from_right))
            after = scale * (powers[4, lines, :] * from_right
                             + r * powers[5, lines, :] * (a_in[lines, lanes] + slab * from_left))
            for k in range(SUB):
                rows = pl.ds(pl.multiple_of((group * SUB + k) * SUB, SUB), SUB)
                edge = first * before[k:k + 1] + last * after[k:k + 1]
                work[rows, lanes] = inverse[rows, :] * (spectrum[rows, lanes] + edge)
        return carry

    lax.fori_loop(0, NY // SUB, ends, 0)
    work[...] = dot3((y_hi[...], y_lo[...]), split(work[...]))
    z = (z_hi[...], z_lo[...])
    half = pot.shape[0]
    for q in range(BLK // 2):
        lanes = slice(q * LANES, (q + 1) * LANES)
        rows = jnp.concatenate([work[:half, lanes], work[half:, lanes]], axis=1)
        pot[:, q * 2 * LANES:(q + 1) * 2 * LANES] = dot3(split(rows), z)
    for side, group in ((0, own), (1, other)):
        half = (core if side == 0 else 1 - core) * (len(own) * tiles)
        for n, ref in enumerate(group):
            for t in range(tiles):
                lanes = pl.ds(t * LANES, LANES)
                at = half + n * tiles + t
                rows = pl.ds(pl.multiple_of(at * SUB, SUB), SUB)
                total = None
                for w in range(BLK):
                    term = flags[u * BLK + w] * (pot[rows, w * LANES:(w + 1) * LANES] * ref[1 + w, :, lanes])
                    total = term if total is None else total + term
                out[:, pl.ds(pl.multiple_of(at * LANES, LANES), LANES)] = -total


def place_kernel(stride, match, *refs):
    parts, (out, rows, sem) = refs[:-4], refs[-3:]
    pair = BLK // 2
    blocks, count = out.shape[0] // BLK, len(parts) // pair
    core = my_core()

    def hits(b, side):
        return [(match[b * stride + side * stride // 2 + n], side * count // 2 + n) for n in range(count // 2)]

    def found(b, side):
        return sum(hit for hit, n in hits(b, side)) > 0

    def move(b, side):
        which = core if side == 0 else 1 - core
        at = b * BLK + which * pair
        return pltpu.make_async_copy(rows.at[b, side], out.at[pl.ds(at, pair)], sem.at[b, side])

    for b in range(blocks):
        for side in range(2):

            @pl.when(found(b, side))
            def _():
                rows[b, side] = jnp.zeros(rows.shape[2:], f32)
                for hit, n in hits(b, side):

                    @pl.when(hit > 0)
                    def _():
                        for u in range(pair):
                            rows[b, side, u] += parts[u * count + n][...]

                move(b, side).start()

    for b in range(blocks):
        for side in range(2):

            @pl.when(found(b, side))
            def _():
                move(b, side).wait()


def tile_device(orbitals, rotation, tile_list, pair_mask):
    per_device, planes, width = orbitals.shape
    n_orb, n_grid = lax.axis_size("orb"), lax.axis_size("grid")
    size_x = planes * n_grid
    half = width // 2
    chips = n_orb // 2
    axes = ("orb", "grid")
    o, g = lax.axis_index("orb"), lax.axis_index("grid")
    core, chip = o % 2, o // 2

    def swap(x, even, odd):
        moves = []
        for a in range(n_orb):
            flip = even if a % 2 == 0 else odd
            moves += [(a * n_grid + b, (a ^ flip) * n_grid + b) for b in range(n_grid)]
        return lax.ppermute(x, axes, moves)

    def cross(x, k):
        moves = [(a * n_grid + b, a * n_grid + (b ^ k)) for a in range(n_orb) for b in range(n_grid)]
        return lax.ppermute(x, axes, moves)

    chunk = half // CHUNKS

    def take(flip, start, lanes, *after):
        return pl.pallas_call(
            functools.partial(take_kernel, flip, start),
            out_shape=jax.ShapeDtypeStruct((per_device, planes, lanes), f32),
            in_specs=[HBM] + [ANY] * len(after), out_specs=VM, scratch_shapes=[DMA], name=f"take_{int(flip)}_{start}",
            compiler_params=grant(4),
        )(orbitals, *after)

    theirs, mine, last = [], [], ()
    for n in range(CHUNKS):
        taken = take(True, n * chunk, chunk, *last)
        theirs.append(swap(taken, 1, 1))
        last = (taken,)
    for n in range(CHUNKS):
        mine.append(take(False, n * chunk, chunk, *last))

    pair = BLK // 2
    firsts = (BLK + 2) * chips
    rows = (firsts + 2 * (pair - 1) * chips) * SUB
    wide_table = jax.ShapeDtypeStruct((rows, 2 * LANES), bf16)
    blocks = per_device // BLK
    high, low, flags, match, alone = pl.pallas_call(
        functools.partial(setup_kernel, per_device),
        out_shape=(wide_table, wide_table, jax.ShapeDtypeStruct((pair * BLK,), f32),
                   jax.ShapeDtypeStruct((blocks * 8,), jnp.int32), jax.ShapeDtypeStruct((1,), jnp.int32)),
        in_specs=[SM, SM, VM, VM], out_specs=(VM, VM, SM, SM, SM), name="setup", compiler_params=grant(8),
    )(tile_list.reshape(-1), jnp.asarray(host_np(chips).reshape(-1)), rotation, pair_mask)

    def rotate(first, count, fields, name, *after):
        part = jax.ShapeDtypeStruct((count, planes, chunk * (len(fields) // 2)), f32)
        send, keep = pl.pallas_call(
            functools.partial(rotate_kernel, first * SUB), out_shape=(part, part),
            in_specs=[VM] * (2 + len(fields)) + [ANY] * len(after),
            out_specs=(VM, VM), name=name, compiler_params=grant(8),
        )(high, low, *fields, *after)
        return send, keep, swap(send, 2, 4)

    sums, last = [], ()
    for n in range(CHUNKS):
        sums.append(rotate(0, firsts // 2, [mine[n], theirs[n]], f"rotate_{n}", *last))
        last = (sums[-1][0],)
    both = [x for n in range(CHUNKS) for x in (mine[n], theirs[n])]
    sums.append(rotate(firsts, (pair - 1) * chips, both, "rotate_rest", *last))
    empty = pl.pallas_call(
        clear_kernel, out_shape=jax.ShapeDtypeStruct(orbitals.shape, f32), in_specs=[ANY], out_specs=HBM,
        scratch_shapes=[pltpu.VMEM((pair, planes, width), f32), DMA((per_device // pair,))], name="clear",
        compiler_params=grant(4),
    )(sums[-1][0])
    passing, last, specs = [], (empty,), [HBM]
    for n, (send, keep, got) in enumerate(sums):
        shape = (keep.shape[0] // 2,) + keep.shape[1:]
        value = pl.pallas_call(
            pass_kernel, out_shape=jax.ShapeDtypeStruct(shape, f32), in_specs=[VM] * 2 + specs, out_specs=VM,
            name=f"pass_{n}", compiler_params=grant(4),
        )(keep, got, *last)
        last, specs = (value,), [ANY]
        passing.append((keep, got, swap(value, 4, 2)))
    own, other = [], []
    for n, (keep, got, passed) in enumerate(passing):
        own.append(pl.pallas_call(
            finish_kernel, out_shape=jax.ShapeDtypeStruct(passed.shape, f32), in_specs=[VM] * 3 + [ANY] * len(own[-1:]),
            out_specs=VM, name=f"finish_{n}", compiler_params=grant(4),
        )(keep, got, passed, *own[-1:]))
        other.append(swap(own[-1], 1, 1))

    c, r = line_np()
    sine_x, eigen_x = sine_np(planes), eigen_np(planes)
    ends = jnp.asarray(np.einsum("jp,pkl->kjl", sine_x, r[None] ** np.arange(planes - 1, -1, -1)[:, None, None])
                       .reshape(-1, LANES), f32)
    inverse = jnp.asarray((COUPLING / (eigen_x[None, :, None] + c[:, None, :])).reshape(-1, LANES), f32)
    basis = jnp.asarray(np.broadcast_to(sine_x[:, [0, -1]].T[:, :, None], (2, planes, LANES)), f32)
    steady = jnp.asarray(np.stack([r / ((1 - r**2) * (1 - r ** (2 * size_x + 2))), r, r**planes]), f32)
    at = planes * g
    exponents = jnp.stack([
        2 * at + planes + 1,
        2 * size_x + 1 - planes - 2 * at,
        2 * size_x + 2 - 2 * at,
        2 * at,
        2 * at + 2 * planes + 2,
        2 * size_x - 2 * planes - 2 * at,
    ]).astype(f32)
    powers = jnp.exp(exponents[:, None, None] * jnp.asarray(np.log(r), f32)[None])
    powers = jnp.where(jnp.arange(6)[:, None, None] < 2, powers, 1.0 - powers)

    y_hi, y_lo = halves_np(y_table())
    z_hi, z_lo = halves_np(z_table())
    zt_hi, zt_lo = halves_np(z_table().T)
    solved = []
    lines = jax.ShapeDtypeStruct((NY, 2 * LANES), f32)
    cube = (NY * SUB, 2 * LANES)
    wide = pltpu.VMEM((width // LANES * SUB, BLK * LANES), f32)
    base_own, base_other = own[:CHUNKS], other[:CHUNKS]
    last = ()
    for u in range(pair):
        more_own, more_other = own[CHUNKS:][:u], other[CHUNKS:][:u]
        counts = (CHUNKS, CHUNKS, len(more_own), len(more_other))
        inputs = [*base_own, *base_other, *more_own, *more_other, y_hi, y_lo, z_hi, z_lo, ends, powers]
        *messages, spectrum, a, b = pl.pallas_call(
            functools.partial(forward_kernel, u, counts + (n_grid - 1,)),
            out_shape=[lines] * (n_grid - 1) + [jax.ShapeDtypeStruct(cube, f32), lines, lines],
            in_specs=[VM] * len(inputs) + [ANY] * len(last),
            out_specs=[VM] * (n_grid + 2),
            scratch_shapes=[wide],
            name=f"forward_{u}",
            compiler_params=grant(16),
        )(*inputs, *last)
        last = (spectrum,)
        solved.append((spectrum, a, b, [cross(m, k) for k, m in enumerate(messages, 1)]))

    terms, last = [], ()
    for u, (spectrum, a, b, received) in enumerate(solved):
        inputs = [*base_own, *base_other, *received, y_hi, y_lo, zt_hi, zt_lo, inverse, basis, powers, steady,
                  spectrum, a, b]
        terms.append(pl.pallas_call(
            functools.partial(backward_kernel, u, (CHUNKS, CHUNKS, len(received))),
            out_shape=jax.ShapeDtypeStruct((planes, width), f32),
            in_specs=[SM] + [VM] * len(inputs) + [ANY] * len(last),
            out_specs=VM,
            scratch_shapes=[pltpu.VMEM(cube, f32), wide],
            name=f"backward_{u}",
            compiler_params=grant(16),
        )(flags, *inputs, *last))
        last = (terms[-1],)

    near_1 = [swap(term, 2, 4) for term in terms]
    near_2 = [swap(term, 4, 2) for term in terms]
    own_parts = [[term, x, y] for term, x, y in zip(terms, near_1, near_2)]
    sib_parts = [[swap(v, 1, 1) for v in group] for group in own_parts]

    def place(target, groups):
        parts = [part for group in groups for part in group]
        return pl.pallas_call(
            functools.partial(place_kernel, 8),
            out_shape=jax.ShapeDtypeStruct(orbitals.shape, f32),
            in_specs=[SM] + [VM] * len(parts) + [HBM],
            out_specs=HBM,
            input_output_aliases={len(parts) + 1: 0},
            scratch_shapes=[pltpu.VMEM((blocks, 2, pair, planes, width), f32), DMA((blocks, 2))],
            name="place",
            compiler_params=grant(8),
        )(match, *parts, target)

    def place_near(target, mine, sibs):
        return place(target, [a + b for a, b in zip(mine, sibs)])

    def place_far(target, mine, sibs):
        far = [swap(group[1], 4, 2) for group in mine]
        return place(target, [a + [x] + b + [swap(x, 1, 1)] for a, b, x in zip(mine, sibs, far)])

    return lax.cond(alone[0] != 0, place_far, place_near, empty, own_parts, sib_parts)


def sine_table(length):
    wave_index = jnp.arange(length, dtype=f32) + 1.0
    return jnp.sqrt(2.0 / (length + 1.0)) * jnp.sin(
        jnp.pi * wave_index[:, None] * wave_index[None, :] / (length + 1.0)
    )


def eigen_values(length):
    wave_index = jnp.arange(length, dtype=f32) + 1.0
    return 2.0 - 2.0 * jnp.cos(jnp.pi * wave_index / (length + 1.0))


def green_kernel(size_x, size_y, size_z):
    summed = (
        eigen_values(size_x)[:, None, None]
        + eigen_values(size_y)[None, :, None]
        + eigen_values(size_z)[None, None, :]
    )
    return COUPLING / (summed + SCREENING)


def pair_lists(tile_list, pair_mask):
    within = jnp.arange(BLK * BLK, dtype=jnp.int32)
    targets = (BLK * tile_list[:, 0:1] + within[None, :] // BLK).reshape(-1)
    sources = (BLK * tile_list[:, 1:2] + within[None, :] % BLK).reshape(-1)
    return (targets, sources, pair_mask[targets, sources])


def compact(targets, sources, live_flags, number):
    ranking = jnp.cumsum(live_flags) - 1
    places = jnp.where(live_flags == 1, ranking, number)
    picked = (
        jnp.zeros((number,), jnp.int32)
        .at[places]
        .set(jnp.arange(live_flags.shape[0], dtype=jnp.int32), mode="drop")
    )
    return (targets[picked], sources[picked])


def along_z(values, matrix):
    number, planes, width_yz = values.shape
    size_z = matrix.shape[0]
    shaped = values.reshape(number, planes, width_yz // size_z, size_z)
    return jnp.einsum("pxrz,zk->pxrk", shaped, matrix, precision=precise).reshape(number, planes, width_yz)


def along_y(values, matrix):
    number, planes, width_yz = values.shape
    size_y = matrix.shape[0]
    shaped = values.reshape(number, planes, size_y, width_yz // size_y)
    return jnp.einsum("pxyz,yk->pxkz", shaped, matrix, precision=precise).reshape(number, planes, width_yz)


def along_x(values, matrix):
    return jnp.einsum("pxc,xk->pkc", values, matrix, precision=precise)


def any_device(orbitals, rotation, tile_list, pair_mask):
    n_orb, n_grid = lax.axis_size("orb"), lax.axis_size("grid")
    number_orbitals, size_x = rotation.shape[0], orbitals.shape[1] * n_grid
    rotated = jnp.einsum(
        "ij,ixc->jxc",
        rotation,
        lax.all_to_all(orbitals, "orb", split_axis=2, concat_axis=0, tiled=True),
        precision=precise,
    )
    planes, width_yz = rotated.shape[1:]
    targets, sources, live_flags = pair_lists(tile_list, pair_mask)
    matrix_x, matrix_y, matrix_z = sine_table(size_x), sine_table(NY), sine_table(NZ)
    kernel = green_kernel(size_x, NY, NZ).reshape(size_x, NY * NZ)
    orbital_ids = jnp.arange(number_orbitals, dtype=jnp.int32)
    targets, sources = compact(targets, sources, live_flags, targets.shape[0] // 2)
    density = rotated[targets] * rotated[sources]
    number = density.shape[0]
    spectrum = along_z(density, matrix_z)
    spectrum = lax.all_to_all(spectrum, "orb", split_axis=0, concat_axis=2, tiled=True)
    spectrum = along_y(spectrum, matrix_y)
    spectrum = lax.all_to_all(spectrum, "grid", split_axis=0, concat_axis=1, tiled=True)
    spectrum = along_x(along_x(spectrum, matrix_x) * kernel, matrix_x)
    spectrum = lax.all_to_all(spectrum, "grid", split_axis=1, concat_axis=0, tiled=True)
    spectrum = along_y(spectrum, matrix_y)
    spectrum = lax.all_to_all(spectrum, "orb", split_axis=2, concat_axis=0, tiled=True)
    potential = along_z(spectrum, matrix_z)
    products = potential * rotated[sources]
    selector = (targets[None, :] == orbital_ids[:, None]).astype(f32)
    partial_value = -jnp.dot(selector, products.reshape(number, planes * width_yz), precision=precise)
    partial_value = partial_value.reshape(number_orbitals, planes, width_yz)
    return lax.all_to_all(partial_value, "orb", split_axis=0, concat_axis=2, tiled=True)


def solution(mesh):
    n_orb, n_grid = mesh.shape["orb"], mesh.shape["grid"]

    def on_device(orbitals, rotation, tile_list, pair_mask):
        per_device, planes, width = orbitals.shape
        fits = n_orb == 8 and 2 * tile_list.shape[0] == n_orb and planes == SUB and per_device % BLK == 0
        fits = fits and width == NY * NZ and 2 * NZ == LANES and n_grid in (2, 4, 8)
        fits = fits and per_device * SUB == LANES and rotation.shape == (LANES, LANES)
        body = tile_device if fits else any_device
        return body(orbitals, rotation, tile_list, pair_mask)

    in_specs = (P("orb", "grid", None), P(), P(), P())
    out_specs = P("orb", "grid", None)
    return jax.shard_map(on_device, mesh=mesh, in_specs=in_specs, out_specs=out_specs, check_vma=False)
```

profile of v0, /device:TPU:0, one launch (start us, length us, event | category | flops | bytes accessed | tf_op | source)
XLA Modules:
  0.0 65.7 jit_solution(387350976356448511)
XLA Ops:
  0.0 1.6 %copy-done = f32[16,8,4096]{2,1,0:T(8,128)S(1)} copy-done((f32[16,8,4096]{2,1,0:T(8,128)S(1)}, f32[16,8,4096]{2,1,0:T(8,128)}, u32[]{:S(2)}) %copy-start) | copy-done | bytes 2097176
  1.6 0.6 collective-permute-start.4
  2.5 0.6 copy-done.22
  3.3 1.5 %setup.1 = (bf16[256,256]{1,0:T(8,128)(2,1)S(1)}, bf16[256,256]{1,0:T(8,128)(2,1)S(1)}, f32[8]{0:T(128)S(1)}, s32[32]{0:T(128)S(1)}, s32[1]{0:T(128)}) custom-call(s32[8]{0:T(128)S(1)} %reshape.62.tiles, s32[1024]{0:T(1024)S(1)} %copy-done.17, f32[128,128]{1,0:T(8,128)S(1)} %copy-done.14, s32[128,128]{1,0:T(8,128)S(1)} %copy-done.15), custom_call_target="tpu_custom_call" | custom-call | tf_op jit(solution)/shard_map/setup/pallas_call | solution.py:447
  4.9 0.5 rotate_0.1
  5.4 3.0 %collective-permute-start.5 = (f32[12,8,1024]{2,1,0:T(8,128)S(1)}, f32[12,8,1024]{2,1,0:T(8,128)S(1)}, u32[]{:S(2)}, u32[]{:S(2)}) collective-permute-start(f32[12,8,1024]{2,1,0:T(8,128)S(1)} %get-tuple-element.121.rest_2_), channel_id=1, source_target_pairs={{0,8},{1,9},{2,10},{3,11},{4,20},{5,21},{6,22},{7,23},{8,0},{9,1},... | collective-permute-start | bytes 1179656 | tf_op jit(solution)/shard_map/ppermute | solution.py:418
  8.4 0.5 rotate_1.1
  9.0 0.7 %rotate_rest.1 = (f32[4,8,2048]{2,1,0:T(8,128)S(1)}, f32[4,8,2048]{2,1,0:T(8,128)S(1)}) custom-call(bf16[256,256]{1,0:T(8,128)(2,1)S(1)} %get-tuple-element.118.high, bf16[256,256]{1,0:T(8,128)(2,1)S(1)} %get-tuple-element.119.low, f32[16,8,1024]{2,1,0:T(8,128)S(1)} %take_0_0.1.rest_0_, f32[16,8,1024]{2,1,0:T(8,128)S(1)} %collective-permute-done.4.rest_1_, ...), custom_call_target="tpu_custom_call" | custom-call | tf_op jit(solution)/shard_map/rotate_rest/pallas_call | solution.py:456
  9.7 2.1 %collective-permute-start.20 = (f32[4,8,2048]{2,1,0:T(8,128)S(1)}, f32[4,8,2048]{2,1,0:T(8,128)S(1)}, u32[]{:S(2)}, u32[]{:S(2)}) collective-permute-start(f32[4,8,2048]{2,1,0:T(8,128)S(1)} %get-tuple-element.123.refs_0_), channel_id=1, source_target_pairs={{0,8},{1,9},{2,10},{3,11},{4,20},{5,21},{6,22},{7,23},{8,0},{9,1},... | collective-permute-start | bytes 786440 | tf_op jit(solution)/shard_map/ppermute | solution.py:418
  11.7 0.2 clear.1.rest_0_
  12.0 2.1 %collective-permute-done.5.got = f32[12,8,1024]{2,1,0:T(8,128)S(1)} collective-permute-done((f32[12,8,1024]{2,1,0:T(8,128)S(1)}, f32[12,8,1024]{2,1,0:T(8,128)S(1)}, u32[]{:S(2)}, u32[]{:S(2)}) %collective-permute-start.5) | collective-permute-done | bytes 393248 | tf_op jit(solution)/shard_map/ppermute | solution.py:418
  14.2 2.1 %collective-permute-start.7 = (f32[6,8,1024]{2,1,0:T(8,128)S(1)}, f32[6,8,1024]{2,1,0:T(8,128)}, u32[]{:S(2)}, u32[]{:S(2)}) collective-permute-start(f32[6,8,1024]{2,1,0:T(8,128)S(1)} %pass_0.1.rest_0_), channel_id=1, source_target_pairs={{0,16},{1,17},{2,18},{3,19},{4,12},{5,13},{6,14},{7,15},{8,24},{9,... | collective-permute-start | bytes 589832 | tf_op jit(solution)/shard_map/ppermute | solution.py:418
  16.3 4.1 %collective-permute-done.8.got = f32[12,8,1024]{2,1,0:T(8,128)S(1)} collective-permute-done((f32[12,8,1024]{2,1,0:T(8,128)S(1)}, f32[12,8,1024]{2,1,0:T(8,128)S(1)}, u32[]{:S(2)}, u32[]{:S(2)}) %collective-permute-start.8) | collective-permute-done | bytes 393248 | tf_op jit(solution)/shard_map/ppermute | solution.py:418
  20.4 2.4 %collective-permute-start.9 = (f32[6,8,1024]{2,1,0:T(8,128)S(1)}, f32[6,8,1024]{2,1,0:T(8,128)}, u32[]{:S(2)}, u32[]{:S(2)}) collective-permute-start(f32[6,8,1024]{2,1,0:T(8,128)S(1)} %pass_1.1.rest_0_), channel_id=1, source_target_pairs={{0,16},{1,17},{2,18},{3,19},{4,12},{5,13},{6,14},{7,15},{8,24},{9,... | collective-permute-start | bytes 589832 | tf_op jit(solution)/shard_map/ppermute | solution.py:418
  22.8 2.5 %collective-permute-done.20.got = f32[4,8,2048]{2,1,0:T(8,128)S(1)} collective-permute-done((f32[4,8,2048]{2,1,0:T(8,128)S(1)}, f32[4,8,2048]{2,1,0:T(8,128)S(1)}, u32[]{:S(2)}, u32[]{:S(2)}) %collective-permute-start.20) | collective-permute-done | bytes 262176 | tf_op jit(solution)/shard_map/ppermute | solution.py:418
  25.4 0.7 %pass_2.1 = f32[2,8,2048]{2,1,0:T(8,128)} custom-call(f32[4,8,2048]{2,1,0:T(8,128)S(1)} %get-tuple-element.131.keep, f32[4,8,2048]{2,1,0:T(8,128)S(1)} %collective-permute-done.20.got, f32[6,8,1024]{2,1,0:T(8,128)S(1)} %pass_1.1.rest_0_), custom_call_target="tpu_custom_call" | custom-call | tf_op jit(solution)/shard_map/pass_2/pallas_call | solution.py:477
  26.1 2.0 %collective-permute-start.21 = (f32[2,8,2048]{2,1,0:T(8,128)}, f32[2,8,2048]{2,1,0:T(8,128)S(1)}, u32[]{:S(2)}, u32[]{:S(2)}) collective-permute-start(f32[2,8,2048]{2,1,0:T(8,128)} %pass_2.1), channel_id=1, source_target_pairs={{0,16},{1,17},{2,18},{3,19},{4,12},{5,13},{6,14},{7,15},{8,24},{9,... | collective-permute-start | bytes 393224 | tf_op jit(solution)/shard_map/ppermute | solution.py:418
  28.3 1.0 %finish_0.1.rest_0_.refs_0_ = f32[6,8,1024]{2,1,0:T(8,128)S(1)} custom-call(f32[12,8,1024]{2,1,0:T(8,128)S(1)} %get-tuple-element.120.keep, f32[12,8,1024]{2,1,0:T(8,128)S(1)} %collective-permute-done.5.got, f32[6,8,1024]{2,1,0:T(8,128)} %collective-permute-done.7.passed), custom_call_target="tpu_custom_call" | custom-call | tf_op jit(solution)/shard_map/finish_0/pallas_call | solution.py:485
  29.3 1.0 %copy-done.4 = f32[12,8,1024]{2,1,0:T(8,128)S(1)} copy-done((f32[12,8,1024]{2,1,0:T(8,128)S(1)}, f32[12,8,1024]{2,1,0:T(8,128)}, u32[]{:S(2)}) %copy-start.4) | copy-done | bytes 393240
  30.3 1.0 %finish_1.1.refs_1_.rest_0_ = f32[6,8,1024]{2,1,0:T(8,128)S(1)} custom-call(f32[12,8,1024]{2,1,0:T(8,128)S(1)} %get-tuple-element.124.keep, f32[12,8,1024]{2,1,0:T(8,128)S(1)} %copy-done.4, f32[6,8,1024]{2,1,0:T(8,128)} %collective-permute-done.9.passed, f32[6,8,1024]{2,1,0:T(8,128)S(1)} %finish_0.1.rest_0_.refs_0_), custom_call_target="tpu_custom_call" | custom-call | tf_op jit(solution)/shard_map/finish_1/pallas_call | solution.py:485
  31.3 0.6 collective-permute-start.11
  31.8 0.9 %copy-done.7 = f32[4,8,2048]{2,1,0:T(8,128)S(1)} copy-done((f32[4,8,2048]{2,1,0:T(8,128)S(1)}, f32[4,8,2048]{2,1,0:T(8,128)}, u32[]{:S(2)}) %copy-start.7) | copy-done | bytes 262168
  33.1 1.2 %forward_0.1 = (f32[64,256]{1,0:T(8,128)S(1)}, f32[64,256]{1,0:T(8,128)S(1)}, f32[64,256]{1,0:T(8,128)S(1)}, f32[512,256]{1,0:T(8,128)S(1)}, f32[64,256]{1,0:T(8,128)S(1)}, /*index=5*/f32[64,256]{1,0:T(8,128)S(1)}) custom-call(f32[6,8,1024]{2,1,0:T(8,128)S(1)} %finish_0.1.rest_0_.refs_0_, f32[6,8,1024]{2,1,0:T(8,128)S(1)} %finish_1.1.refs_1_.rest_0_, ...), custom_call_target="tpu_custom_call" | custom-call | tf_op jit(solution)/shard_map/forward_0/pallas_call | solution.py:523
  34.3 1.6 %collective-permute-start.12 = (f32[64,256]{1,0:T(8,128)S(1)}, f32[64,256]{1,0:T(8,128)S(1)}, u32[]{:S(2)}, u32[]{:S(2)}) collective-permute-start(f32[64,256]{1,0:T(8,128)S(1)} %get-tuple-element.125), channel_id=1, source_target_pairs={{0,1},{1,0},{2,3},{3,2},{4,5},{5,4},{6,7},{7,6},{8,9},{9,8},{10,11... | collective-permute-start | bytes 196616 | tf_op jit(solution)/shard_map/ppermute | solution.py:422
  35.9 2.6 %collective-permute-start.13 = (f32[64,256]{1,0:T(8,128)S(1)}, f32[64,256]{1,0:T(8,128)S(1)}, u32[]{:S(2)}, u32[]{:S(2)}) collective-permute-start(f32[64,256]{1,0:T(8,128)S(1)} %get-tuple-element.126), channel_id=1, source_target_pairs={{0,2},{1,3},{2,0},{3,1},{4,6},{5,7},{6,4},{7,5},{8,10},{9,11},{10,... | collective-permute-start | bytes 196616 | tf_op jit(solution)/shard_map/ppermute | solution.py:422
  38.5 0.2 collective-permute-start.14
  38.8 1.2 %forward_1.1 = (f32[64,256]{1,0:T(8,128)S(1)}, f32[64,256]{1,0:T(8,128)S(1)}, f32[64,256]{1,0:T(8,128)S(1)}, f32[512,256]{1,0:T(8,128)S(1)}, f32[64,256]{1,0:T(8,128)S(1)}, /*index=5*/f32[64,256]{1,0:T(8,128)S(1)}) custom-call(f32[6,8,1024]{2,1,0:T(8,128)S(1)} %finish_0.1.rest_0_.refs_0_, f32[6,8,1024]{2,1,0:T(8,128)S(1)} %finish_1.1.refs_1_.rest_0_, ...), custom_call_target="tpu_custom_call" | custom-call | tf_op jit(solution)/shard_map/forward_1/pallas_call | solution.py:523
  39.9 0.7 %collective-permute-start.23 = (f32[64,256]{1,0:T(8,128)S(1)}, f32[64,256]{1,0:T(8,128)S(1)}, u32[]{:S(2)}, u32[]{:S(2)}) collective-permute-start(f32[64,256]{1,0:T(8,128)S(1)} %get-tuple-element.132), channel_id=1, source_target_pairs={{0,1},{1,0},{2,3},{3,2},{4,5},{5,4},{6,7},{7,6},{8,9},{9,8},{10,11... | collective-permute-start | bytes 196616 | tf_op jit(solution)/shard_map/ppermute | solution.py:422
  40.7 3.5 %collective-permute-start.24 = (f32[64,256]{1,0:T(8,128)S(1)}, f32[64,256]{1,0:T(8,128)S(1)}, u32[]{:S(2)}, u32[]{:S(2)}) collective-permute-start(f32[64,256]{1,0:T(8,128)S(1)} %get-tuple-element.133), channel_id=1, source_target_pairs={{0,2},{1,3},{2,0},{3,1},{4,6},{5,7},{6,4},{7,5},{8,10},{9,11},{10,... | collective-permute-start | bytes 196616 | tf_op jit(solution)/shard_map/ppermute | solution.py:422
  44.2 0.2 collective-permute-start.25
  44.4 0.7 %collective-permute-done.14.refs_6_ = f32[64,256]{1,0:T(8,128)S(1)} collective-permute-done((f32[64,256]{1,0:T(8,128)S(1)}, f32[64,256]{1,0:T(8,128)S(1)}, u32[]{:S(2)}, u32[]{:S(2)}) %collective-permute-start.14) | collective-permute-done | bytes 65568 | tf_op jit(solution)/shard_map/ppermute | solution.py:422
  45.1 2.3 %backward_0.1.refs_18_ = f32[8,4096]{1,0:T(8,128)S(1)} custom-call(f32[8]{0:T(128)S(1)} %get-tuple-element.117.flags, f32[6,8,1024]{2,1,0:T(8,128)S(1)} %finish_0.1.rest_0_.refs_0_, f32[6,8,1024]{2,1,0:T(8,128)S(1)} %finish_1.1.refs_1_.rest_0_, f32[6,8,1024]{2,1,0:T(8,128)S(1)} %collective-permute-done.10.refs_2_, ...), custom_call_target="tpu_custom_call" | custom-call | tf_op jit(solution)/shard_map/backward_0/pallas_call | solution.py:539
  47.4 1.8 %collective-permute-done.24.refs_5_ = f32[64,256]{1,0:T(8,128)S(1)} collective-permute-done((f32[64,256]{1,0:T(8,128)S(1)}, f32[64,256]{1,0:T(8,128)S(1)}, u32[]{:S(2)}, u32[]{:S(2)}) %collective-permute-start.24) | collective-permute-done | bytes 65568 | tf_op jit(solution)/shard_map/ppermute | solution.py:422
  49.3 1.1 %collective-permute-done.25.refs_6_ = f32[64,256]{1,0:T(8,128)S(1)} collective-permute-done((f32[64,256]{1,0:T(8,128)S(1)}, f32[64,256]{1,0:T(8,128)S(1)}, u32[]{:S(2)}, u32[]{:S(2)}) %collective-permute-start.25) | collective-permute-done | bytes 65568 | tf_op jit(solution)/shard_map/ppermute | solution.py:422
  50.3 2.3 %backward_1.1 = f32[8,4096]{1,0:T(8,128)S(1)} custom-call(f32[8]{0:T(128)S(1)} %get-tuple-element.117.flags, f32[6,8,1024]{2,1,0:T(8,128)S(1)} %finish_0.1.rest_0_.refs_0_, f32[6,8,1024]{2,1,0:T(8,128)S(1)} %finish_1.1.refs_1_.rest_0_, f32[6,8,1024]{2,1,0:T(8,128)S(1)} %collective-permute-done.10.refs_2_, f32[6,8,1024]{2,1,0:T(8,128)S(1)} %collective-permute-done.11.refs_3_, ...), custom_call_target="tpu_custom_call" | custom-call | tf_op jit(solution)/shard_map/backward_1/pallas_call | solution.py:539
  52.7 1.6 %collective-permute-start.27 = (f32[8,4096]{1,0:T(8,128)S(1)}, f32[8,4096]{1,0:T(8,128)S(1)}, u32[]{:S(2)}, u32[]{:S(2)}) collective-permute-start(f32[8,4096]{1,0:T(8,128)S(1)} %backward_1.1), channel_id=1, source_target_pairs={{0,16},{1,17},{2,18},{3,19},{4,12},{5,13},{6,14},{7,15},{8,24},{9,... | collective-permute-start | bytes 393224 | tf_op jit(solution)/shard_map/ppermute | solution.py:418
  54.2 1.5 %collective-permute-start.26 = (f32[8,4096]{1,0:T(8,128)S(1)}, f32[8,4096]{1,0:T(8,128)S(1)}, u32[]{:S(2)}, u32[]{:S(2)}) collective-permute-start(f32[8,4096]{1,0:T(8,128)S(1)} %backward_1.1), channel_id=1, source_target_pairs={{0,8},{1,9},{2,10},{3,11},{4,20},{5,21},{6,22},{7,23},{8,0},{9,1},... | collective-permute-start | bytes 393224 | tf_op jit(solution)/shard_map/ppermute | solution.py:418
  55.7 0.5 collective-permute-start.16
  56.3 0.5 collective-permute-start.15
  56.8 1.6 %collective-permute-done.27 = f32[8,4096]{1,0:T(8,128)S(1)} collective-permute-done((f32[8,4096]{1,0:T(8,128)S(1)}, f32[8,4096]{1,0:T(8,128)S(1)}, u32[]{:S(2)}, u32[]{:S(2)}) %collective-permute-start.27) | collective-permute-done | bytes 131104 | tf_op jit(solution)/shard_map/ppermute | solution.py:418
  58.4 1.8 %collective-permute-done.26 = f32[8,4096]{1,0:T(8,128)S(1)} collective-permute-done((f32[8,4096]{1,0:T(8,128)S(1)}, f32[8,4096]{1,0:T(8,128)S(1)}, u32[]{:S(2)}, u32[]{:S(2)}) %collective-permute-start.26) | collective-permute-done | bytes 131104 | tf_op jit(solution)/shard_map/ppermute | solution.py:418
  60.2 1.7 %collective-permute-done.16 = f32[8,4096]{1,0:T(8,128)S(1)} collective-permute-done((f32[8,4096]{1,0:T(8,128)S(1)}, f32[8,4096]{1,0:T(8,128)S(1)}, u32[]{:S(2)}, u32[]{:S(2)}) %collective-permute-start.16) | collective-permute-done | bytes 131104 | tf_op jit(solution)/shard_map/ppermute | solution.py:418
  62.0 0.4 collective-permute-start.18
  63.2 0.1 collective-permute-done.19
  63.3 0.2 collective-permute-done.18
  63.5 0.9 %conditional.1 = (f32[16,8,4096]{2,1,0:T(8,128)S(1)}) conditional(s32[]{:T(128)} %bitcast, (s32[32]{0:T(128)S(1)}, f32[8,4096]{1,0:T(8,128)S(1)}, f32[8,4096]{1,0:T(8,128)S(1)}, f32[8,4096]{1,0:T(8,128)S(1)}, f32[8,4096]{1,0:T(8,128)S(1)}, /*index=5*/f32[8,4096]{1,0:T(8,128)S(1)}, f32[8,4096]{1,0:T(8,128)S(1)}, f32[8,4096]{1,0:T(8,128)S(1)}, ...), branch_computations={%region_0.1_spmd, %region_1.2_spmd} | conditional | bytes 2097320 | solution.py:575
  63.5 0.9 %place.2 = f32[16,8,4096]{2,1,0:T(8,128)S(1)} custom-call(s32[32]{0:T(128)S(1)} %get-tuple-element.64.match, f32[8,4096]{1,0:T(8,128)S(1)} %get-tuple-element.65.refs_0_, f32[8,4096]{1,0:T(8,128)S(1)} %get-tuple-element.66.refs_1_, f32[8,4096]{1,0:T(8,128)S(1)} %get-tuple-element.67.refs_2_, ...), custom_call_target="tpu_custom_call", output_to_operand_aliasing={{}: (13, {})} | custom-call | tf_op jit(solution)/shard_map/cond/branch_0_fun/place/pallas_call | solution.py:557
  64.4 1.3 %copy-done.20 = f32[16,8,4096]{2,1,0:T(8,128)} copy-done((f32[16,8,4096]{2,1,0:T(8,128)}, f32[16,8,4096]{2,1,0:T(8,128)S(1)}, u32[]{:S(2)}) %copy-start.20) | copy-done | bytes 2097176
  (79 shorter events, 1.3 us)
Async XLA Ops:
  0.0 1.6 %copy-start = (f32[16,8,4096]{2,1,0:T(8,128)S(1)}, f32[16,8,4096]{2,1,0:T(8,128)}, u32[]{:S(2)}) copy-start(f32[16,8,4096]{2,1,0:T(8,128)} %source.7) | copy-start | bytes 6291460
  1.6 3.2 %collective-permute-start.4 = (f32[16,8,1024]{2,1,0:T(8,128)S(1)}, f32[16,8,1024]{2,1,0:T(8,128)S(1)}, u32[]{:S(2)}, u32[]{:S(2)}) collective-permute-start(f32[16,8,1024]{2,1,0:T(8,128)S(1)} %take_1_0.1.rest_0_), channel_id=1, source_target_pairs={{0,4},{1,5},{2,6},{3,7},{4,0},{5,1},{6,2},{7,3},{8,12},{9,13},{10,... | collective-permute-start | bytes 1572872 | tf_op jit(solution)/shard_map/ppermute | solution.py:418
  2.3 6.1 %collective-permute-start.6 = (f32[16,8,1024]{2,1,0:T(8,128)S(1)}, f32[16,8,1024]{2,1,0:T(8,128)S(1)}, u32[]{:S(2)}, u32[]{:S(2)}) collective-permute-start(f32[16,8,1024]{2,1,0:T(8,128)S(1)} %take_1_1024.1.rest_0_), channel_id=1, source_target_pairs={{0,4},{1,5},{2,6},{3,7},{4,0},{5,1},{6,2},{7,3},{8,12},{9,13},{10,... | collective-permute-start | bytes 1572872 | tf_op jit(solution)/shard_map/ppermute | solution.py:418
  2.4 0.9 %copy-start.15 = (s32[128,128]{1,0:T(8,128)S(1)}, s32[128,128]{1,0:T(8,128)}, u32[]{:S(2)}) copy-start(s32[128,128]{1,0:T(8,128)} %mask.1) | copy-start | bytes 196612
  2.4 0.9 %copy-start.17 = (s32[1024]{0:T(1024)S(1)}, s32[1024]{0:T(1024)}, u32[]{:S(2)}) copy-start(s32[1024]{0:T(1024)} %constant.51.clone.host) | copy-start | bytes 12292
  5.4 8.8 %collective-permute-start.5 = (f32[12,8,1024]{2,1,0:T(8,128)S(1)}, f32[12,8,1024]{2,1,0:T(8,128)S(1)}, u32[]{:S(2)}, u32[]{:S(2)}) collective-permute-start(f32[12,8,1024]{2,1,0:T(8,128)S(1)} %get-tuple-element.121.rest_2_), channel_id=1, source_target_pairs={{0,8},{1,9},{2,10},{3,11},{4,20},{5,21},{6,22},{7,23},{8,0},{9,1},... | collective-permute-start | bytes 1179656 | tf_op jit(solution)/shard_map/ppermute | solution.py:418
  8.9 11.5 %collective-permute-start.8 = (f32[12,8,1024]{2,1,0:T(8,128)S(1)}, f32[12,8,1024]{2,1,0:T(8,128)S(1)}, u32[]{:S(2)}, u32[]{:S(2)}) collective-permute-start(f32[12,8,1024]{2,1,0:T(8,128)S(1)} %get-tuple-element.122.rest_4_), channel_id=1, source_target_pairs={{0,8},{1,9},{2,10},{3,11},{4,20},{5,21},{6,22},{7,23},{8,0},{9,1},... | collective-permute-start | bytes 1179656 | tf_op jit(solution)/shard_map/ppermute | solution.py:418
  9.7 15.7 %copy-start.6 = (f32[4,8,2048]{2,1,0:T(8,128)}, f32[4,8,2048]{2,1,0:T(8,128)S(1)}, u32[]{:S(2)}) copy-start(f32[4,8,2048]{2,1,0:T(8,128)S(1)} %get-tuple-element.131.keep) | copy-start | bytes 786436
  9.7 15.7 %collective-permute-start.20 = (f32[4,8,2048]{2,1,0:T(8,128)S(1)}, f32[4,8,2048]{2,1,0:T(8,128)S(1)}, u32[]{:S(2)}, u32[]{:S(2)}) collective-permute-start(f32[4,8,2048]{2,1,0:T(8,128)S(1)} %get-tuple-element.123.refs_0_), channel_id=1, source_target_pairs={{0,8},{1,9},{2,10},{3,11},{4,20},{5,21},{6,22},{7,23},{8,0},{9,1},... | collective-permute-start | bytes 786440 | tf_op jit(solution)/shard_map/ppermute | solution.py:418
  12.0 13.4 %copy-start.18 = (f32[16,8,4096]{2,1,0:T(8,128)}, f32[16,8,4096]{2,1,0:T(8,128)S(1)}, u32[]{:S(2)}) copy-start(f32[16,8,4096]{2,1,0:T(8,128)S(1)} %clear.1.rest_0_) | copy-start | bytes 6291460
  14.2 14.1 %collective-permute-start.7 = (f32[6,8,1024]{2,1,0:T(8,128)S(1)}, f32[6,8,1024]{2,1,0:T(8,128)}, u32[]{:S(2)}, u32[]{:S(2)}) collective-permute-start(f32[6,8,1024]{2,1,0:T(8,128)S(1)} %pass_0.1.rest_0_), channel_id=1, source_target_pairs={{0,16},{1,17},{2,18},{3,19},{4,12},{5,13},{6,14},{7,15},{8,24},{9,... | collective-permute-start | bytes 589832 | tf_op jit(solution)/shard_map/ppermute | solution.py:418
  20.4 5.0 %copy-start.3 = (f32[12,8,1024]{2,1,0:T(8,128)}, f32[12,8,1024]{2,1,0:T(8,128)S(1)}, u32[]{:S(2)}) copy-start(f32[12,8,1024]{2,1,0:T(8,128)S(1)} %collective-permute-done.8.got) | copy-start | bytes 1179652
  20.4 8.9 %collective-permute-start.9 = (f32[6,8,1024]{2,1,0:T(8,128)S(1)}, f32[6,8,1024]{2,1,0:T(8,128)}, u32[]{:S(2)}, u32[]{:S(2)}) collective-permute-start(f32[6,8,1024]{2,1,0:T(8,128)S(1)} %pass_1.1.rest_0_), channel_id=1, source_target_pairs={{0,16},{1,17},{2,18},{3,19},{4,12},{5,13},{6,14},{7,15},{8,24},{9,... | collective-permute-start | bytes 589832 | tf_op jit(solution)/shard_map/ppermute | solution.py:418
  25.4 7.6 %copy-start.5 = (f32[512,128]{1,0:T(8,128)S(1)}, f32[512,128]{1,0:T(8,128)}, u32[]{:S(2)}) copy-start(f32[512,128]{1,0:T(8,128)} %constant.52.clone.refs_8_.refs_10_) | copy-start | bytes 786436
  25.4 7.6 %copy-start.12 = (bf16[256,256]{1,0:T(8,128)(2,1)S(1)}, bf16[256,256]{1,0:T(8,128)(2,1)}, u32[]{:S(2)}) copy-start(bf16[256,256]{1,0:T(8,128)(2,1)} %constant.59.clone.refs_6_.refs_8_) | copy-start | bytes 393220
  26.1 7.0 %copy-start.1 = (bf16[512,512]{1,0:T(8,128)(2,1)S(1)}, bf16[512,512]{1,0:T(8,128)(2,1)}, u32[]{:S(2)}) copy-start(bf16[512,512]{1,0:T(8,128)(2,1)} %constant.58.clone.refs_5_.refs_8_.refs_7_) | copy-start | bytes 1572868
  26.1 7.0 %copy-start.2 = (bf16[512,512]{1,0:T(8,128)(2,1)S(1)}, bf16[512,512]{1,0:T(8,128)(2,1)}, u32[]{:S(2)}) copy-start(bf16[512,512]{1,0:T(8,128)(2,1)} %constant.57.clone.refs_4_.refs_7_.refs_6_) | copy-start | bytes 1572868
  26.1 7.0 %copy-start.11 = (bf16[256,256]{1,0:T(8,128)(2,1)S(1)}, bf16[256,256]{1,0:T(8,128)(2,1)}, u32[]{:S(2)}) copy-start(bf16[256,256]{1,0:T(8,128)(2,1)} %constant.60.clone.refs_7_.refs_9_) | copy-start | bytes 393220
  26.1 5.7 %collective-permute-start.21 = (f32[2,8,2048]{2,1,0:T(8,128)}, f32[2,8,2048]{2,1,0:T(8,128)S(1)}, u32[]{:S(2)}, u32[]{:S(2)}) collective-permute-start(f32[2,8,2048]{2,1,0:T(8,128)} %pass_2.1), channel_id=1, source_target_pairs={{0,16},{1,17},{2,18},{3,19},{4,12},{5,13},{6,14},{7,15},{8,24},{9,... | collective-permute-start | bytes 393224 | tf_op jit(solution)/shard_map/ppermute | solution.py:418
  28.2 4.7 %copy-start.21 = (f32[64,128]{1,0:T(8,128)S(1)}, f32[64,128]{1,0:T(8,128)}, u32[]{:S(2)}) copy-start(f32[64,128]{1,0:T(8,128)} %constant.56.clone) | copy-start | bytes 98308
  29.2 3.8 %collective-permute-start.10 = (f32[6,8,1024]{2,1,0:T(8,128)S(1)}, f32[6,8,1024]{2,1,0:T(8,128)S(1)}, u32[]{:S(2)}, u32[]{:S(2)}) collective-permute-start(f32[6,8,1024]{2,1,0:T(8,128)S(1)} %finish_0.1.rest_0_.refs_0_), channel_id=1, source_target_pairs={{0,4},{1,5},{2,6},{3,7},{4,0},{5,1},{6,2},{7,3},{8,12},{9,13},{10,... | collective-permute-start | bytes 589832 | tf_op jit(solution)/shard_map/ppermute | solution.py:418
  29.3 1.0 %copy-start.4 = (f32[12,8,1024]{2,1,0:T(8,128)S(1)}, f32[12,8,1024]{2,1,0:T(8,128)}, u32[]{:S(2)}) copy-start(f32[12,8,1024]{2,1,0:T(8,128)} %copy-done.3) | copy-start | bytes 1179652
  31.3 1.7 %collective-permute-start.11 = (f32[6,8,1024]{2,1,0:T(8,128)S(1)}, f32[6,8,1024]{2,1,0:T(8,128)S(1)}, u32[]{:S(2)}, u32[]{:S(2)}) collective-permute-start(f32[6,8,1024]{2,1,0:T(8,128)S(1)} %finish_1.1.refs_1_.rest_0_), channel_id=1, source_target_pairs={{0,4},{1,5},{2,6},{3,7},{4,0},{5,1},{6,2},{7,3},{8,12},{9,13},{10,... | collective-permute-start | bytes 589832 | tf_op jit(solution)/shard_map/ppermute | solution.py:418
  31.8 1.0 %copy-start.7 = (f32[4,8,2048]{2,1,0:T(8,128)S(1)}, f32[4,8,2048]{2,1,0:T(8,128)}, u32[]{:S(2)}) copy-start(f32[4,8,2048]{2,1,0:T(8,128)} %copy-done.6) | copy-start | bytes 786436
  32.8 6.0 %collective-permute-start.22 = (f32[2,8,2048]{2,1,0:T(8,128)S(1)}, f32[2,8,2048]{2,1,0:T(8,128)S(1)}, u32[]{:S(2)}, u32[]{:S(2)}) collective-permute-start(f32[2,8,2048]{2,1,0:T(8,128)S(1)} %finish_2.1.refs_4_), channel_id=1, source_target_pairs={{0,4},{1,5},{2,6},{3,7},{4,0},{5,1},{6,2},{7,3},{8,12},{9,13},{10,... | collective-permute-start | bytes 393224 | tf_op jit(solution)/shard_map/ppermute | solution.py:418
  34.2 10.8 %copy-start.8 = (f32[512,128]{1,0:T(8,128)S(1)}, f32[512,128]{1,0:T(8,128)}, u32[]{:S(2)}) copy-start(f32[512,128]{1,0:T(8,128)} %constant.53.clone.refs_11_) | copy-start | bytes 786436
  34.2 10.8 %copy-start.9 = (bf16[256,256]{1,0:T(8,128)(2,1)S(1)}, bf16[256,256]{1,0:T(8,128)(2,1)}, u32[]{:S(2)}) copy-start(bf16[256,256]{1,0:T(8,128)(2,1)} %constant.62.clone.refs_10_) | copy-start | bytes 393220
  34.3 10.8 %copy-start.10 = (bf16[256,256]{1,0:T(8,128)(2,1)S(1)}, bf16[256,256]{1,0:T(8,128)(2,1)}, u32[]{:S(2)}) copy-start(bf16[256,256]{1,0:T(8,128)(2,1)} %constant.61.clone.refs_9_) | copy-start | bytes 393220
  34.3 10.8 %copy-start.13 = (f32[3,64,128]{2,1,0:T(8,128)S(1)}, f32[3,64,128]{2,1,0:T(8,128)}, u32[]{:S(2)}) copy-start(f32[3,64,128]{2,1,0:T(8,128)} %constant.55.clone.refs_14_) | copy-start | bytes 294916
  34.3 10.8 %copy-start.16 = (f32[2,8,128]{2,1,0:T(8,128)S(1)}, f32[2,8,128]{2,1,0:T(8,128)}, u32[]{:S(2)}) copy-start(f32[2,8,128]{2,1,0:T(8,128)} %constant.54.clone.refs_12_) | copy-start | bytes 24580
  34.3 9.9 %collective-permute-start.12 = (f32[64,256]{1,0:T(8,128)S(1)}, f32[64,256]{1,0:T(8,128)S(1)}, u32[]{:S(2)}, u32[]{:S(2)}) collective-permute-start(f32[64,256]{1,0:T(8,128)S(1)} %get-tuple-element.125), channel_id=1, source_target_pairs={{0,1},{1,0},{2,3},{3,2},{4,5},{5,4},{6,7},{7,6},{8,9},{9,8},{10,11... | collective-permute-start | bytes 196616 | tf_op jit(solution)/shard_map/ppermute | solution.py:422
  35.9 8.4 %collective-permute-start.13 = (f32[64,256]{1,0:T(8,128)S(1)}, f32[64,256]{1,0:T(8,128)S(1)}, u32[]{:S(2)}, u32[]{:S(2)}) collective-permute-start(f32[64,256]{1,0:T(8,128)S(1)} %get-tuple-element.126), channel_id=1, source_target_pairs={{0,2},{1,3},{2,0},{3,1},{4,6},{5,7},{6,4},{7,5},{8,10},{9,11},{10,... | collective-permute-start | bytes 196616 | tf_op jit(solution)/shard_map/ppermute | solution.py:422
  38.5 6.5 %collective-permute-start.14 = (f32[64,256]{1,0:T(8,128)S(1)}, f32[64,256]{1,0:T(8,128)S(1)}, u32[]{:S(2)}, u32[]{:S(2)}) collective-permute-start(f32[64,256]{1,0:T(8,128)S(1)} %get-tuple-element.127), channel_id=1, source_target_pairs={{0,3},{1,2},{2,1},{3,0},{4,7},{5,6},{6,5},{7,4},{8,11},{9,10},{10,... | collective-permute-start | bytes 196616 | tf_op jit(solution)/shard_map/ppermute | solution.py:422
  39.9 7.5 %collective-permute-start.23 = (f32[64,256]{1,0:T(8,128)S(1)}, f32[64,256]{1,0:T(8,128)S(1)}, u32[]{:S(2)}, u32[]{:S(2)}) collective-permute-start(f32[64,256]{1,0:T(8,128)S(1)} %get-tuple-element.132), channel_id=1, source_target_pairs={{0,1},{1,0},{2,3},{3,2},{4,5},{5,4},{6,7},{7,6},{8,9},{9,8},{10,11... | collective-permute-start | bytes 196616 | tf_op jit(solution)/shard_map/ppermute | solution.py:422
  40.7 8.6 %collective-permute-start.24 = (f32[64,256]{1,0:T(8,128)S(1)}, f32[64,256]{1,0:T(8,128)S(1)}, u32[]{:S(2)}, u32[]{:S(2)}) collective-permute-start(f32[64,256]{1,0:T(8,128)S(1)} %get-tuple-element.133), channel_id=1, source_target_pairs={{0,2},{1,3},{2,0},{3,1},{4,6},{5,7},{6,4},{7,5},{8,10},{9,11},{10,... | collective-permute-start | bytes 196616 | tf_op jit(solution)/shard_map/ppermute | solution.py:422
  44.2 6.2 %collective-permute-start.25 = (f32[64,256]{1,0:T(8,128)S(1)}, f32[64,256]{1,0:T(8,128)S(1)}, u32[]{:S(2)}, u32[]{:S(2)}) collective-permute-start(f32[64,256]{1,0:T(8,128)S(1)} %get-tuple-element.134), channel_id=1, source_target_pairs={{0,3},{1,2},{2,1},{3,0},{4,7},{5,6},{6,5},{7,4},{8,11},{9,10},{10,... | collective-permute-start | bytes 196616 | tf_op jit(solution)/shard_map/ppermute | solution.py:422
  47.4 16.1 %copy-start.19 = (f32[16,8,4096]{2,1,0:T(8,128)S(1)}, f32[16,8,4096]{2,1,0:T(8,128)}, u32[]{:S(2)}) copy-start(f32[16,8,4096]{2,1,0:T(8,128)} %copy-done.18) | copy-start | bytes 6291460
  52.6 4.2 %collective-permute-start.28 = (f32[8,4096]{1,0:T(8,128)S(1)}, f32[8,4096]{1,0:T(8,128)S(1)}, u32[]{:S(2)}, u32[]{:S(2)}) collective-permute-start(f32[8,4096]{1,0:T(8,128)S(1)} %backward_1.1), channel_id=1, source_target_pairs={{0,4},{1,5},{2,6},{3,7},{4,0},{5,1},{6,2},{7,3},{8,12},{9,13},{10,... | collective-permute-start | bytes 393224 | tf_op jit(solution)/shard_map/ppermute | solution.py:418
  52.7 5.8 %collective-permute-start.27 = (f32[8,4096]{1,0:T(8,128)S(1)}, f32[8,4096]{1,0:T(8,128)S(1)}, u32[]{:S(2)}, u32[]{:S(2)}) collective-permute-start(f32[8,4096]{1,0:T(8,128)S(1)} %backward_1.1), channel_id=1, source_target_pairs={{0,16},{1,17},{2,18},{3,19},{4,12},{5,13},{6,14},{7,15},{8,24},{9,... | collective-permute-start | bytes 393224 | tf_op jit(solution)/shard_map/ppermute | solution.py:418
  54.2 6.0 %collective-permute-start.26 = (f32[8,4096]{1,0:T(8,128)S(1)}, f32[8,4096]{1,0:T(8,128)S(1)}, u32[]{:S(2)}, u32[]{:S(2)}) collective-permute-start(f32[8,4096]{1,0:T(8,128)S(1)} %backward_1.1), channel_id=1, source_target_pairs={{0,8},{1,9},{2,10},{3,11},{4,20},{5,21},{6,22},{7,23},{8,0},{9,1},... | collective-permute-start | bytes 393224 | tf_op jit(solution)/shard_map/ppermute | solution.py:418
  55.7 6.2 %collective-permute-start.16 = (f32[8,4096]{1,0:T(8,128)S(1)}, f32[8,4096]{1,0:T(8,128)S(1)}, u32[]{:S(2)}, u32[]{:S(2)}) collective-permute-start(f32[8,4096]{1,0:T(8,128)S(1)} %backward_0.1.refs_18_), channel_id=1, source_target_pairs={{0,16},{1,17},{2,18},{3,19},{4,12},{5,13},{6,14},{7,15},{8,24},{9,... | collective-permute-start | bytes 393224 | tf_op jit(solution)/shard_map/ppermute | solution.py:418
  56.3 5.8 %collective-permute-start.15 = (f32[8,4096]{1,0:T(8,128)S(1)}, f32[8,4096]{1,0:T(8,128)S(1)}, u32[]{:S(2)}, u32[]{:S(2)}) collective-permute-start(f32[8,4096]{1,0:T(8,128)S(1)} %backward_0.1.refs_18_), channel_id=1, source_target_pairs={{0,8},{1,9},{2,10},{3,11},{4,20},{5,21},{6,22},{7,23},{8,0},{9,1},... | collective-permute-start | bytes 393224 | tf_op jit(solution)/shard_map/ppermute | solution.py:418
  56.8 6.3 %collective-permute-start.17 = (f32[8,4096]{1,0:T(8,128)S(1)}, f32[8,4096]{1,0:T(8,128)S(1)}, u32[]{:S(2)}, u32[]{:S(2)}) collective-permute-start(f32[8,4096]{1,0:T(8,128)S(1)} %backward_0.1.refs_18_), channel_id=1, source_target_pairs={{0,4},{1,5},{2,6},{3,7},{4,0},{5,1},{6,2},{7,3},{8,12},{9,13},{10,... | collective-permute-start | bytes 393224 | tf_op jit(solution)/shard_map/ppermute | solution.py:418
  58.4 4.7 %collective-permute-start.30 = (f32[8,4096]{1,0:T(8,128)S(1)}, f32[8,4096]{1,0:T(8,128)S(1)}, u32[]{:S(2)}, u32[]{:S(2)}) collective-permute-start(f32[8,4096]{1,0:T(8,128)S(1)} %collective-permute-done.27), channel_id=1, source_target_pairs={{0,4},{1,5},{2,6},{3,7},{4,0},{5,1},{6,2},{7,3},{8,12},{9,13},{10,... | collective-permute-start | bytes 393224 | tf_op jit(solution)/shard_map/ppermute | solution.py:418
  60.2 2.9 %collective-permute-start.29 = (f32[8,4096]{1,0:T(8,128)S(1)}, f32[8,4096]{1,0:T(8,128)S(1)}, u32[]{:S(2)}, u32[]{:S(2)}) collective-permute-start(f32[8,4096]{1,0:T(8,128)S(1)} %collective-permute-done.26), channel_id=1, source_target_pairs={{0,4},{1,5},{2,6},{3,7},{4,0},{5,1},{6,2},{7,3},{8,12},{9,13},{10,... | collective-permute-start | bytes 393224 | tf_op jit(solution)/shard_map/ppermute | solution.py:418
  61.9 1.3 %collective-permute-start.19 = (f32[8,4096]{1,0:T(8,128)S(1)}, f32[8,4096]{1,0:T(8,128)S(1)}, u32[]{:S(2)}, u32[]{:S(2)}) collective-permute-start(f32[8,4096]{1,0:T(8,128)S(1)} %collective-permute-done.16), channel_id=1, source_target_pairs={{0,4},{1,5},{2,6},{3,7},{4,0},{5,1},{6,2},{7,3},{8,12},{9,13},{10,... | collective-permute-start | bytes 393224 | tf_op jit(solution)/shard_map/ppermute | solution.py:418
  62.0 1.4 %collective-permute-start.18 = (f32[8,4096]{1,0:T(8,128)S(1)}, f32[8,4096]{1,0:T(8,128)S(1)}, u32[]{:S(2)}, u32[]{:S(2)}) collective-permute-start(f32[8,4096]{1,0:T(8,128)S(1)} %collective-permute-done.15), channel_id=1, source_target_pairs={{0,4},{1,5},{2,6},{3,7},{4,0},{5,1},{6,2},{7,3},{8,12},{9,13},{10,... | collective-permute-start | bytes 393224 | tf_op jit(solution)/shard_map/ppermute | solution.py:418
  64.3 1.3 %copy-start.20 = (f32[16,8,4096]{2,1,0:T(8,128)}, f32[16,8,4096]{2,1,0:T(8,128)S(1)}, u32[]{:S(2)}) copy-start(f32[16,8,4096]{2,1,0:T(8,128)S(1)} %get-tuple-element.178) | copy-start | bytes 6291460
  (2 other events, 1.5 us)
where the time goes:
time: 66 us; the launch traced here: 65.7 us
  starting transfers between devices  26.6 us (40%)
  waiting for transfers between devices  17.9 us (27%)
  Pallas kernels  14 us (21%)
  local copies, waits for them, and re-layouts  5.8 us (9%)
  between operations  1.13 us (2%)
    ppermute x21, starting transfers between devices, swap(): return lax.ppermute(x, axes, moves)  17.7 us
    ppermute x21, waiting for transfers between devices, swap(): return lax.ppermute(x, axes, moves)  14.3 us
    ppermute x6, starting transfers between devices, cross(): return lax.ppermute(x, axes, moves)  8.9 us
    unnamed x47, local copies, waits for them, and re-layouts  5.63 us
    pallas_call x2, Pallas kernels, tile_device(): pl.pallas_call(functools.partial(backward_kernel, u, (CHUNKS, CHUNKS, len...  4.53 us
    ppermute x6, waiting for transfers between devices, cross(): return lax.ppermute(x, axes, moves)  3.62 us
    pallas_call x2, Pallas kernels, tile_device(): pl.pallas_call(functools.partial(forward_kernel, u, counts + (n_grid - 1,...  2.33 us
    pallas_call x3, Pallas kernels, tile_device(): pl.pallas_call(finish_kernel, out_shape=jax.ShapeDtypeStruct(passed.shape...  1.94 us
  transfers between devices with their start and end apart: 27, of which 12 were waited for; matrix products, arithmetic and copies ran while one was open for 1% of the time, Pallas kernels for 17%

commit v1 on v0

--- a/solution.py
+++ b/solution.py
@@ -120,10 +120,22 @@
     copy.wait()
 
 
-def setup_kernel(per_device, tiles, host, rotation, mask, high, low, flags, match, alone):
+def setup_kernel(per_device, n_grid, tiles, host, rotation, mask, log_r, high, low, powers, flags, match, alone):
     o, core, chip = my_place()
-    chips = tiles.shape[0] // 2
-    owners = [lax.div(tiles[2 * t] * BLK, 2 * per_device) for t in range(chips)]
+    at, size_x = SUB * lax.axis_index("grid"), SUB * n_grid
+    exponents = (
+        2 * at + SUB + 1,
+        2 * size_x + 1 - SUB - 2 * at,
+        2 * size_x + 2 - 2 * at,
+        2 * at,
+        2 * at + 2 * SUB + 2,
+        2 * size_x - 2 * SUB - 2 * at,
+    )
+    for n, exponent in enumerate(exponents):
+        power = jnp.exp(exponent.astype(f32) * log_r[...])
+        powers[n] = power if n < 2 else 1.0 - power
+    chips = tiles.shape[0]
+    owners = [lax.div(tiles[t, 0] * BLK, 2 * per_device) for t in range(chips)]
     key = 0
     for t in range(chips):
         key = key + owners[t] * chips**t
@@ -138,7 +150,7 @@
     heads = []
     for where in order:
         tile = host[key * chips + where]
-        heads.append((BLK * tiles[2 * tile], BLK * tiles[2 * tile + 1]))
+        heads.append((BLK * tiles[tile, 0], BLK * tiles[tile, 1]))
     wanted = []
     for a, b in heads:
         wanted += [a + (1 - core) * pair] + [b + w for w in range(BLK)] + [a + core * pair]
@@ -170,7 +182,7 @@
     blocks = per_device // BLK
     parts = [chip, chip ^ bit_1, chip ^ bit_2, chip ^ 3, chip, chip ^ bit_2, chip ^ bit_1, chip ^ 3]
     for n, where in enumerate(parts):
-        home = tiles[2 * host[key * chips + where]]
+        home = tiles[host[key * chips + where], 0]
         for block in range(blocks):
             hit = home == o * blocks + block
             if n % 4 == 3:
@@ -401,7 +413,7 @@
 
 
 def tile_device(orbitals, rotation, tile_list, pair_mask):
-    per_device, planes, width = orbitals.shape
+    shape = per_device, planes, width = orbitals.shape
     n_orb, n_grid = lax.axis_size("orb"), lax.axis_size("grid")
     size_x = planes * n_grid
     half = width // 2
@@ -422,6 +434,7 @@
         return lax.ppermute(x, axes, moves)
 
     chunk = half // CHUNKS
+    orbitals = pltpu.with_memory_space_constraint(orbitals, pltpu.HBM)
 
     def take(flip, start, lanes, *after):
         return pl.pallas_call(
@@ -444,12 +457,13 @@
     rows = (firsts + 2 * (pair - 1) * chips) * SUB
     wide_table = jax.ShapeDtypeStruct((rows, 2 * LANES), bf16)
     blocks = per_device // BLK
-    high, low, flags, match, alone = pl.pallas_call(
-        functools.partial(setup_kernel, per_device),
-        out_shape=(wide_table, wide_table, jax.ShapeDtypeStruct((pair * BLK,), f32),
+    c, r = line_np()
+    high, low, powers, flags, match, alone = pl.pallas_call(
+        functools.partial(setup_kernel, per_device, n_grid),
+        out_shape=(wide_table, wide_table, jax.ShapeDtypeStruct((6, NY, LANES), f32), jax.ShapeDtypeStruct((pair * BLK,), f32),
                    jax.ShapeDtypeStruct((blocks * 8,), jnp.int32), jax.ShapeDtypeStruct((1,), jnp.int32)),
-        in_specs=[SM, SM, VM, VM], out_specs=(VM, VM, SM, SM, SM), name="setup", compiler_params=grant(8),
-    )(tile_list.reshape(-1), jnp.asarray(host_np(chips).reshape(-1)), rotation, pair_mask)
+        in_specs=[SM, SM, VM, VM, VM], out_specs=(VM, VM, VM, SM, SM, SM), name="setup", compiler_params=grant(4),
+    )(tile_list, jnp.asarray(host_np(chips).reshape(-1)), rotation, pair_mask, jnp.asarray(np.log(r), f32))
 
     def rotate(first, count, fields, name, *after):
         part = jax.ShapeDtypeStruct((count, planes, chunk * (len(fields) // 2)), f32)
@@ -467,45 +481,45 @@
     both = [x for n in range(CHUNKS) for x in (mine[n], theirs[n])]
     sums.append(rotate(firsts, (pair - 1) * chips, both, "rotate_rest", *last))
     empty = pl.pallas_call(
-        clear_kernel, out_shape=jax.ShapeDtypeStruct(orbitals.shape, f32), in_specs=[ANY], out_specs=HBM,
+        clear_kernel, out_shape=pltpu.HBM(shape, f32), in_specs=[ANY], out_specs=HBM,
         scratch_shapes=[pltpu.VMEM((pair, planes, width), f32), DMA((per_device // pair,))], name="clear",
         compiler_params=grant(4),
     )(sums[-1][0])
-    passing, last, specs = [], (empty,), [HBM]
-    for n, (send, keep, got) in enumerate(sums):
-        shape = (keep.shape[0] // 2,) + keep.shape[1:]
+    passing, own, other = [], [], []
+
+    def pass_on(n, *after, spec=ANY):
+        send, keep, got = sums[n]
+        count = keep.shape[0] // 2
         value = pl.pallas_call(
-            pass_kernel, out_shape=jax.ShapeDtypeStruct(shape, f32), in_specs=[VM] * 2 + specs, out_specs=VM,
-            name=f"pass_{n}", compiler_params=grant(4),
-        )(keep, got, *last)
-        last, specs = (value,), [ANY]
+            pass_kernel, out_shape=jax.ShapeDtypeStruct((count,) + keep.shape[1:], f32),
+            in_specs=[VM] * 2 + [spec] * len(after), out_specs=VM, name=f"pass_{n}", compiler_params=grant(4),
+        )(keep, got, *after)
         passing.append((keep, got, swap(value, 4, 2)))
-    own, other = [], []
-    for n, (keep, got, passed) in enumerate(passing):
+        return value
+
+    def finish(n, *after):
+        keep, got, passed = passing[n]
         own.append(pl.pallas_call(
-            finish_kernel, out_shape=jax.ShapeDtypeStruct(passed.shape, f32), in_specs=[VM] * 3 + [ANY] * len(own[-1:]),
+            finish_kernel, out_shape=jax.ShapeDtypeStruct(passed.shape, f32), in_specs=[VM] * 3 + [ANY] * len(after),
             out_specs=VM, name=f"finish_{n}", compiler_params=grant(4),
-        )(keep, got, passed, *own[-1:]))
+        )(keep, got, passed, *after))
         other.append(swap(own[-1], 1, 1))
-
-    c, r = line_np()
+        return own[-1]
+
+    step = pass_on(0, empty, spec=HBM)
+    for n in range(1, CHUNKS):
+        step = pass_on(n, step)
+    step = finish(0, step)
+    step = pass_on(CHUNKS, step)
+    for n in range(1, CHUNKS):
+        step = finish(n, step)
+
     sine_x, eigen_x = sine_np(planes), eigen_np(planes)
     ends = jnp.asarray(np.einsum("jp,pkl->kjl", sine_x, r[None] ** np.arange(planes - 1, -1, -1)[:, None, None])
                        .reshape(-1, LANES), f32)
     inverse = jnp.asarray((COUPLING / (eigen_x[None, :, None] + c[:, None, :])).reshape(-1, LANES), f32)
     basis = jnp.asarray(np.broadcast_to(sine_x[:, [0, -1]].T[:, :, None], (2, planes, LANES)), f32)
     steady = jnp.asarray(np.stack([r / ((1 - r**2) * (1 - r ** (2 * size_x + 2))), r, r**planes]), f32)
-    at = planes * g
-    exponents = jnp.stack([
-        2 * at + planes + 1,
-        2 * size_x + 1 - planes - 2 * at,
-        2 * size_x + 2 - 2 * at,
-        2 * at,
-        2 * at + 2 * planes + 2,
-        2 * size_x - 2 * planes - 2 * at,
-    ]).astype(f32)
-    powers = jnp.exp(exponents[:, None, None] * jnp.asarray(np.log(r), f32)[None])
-    powers = jnp.where(jnp.arange(6)[:, None, None] < 2, powers, 1.0 - powers)
 
     y_hi, y_lo = halves_np(y_table())
     z_hi, z_lo = halves_np(z_table())
@@ -517,6 +531,8 @@
     base_own, base_other = own[:CHUNKS], other[:CHUNKS]
     last = ()
     for u in range(pair):
+        if u:
+            finish(CHUNKS, *last)
         more_own, more_other = own[CHUNKS:][:u], other[CHUNKS:][:u]
         counts = (CHUNKS, CHUNKS, len(more_own), len(more_other))
         inputs = [*base_own, *base_other, *more_own, *more_other, y_hi, y_lo, z_hi, z_lo, ends, powers]
@@ -556,7 +572,7 @@
         parts = [part for group in groups for part in group]
         return pl.pallas_call(
             functools.partial(place_kernel, 8),
-            out_shape=jax.ShapeDtypeStruct(orbitals.shape, f32),
+            out_shape=pltpu.HBM(shape, f32),
             in_specs=[SM] + [VM] * len(parts) + [HBM],
             out_specs=HBM,
             input_output_aliases={len(parts) + 1: 0},

time: 66 us -> 62.4 us (0.945)
  the two profiles are of different devices: /device:TPU:0 before, /device:TPU:16 now
where the time goes in v1:
time: 62.4 us; the launch traced here: 61.8 us
  starting transfers between devices  22.6 us (36%)
  waiting for transfers between devices  20.7 us (33%)
  Pallas kernels  17.3 us (28%)
  between operations  1.03 us (2%)
    ppermute x21, waiting for transfers between devices, swap(): return lax.ppermute(x, axes, moves)  15.9 us
    ppermute x21, starting transfers between devices, swap(): return lax.ppermute(x, axes, moves)  15 us
    ppermute x6, starting transfers between devices, cross(): return lax.ppermute(x, axes, moves)  7.64 us
    ppermute x6, waiting for transfers between devices, cross(): return lax.ppermute(x, axes, moves)  4.71 us
    pallas_call x2, Pallas kernels, tile_device(): pl.pallas_call(functools.partial(backward_kernel, u, (CHUNKS, CHUNKS, len...  4.54 us
    pallas_call x4, Pallas kernels, take(): pl.pallas_call(functools.partial(take_kernel, flip, start), out_shape=jax...  4.21 us
    pallas_call x2, Pallas kernels, tile_device(): pl.pallas_call(functools.partial(forward_kernel, u, counts + (n_grid - 1,...  2.33 us
    pallas_call x3, Pallas kernels, rotate(): pl.pallas_call(functools.partial(rotate_kernel, first * SUB), out_shape=(...  1.68 us
  transfers between devices with their start and end apart: 27, of which 9 were waited for; matrix products, arithmetic and copies ran while one was open for 0% of the time, Pallas kernels for 24%

profile of v1, /device:TPU:16, one launch (start us, length us, event | category | flops | bytes accessed | tf_op | source)
XLA Modules:
  0.0 61.8 jit_solution(3284827179077724202)
XLA Ops:
  0.0 1.0 %take_1_0.1.rest_0_ = f32[16,8,1024]{2,1,0:T(8,128)S(1)} custom-call(f32[16,8,4096]{2,1,0:T(8,128)} %source.7), custom_call_target="tpu_custom_call" | custom-call | tf_op jit(solution)/shard_map/take_1_0/pallas_call | solution.py:440
  1.1 0.1 collective-permute-start.4
  1.1 1.1 %take_1_1024.1.rest_0_ = f32[16,8,1024]{2,1,0:T(8,128)S(1)} custom-call(f32[16,8,4096]{2,1,0:T(8,128)} %source.7, f32[16,8,1024]{2,1,0:T(8,128)S(1)} %take_1_0.1.rest_0_), custom_call_target="tpu_custom_call" | custom-call | tf_op jit(solution)/shard_map/take_1_1024/pallas_call | solution.py:440
  2.3 0.5 collective-permute-start.6
  2.8 1.0 %take_0_0.1.rest_0_ = f32[16,8,1024]{2,1,0:T(8,128)S(1)} custom-call(f32[16,8,4096]{2,1,0:T(8,128)} %source.7, f32[16,8,1024]{2,1,0:T(8,128)S(1)} %take_1_1024.1.rest_0_), custom_call_target="tpu_custom_call" | custom-call | tf_op jit(solution)/shard_map/take_0_0/pallas_call | solution.py:440
  3.9 0.1 copy.21.tiles
  4.0 1.6 %setup.1 = (bf16[256,256]{1,0:T(8,128)(2,1)S(1)}, bf16[256,256]{1,0:T(8,128)(2,1)S(1)}, f32[6,64,128]{2,1,0:T(8,128)S(1)}, f32[8]{0:T(128)S(1)}, s32[32]{0:T(128)S(1)}, /*index=5*/s32[1]{0:T(128)}) custom-call(s32[4,2]{1,0:T(4,128)S(1)} %copy.21.tiles, s32[1024]{0:T(1024)S(1)} %copy-done.13, f32[128,128]{1,0:T(8,128)S(1)} %copy-done.9, ...), custom_call_target="tpu_custom_call" | custom-call | tf_op jit(solution)/shard_map/setup/pallas_call | solution.py:461
  5.6 0.5 rotate_0.1
  6.1 1.6 %collective-permute-start.5 = (f32[12,8,1024]{2,1,0:T(8,128)S(1)}, f32[12,8,1024]{2,1,0:T(8,128)S(1)}, u32[]{:S(2)}, u32[]{:S(2)}) collective-permute-start(f32[12,8,1024]{2,1,0:T(8,128)S(1)} %get-tuple-element.122.rest_2_), channel_id=1, source_target_pairs={{0,8},{1,9},{2,10},{3,11},{4,20},{5,21},{6,22},{7,23},{8,0},{9,1},... | collective-permute-start | bytes 1179656 | tf_op jit(solution)/shard_map/ppermute | solution.py:430
  7.6 1.0 %take_0_1024.1.rest_0_.rest_2_ = f32[16,8,1024]{2,1,0:T(8,128)S(1)} custom-call(f32[16,8,4096]{2,1,0:T(8,128)} %source.7, f32[16,8,1024]{2,1,0:T(8,128)S(1)} %take_1_1024.1.rest_0_), custom_call_target="tpu_custom_call" | custom-call | tf_op jit(solution)/shard_map/take_0_1024/pallas_call | solution.py:440
  8.7 0.5 rotate_1.1
  9.2 0.6 collective-permute-start.8
  9.8 0.7 %rotate_rest.1 = (f32[4,8,2048]{2,1,0:T(8,128)S(1)}, f32[4,8,2048]{2,1,0:T(8,128)S(1)}) custom-call(bf16[256,256]{1,0:T(8,128)(2,1)S(1)} %get-tuple-element.119.high, bf16[256,256]{1,0:T(8,128)(2,1)S(1)} %get-tuple-element.120.low, f32[16,8,1024]{2,1,0:T(8,128)S(1)} %take_0_0.1.rest_0_, f32[16,8,1024]{2,1,0:T(8,128)S(1)} %collective-permute-done.4.rest_1_, ...), custom_call_target="tpu_custom_call" | custom-call | tf_op jit(solution)/shard_map/rotate_rest/pallas_call | solution.py:470
  10.5 1.6 %collective-permute-start.10 = (f32[4,8,2048]{2,1,0:T(8,128)S(1)}, f32[4,8,2048]{2,1,0:T(8,128)S(1)}, u32[]{:S(2)}, u32[]{:S(2)}) collective-permute-start(f32[4,8,2048]{2,1,0:T(8,128)S(1)} %get-tuple-element.124.refs_0_), channel_id=1, source_target_pairs={{0,8},{1,9},{2,10},{3,11},{4,20},{5,21},{6,22},{7,23},{8,0},{9,1},... | collective-permute-start | bytes 786440 | tf_op jit(solution)/shard_map/ppermute | solution.py:430
  12.1 1.4 %clear.1.rest_0_ = f32[16,8,4096]{2,1,0:T(8,128)} custom-call(f32[4,8,2048]{2,1,0:T(8,128)S(1)} %get-tuple-element.124.refs_0_), custom_call_target="tpu_custom_call" | custom-call | tf_op jit(solution)/shard_map/clear/pallas_call | solution.py:483
  13.5 0.5 collective-permute-done.5.got
  14.0 1.6 %collective-permute-start.7 = (f32[6,8,1024]{2,1,0:T(8,128)S(1)}, f32[6,8,1024]{2,1,0:T(8,128)S(1)}, u32[]{:S(2)}, u32[]{:S(2)}) collective-permute-start(f32[6,8,1024]{2,1,0:T(8,128)S(1)} %pass_0.1.rest_0_), channel_id=1, source_target_pairs={{0,16},{1,17},{2,18},{3,19},{4,12},{5,13},{6,14},{7,15},{8,24},{9,... | collective-permute-start | bytes 589832 | tf_op jit(solution)/shard_map/ppermute | solution.py:430
  15.5 4.9 %collective-permute-done.8.got = f32[12,8,1024]{2,1,0:T(8,128)S(1)} collective-permute-done((f32[12,8,1024]{2,1,0:T(8,128)S(1)}, f32[12,8,1024]{2,1,0:T(8,128)S(1)}, u32[]{:S(2)}, u32[]{:S(2)}) %collective-permute-start.8) | collective-permute-done | bytes 393248 | tf_op jit(solution)/shard_map/ppermute | solution.py:430
  20.5 1.6 %collective-permute-start.9 = (f32[6,8,1024]{2,1,0:T(8,128)S(1)}, f32[6,8,1024]{2,1,0:T(8,128)S(1)}, u32[]{:S(2)}, u32[]{:S(2)}) collective-permute-start(f32[6,8,1024]{2,1,0:T(8,128)S(1)} %pass_1.1.rest_0_), channel_id=1, source_target_pairs={{0,16},{1,17},{2,18},{3,19},{4,12},{5,13},{6,14},{7,15},{8,24},{9,... | collective-permute-start | bytes 589832 | tf_op jit(solution)/shard_map/ppermute | solution.py:430
  22.1 3.0 %collective-permute-done.10.got = f32[4,8,2048]{2,1,0:T(8,128)S(1)} collective-permute-done((f32[4,8,2048]{2,1,0:T(8,128)S(1)}, f32[4,8,2048]{2,1,0:T(8,128)S(1)}, u32[]{:S(2)}, u32[]{:S(2)}) %collective-permute-start.10) | collective-permute-done | bytes 262176 | tf_op jit(solution)/shard_map/ppermute | solution.py:430
  25.2 1.1 %collective-permute-done.9.passed = f32[6,8,1024]{2,1,0:T(8,128)S(1)} collective-permute-done((f32[6,8,1024]{2,1,0:T(8,128)S(1)}, f32[6,8,1024]{2,1,0:T(8,128)S(1)}, u32[]{:S(2)}, u32[]{:S(2)}) %collective-permute-start.9) | collective-permute-done | bytes 196640 | tf_op jit(solution)/shard_map/ppermute | solution.py:430
  26.3 0.1 collective-permute-start.12
  26.4 0.5 collective-permute-start.11
  26.9 1.5 %collective-permute-start.21 = (f32[2,8,2048]{2,1,0:T(8,128)S(1)}, f32[2,8,2048]{2,1,0:T(8,128)S(1)}, u32[]{:S(2)}, u32[]{:S(2)}) collective-permute-start(f32[2,8,2048]{2,1,0:T(8,128)S(1)} %pass_2.1.rest_0_), channel_id=1, source_target_pairs={{0,16},{1,17},{2,18},{3,19},{4,12},{5,13},{6,14},{7,15},{8,24},{9,... | collective-permute-start | bytes 393224 | tf_op jit(solution)/shard_map/ppermute | solution.py:430
  28.4 1.2 %forward_0.1 = (f32[64,256]{1,0:T(8,128)S(1)}, f32[64,256]{1,0:T(8,128)S(1)}, f32[64,256]{1,0:T(8,128)S(1)}, f32[512,256]{1,0:T(8,128)S(1)}, f32[64,256]{1,0:T(8,128)S(1)}, /*index=5*/f32[64,256]{1,0:T(8,128)S(1)}) custom-call(f32[6,8,1024]{2,1,0:T(8,128)S(1)} %finish_0.1.rest_0_.refs_0_, f32[6,8,1024]{2,1,0:T(8,128)S(1)} %finish_1.1.refs_1_, ...), custom_call_target="tpu_custom_call" | custom-call | tf_op jit(solution)/shard_map/forward_0/pallas_call | solution.py:539
  29.6 2.2 %collective-permute-done.21.passed = f32[2,8,2048]{2,1,0:T(8,128)S(1)} collective-permute-done((f32[2,8,2048]{2,1,0:T(8,128)S(1)}, f32[2,8,2048]{2,1,0:T(8,128)S(1)}, u32[]{:S(2)}, u32[]{:S(2)}) %collective-permute-start.21) | collective-permute-done | bytes 131104 | tf_op jit(solution)/shard_map/ppermute | solution.py:430
  31.9 0.1 collective-permute-start.22
  32.0 1.6 %collective-permute-start.13 = (f32[64,256]{1,0:T(8,128)S(1)}, f32[64,256]{1,0:T(8,128)S(1)}, u32[]{:S(2)}, u32[]{:S(2)}) collective-permute-start(f32[64,256]{1,0:T(8,128)S(1)} %get-tuple-element.128), channel_id=1, source_target_pairs={{0,1},{1,0},{2,3},{3,2},{4,5},{5,4},{6,7},{7,6},{8,9},{9,8},{10,11... | collective-permute-start | bytes 196616 | tf_op jit(solution)/shard_map/ppermute | solution.py:434
  33.6 0.3 collective-permute-start.14
  34.0 1.6 %collective-permute-start.15 = (f32[64,256]{1,0:T(8,128)S(1)}, f32[64,256]{1,0:T(8,128)S(1)}, u32[]{:S(2)}, u32[]{:S(2)}) collective-permute-start(f32[64,256]{1,0:T(8,128)S(1)} %get-tuple-element.130), channel_id=1, source_target_pairs={{0,3},{1,2},{2,1},{3,0},{4,7},{5,6},{6,5},{7,4},{8,11},{9,10},{10,... | collective-permute-start | bytes 196616 | tf_op jit(solution)/shard_map/ppermute | solution.py:434
  35.5 1.2 %forward_1.1 = (f32[64,256]{1,0:T(8,128)S(1)}, f32[64,256]{1,0:T(8,128)S(1)}, f32[64,256]{1,0:T(8,128)S(1)}, f32[512,256]{1,0:T(8,128)S(1)}, f32[64,256]{1,0:T(8,128)S(1)}, /*index=5*/f32[64,256]{1,0:T(8,128)S(1)}) custom-call(f32[6,8,1024]{2,1,0:T(8,128)S(1)} %finish_0.1.rest_0_.refs_0_, f32[6,8,1024]{2,1,0:T(8,128)S(1)} %finish_1.1.refs_1_, ...), custom_call_target="tpu_custom_call" | custom-call | tf_op jit(solution)/shard_map/forward_1/pallas_call | solution.py:539
  36.7 2.5 %collective-permute-start.23 = (f32[64,256]{1,0:T(8,128)S(1)}, f32[64,256]{1,0:T(8,128)S(1)}, u32[]{:S(2)}, u32[]{:S(2)}) collective-permute-start(f32[64,256]{1,0:T(8,128)S(1)} %get-tuple-element.134), channel_id=1, source_target_pairs={{0,1},{1,0},{2,3},{3,2},{4,5},{5,4},{6,7},{7,6},{8,9},{9,8},{10,11... | collective-permute-start | bytes 196616 | tf_op jit(solution)/shard_map/ppermute | solution.py:434
  39.3 1.5 %collective-permute-start.25 = (f32[64,256]{1,0:T(8,128)S(1)}, f32[64,256]{1,0:T(8,128)S(1)}, u32[]{:S(2)}, u32[]{:S(2)}) collective-permute-start(f32[64,256]{1,0:T(8,128)S(1)} %get-tuple-element.136), channel_id=1, source_target_pairs={{0,3},{1,2},{2,1},{3,0},{4,7},{5,6},{6,5},{7,4},{8,11},{9,10},{10,... | collective-permute-start | bytes 196616 | tf_op jit(solution)/shard_map/ppermute | solution.py:434
  40.8 4.7 %collective-permute-done.15.refs_6_ = f32[64,256]{1,0:T(8,128)S(1)} collective-permute-done((f32[64,256]{1,0:T(8,128)S(1)}, f32[64,256]{1,0:T(8,128)S(1)}, u32[]{:S(2)}, u32[]{:S(2)}) %collective-permute-start.15) | collective-permute-done | bytes 65568 | tf_op jit(solution)/shard_map/ppermute | solution.py:434
  45.5 2.3 %backward_0.1.refs_18_ = f32[8,4096]{1,0:T(8,128)S(1)} custom-call(f32[8]{0:T(128)S(1)} %get-tuple-element.118.flags, f32[6,8,1024]{2,1,0:T(8,128)S(1)} %finish_0.1.rest_0_.refs_0_, f32[6,8,1024]{2,1,0:T(8,128)S(1)} %finish_1.1.refs_1_, f32[6,8,1024]{2,1,0:T(8,128)S(1)} %collective-permute-done.11.refs_2_, ...), custom_call_target="tpu_custom_call" | custom-call | tf_op jit(solution)/shard_map/backward_0/pallas_call | solution.py:555
  47.8 0.1 collective-permute-start.18
  47.9 1.6 %collective-permute-start.17 = (f32[8,4096]{1,0:T(8,128)S(1)}, f32[8,4096]{1,0:T(8,128)S(1)}, u32[]{:S(2)}, u32[]{:S(2)}) collective-permute-start(f32[8,4096]{1,0:T(8,128)S(1)} %backward_0.1.refs_18_), channel_id=1, source_target_pairs={{0,16},{1,17},{2,18},{3,19},{4,12},{5,13},{6,14},{7,15},{8,24},{9,... | collective-permute-start | bytes 393224 | tf_op jit(solution)/shard_map/ppermute | solution.py:430
  49.5 1.5 %collective-permute-start.16 = (f32[8,4096]{1,0:T(8,128)S(1)}, f32[8,4096]{1,0:T(8,128)S(1)}, u32[]{:S(2)}, u32[]{:S(2)}) collective-permute-start(f32[8,4096]{1,0:T(8,128)S(1)} %backward_0.1.refs_18_), channel_id=1, source_target_pairs={{0,8},{1,9},{2,10},{3,11},{4,20},{5,21},{6,22},{7,23},{8,0},{9,1},... | collective-permute-start | bytes 393224 | tf_op jit(solution)/shard_map/ppermute | solution.py:430
  51.0 2.3 %backward_1.1 = f32[8,4096]{1,0:T(8,128)S(1)} custom-call(f32[8]{0:T(128)S(1)} %get-tuple-element.118.flags, f32[6,8,1024]{2,1,0:T(8,128)S(1)} %finish_0.1.rest_0_.refs_0_, f32[6,8,1024]{2,1,0:T(8,128)S(1)} %finish_1.1.refs_1_, f32[6,8,1024]{2,1,0:T(8,128)S(1)} %collective-permute-done.11.refs_2_, f32[6,8,1024]{2,1,0:T(8,128)S(1)} %collective-permute-done.12.refs_3_, ...), custom_call_target="tpu_custom_call" | custom-call | tf_op jit(solution)/shard_map/backward_1/pallas_call | solution.py:555
  53.2 0.6 collective-permute-start.27
  53.8 0.5 collective-permute-start.26
  54.4 0.5 collective-permute-start.20
  54.9 3.9 %collective-permute-done.27 = f32[8,4096]{1,0:T(8,128)S(1)} collective-permute-done((f32[8,4096]{1,0:T(8,128)S(1)}, f32[8,4096]{1,0:T(8,128)S(1)}, u32[]{:S(2)}, u32[]{:S(2)}) %collective-permute-start.27) | collective-permute-done | bytes 131104 | tf_op jit(solution)/shard_map/ppermute | solution.py:430
  58.8 0.5 collective-permute-start.29
  60.1 0.1 collective-permute-done.30
  60.2 0.2 collective-permute-done.29
  60.4 1.5 %conditional.1 = (f32[16,8,4096]{2,1,0:T(8,128)}) conditional(s32[]{:T(128)} %bitcast, (s32[32]{0:T(128)S(1)}, f32[8,4096]{1,0:T(8,128)S(1)}, f32[8,4096]{1,0:T(8,128)S(1)}, f32[8,4096]{1,0:T(8,128)S(1)}, f32[8,4096]{1,0:T(8,128)S(1)}, /*index=5*/f32[8,4096]{1,0:T(8,128)S(1)}, f32[8,4096]{1,0:T(8,128)S(1)}, f32[8,4096]{1,0:T(8,128)S(1)}, ...), branch_computations={%region_0.0_spmd, %region_1.0_spmd} | conditional | bytes 2097320 | solution.py:591
  60.4 1.5 %place.2 = f32[16,8,4096]{2,1,0:T(8,128)} custom-call(s32[32]{0:T(128)S(1)} %get-tuple-element.64.match, f32[8,4096]{1,0:T(8,128)S(1)} %get-tuple-element.65.refs_0_, f32[8,4096]{1,0:T(8,128)S(1)} %get-tuple-element.66.refs_1_, f32[8,4096]{1,0:T(8,128)S(1)} %get-tuple-element.67.refs_2_, ...), custom_call_target="tpu_custom_call", output_to_operand_aliasing={{}: (13, {})} | custom-call | tf_op jit(solution)/shard_map/cond/branch_0_fun/place/pallas_call | solution.py:573
  (58 shorter events, 0.4 us)
Async XLA Ops:
  1.1 4.5 %collective-permute-start.4 = (f32[16,8,1024]{2,1,0:T(8,128)S(1)}, f32[16,8,1024]{2,1,0:T(8,128)S(1)}, u32[]{:S(2)}, u32[]{:S(2)}) collective-permute-start(f32[16,8,1024]{2,1,0:T(8,128)S(1)} %take_1_0.1.rest_0_), channel_id=1, source_target_pairs={{0,4},{1,5},{2,6},{3,7},{4,0},{5,1},{6,2},{7,3},{8,12},{9,13},{10,... | collective-permute-start | bytes 1572872 | tf_op jit(solution)/shard_map/ppermute | solution.py:430
  2.2 1.7 %copy-start.14 = (s32[4,2]{0,1:T(2,128)S(1)}, s32[4,2]{0,1:T(2,128)}, u32[]{:S(2)}) copy-start(s32[4,2]{0,1:T(2,128)} %param.20) | copy-start | bytes 100
  2.2 1.8 %copy-start.9 = (f32[128,128]{1,0:T(8,128)S(1)}, f32[128,128]{1,0:T(8,128)}, u32[]{:S(2)}) copy-start(f32[128,128]{1,0:T(8,128)} %rotation.1) | copy-start | bytes 196612
  2.2 1.7 %copy-start.10 = (s32[128,128]{1,0:T(8,128)S(1)}, s32[128,128]{1,0:T(8,128)}, u32[]{:S(2)}) copy-start(s32[128,128]{1,0:T(8,128)} %mask.1) | copy-start | bytes 196612
  2.2 1.7 %copy-start.12 = (f32[64,128]{1,0:T(8,128)S(1)}, f32[64,128]{1,0:T(8,128)}, u32[]{:S(2)}) copy-start(f32[64,128]{1,0:T(8,128)} %constant.28.clone.log_r) | copy-start | bytes 98308
  2.3 1.7 %copy-start.13 = (s32[1024]{0:T(1024)S(1)}, s32[1024]{0:T(1024)}, u32[]{:S(2)}) copy-start(s32[1024]{0:T(1024)} %constant.27.clone.host) | copy-start | bytes 12292
  2.3 6.4 %collective-permute-start.6 = (f32[16,8,1024]{2,1,0:T(8,128)S(1)}, f32[16,8,1024]{2,1,0:T(8,128)S(1)}, u32[]{:S(2)}, u32[]{:S(2)}) collective-permute-start(f32[16,8,1024]{2,1,0:T(8,128)S(1)} %take_1_1024.1.rest_0_), channel_id=1, source_target_pairs={{0,4},{1,5},{2,6},{3,7},{4,0},{5,1},{6,2},{7,3},{8,12},{9,13},{10,... | collective-permute-start | bytes 1572872 | tf_op jit(solution)/shard_map/ppermute | solution.py:430
  6.1 7.8 %collective-permute-start.5 = (f32[12,8,1024]{2,1,0:T(8,128)S(1)}, f32[12,8,1024]{2,1,0:T(8,128)S(1)}, u32[]{:S(2)}, u32[]{:S(2)}) collective-permute-start(f32[12,8,1024]{2,1,0:T(8,128)S(1)} %get-tuple-element.122.rest_2_), channel_id=1, source_target_pairs={{0,8},{1,9},{2,10},{3,11},{4,20},{5,21},{6,22},{7,23},{8,0},{9,1},... | collective-permute-start | bytes 1179656 | tf_op jit(solution)/shard_map/ppermute | solution.py:430
  9.2 11.3 %collective-permute-start.8 = (f32[12,8,1024]{2,1,0:T(8,128)S(1)}, f32[12,8,1024]{2,1,0:T(8,128)S(1)}, u32[]{:S(2)}, u32[]{:S(2)}) collective-permute-start(f32[12,8,1024]{2,1,0:T(8,128)S(1)} %get-tuple-element.123.rest_4_), channel_id=1, source_target_pairs={{0,8},{1,9},{2,10},{3,11},{4,20},{5,21},{6,22},{7,23},{8,0},{9,1},... | collective-permute-start | bytes 1179656 | tf_op jit(solution)/shard_map/ppermute | solution.py:430
  10.5 14.7 %collective-permute-start.10 = (f32[4,8,2048]{2,1,0:T(8,128)S(1)}, f32[4,8,2048]{2,1,0:T(8,128)S(1)}, u32[]{:S(2)}, u32[]{:S(2)}) collective-permute-start(f32[4,8,2048]{2,1,0:T(8,128)S(1)} %get-tuple-element.124.refs_0_), channel_id=1, source_target_pairs={{0,8},{1,9},{2,10},{3,11},{4,20},{5,21},{6,22},{7,23},{8,0},{9,1},... | collective-permute-start | bytes 786440 | tf_op jit(solution)/shard_map/ppermute | solution.py:430
  14.0 8.1 %collective-permute-start.7 = (f32[6,8,1024]{2,1,0:T(8,128)S(1)}, f32[6,8,1024]{2,1,0:T(8,128)S(1)}, u32[]{:S(2)}, u32[]{:S(2)}) collective-permute-start(f32[6,8,1024]{2,1,0:T(8,128)S(1)} %pass_0.1.rest_0_), channel_id=1, source_target_pairs={{0,16},{1,17},{2,18},{3,19},{4,12},{5,13},{6,14},{7,15},{8,24},{9,... | collective-permute-start | bytes 589832 | tf_op jit(solution)/shard_map/ppermute | solution.py:430
  20.5 7.9 %copy-start = (bf16[512,512]{1,0:T(8,128)(2,1)S(1)}, bf16[512,512]{1,0:T(8,128)(2,1)}, u32[]{:S(2)}) copy-start(bf16[512,512]{1,0:T(8,128)(2,1)} %constant.34.clone.refs_5_.refs_8_.refs_7_) | copy-start | bytes 1572868
  20.5 7.9 %copy-start.1 = (bf16[512,512]{1,0:T(8,128)(2,1)S(1)}, bf16[512,512]{1,0:T(8,128)(2,1)}, u32[]{:S(2)}) copy-start(bf16[512,512]{1,0:T(8,128)(2,1)} %constant.33.clone.refs_4_.refs_7_.refs_6_) | copy-start | bytes 1572868
  20.5 7.9 %copy-start.2 = (f32[512,128]{1,0:T(8,128)S(1)}, f32[512,128]{1,0:T(8,128)}, u32[]{:S(2)}) copy-start(f32[512,128]{1,0:T(8,128)} %constant.29.clone.refs_8_.refs_10_) | copy-start | bytes 786436
  20.5 8.0 %copy-start.6 = (bf16[256,256]{1,0:T(8,128)(2,1)S(1)}, bf16[256,256]{1,0:T(8,128)(2,1)}, u32[]{:S(2)}) copy-start(bf16[256,256]{1,0:T(8,128)(2,1)} %constant.36.clone.refs_7_.refs_9_) | copy-start | bytes 393220
  20.5 8.0 %copy-start.7 = (bf16[256,256]{1,0:T(8,128)(2,1)S(1)}, bf16[256,256]{1,0:T(8,128)(2,1)}, u32[]{:S(2)}) copy-start(bf16[256,256]{1,0:T(8,128)(2,1)} %constant.35.clone.refs_6_.refs_8_) | copy-start | bytes 393220
  20.5 5.7 %collective-permute-start.9 = (f32[6,8,1024]{2,1,0:T(8,128)S(1)}, f32[6,8,1024]{2,1,0:T(8,128)S(1)}, u32[]{:S(2)}, u32[]{:S(2)}) collective-permute-start(f32[6,8,1024]{2,1,0:T(8,128)S(1)} %pass_1.1.rest_0_), channel_id=1, source_target_pairs={{0,16},{1,17},{2,18},{3,19},{4,12},{5,13},{6,14},{7,15},{8,24},{9,... | collective-permute-start | bytes 589832 | tf_op jit(solution)/shard_map/ppermute | solution.py:430
  26.3 2.1 %collective-permute-start.12 = (f32[6,8,1024]{2,1,0:T(8,128)S(1)}, f32[6,8,1024]{2,1,0:T(8,128)S(1)}, u32[]{:S(2)}, u32[]{:S(2)}) collective-permute-start(f32[6,8,1024]{2,1,0:T(8,128)S(1)} %finish_1.1.refs_1_), channel_id=1, source_target_pairs={{0,4},{1,5},{2,6},{3,7},{4,0},{5,1},{6,2},{7,3},{8,12},{9,13},{10,... | collective-permute-start | bytes 589832 | tf_op jit(solution)/shard_map/ppermute | solution.py:430
  26.4 2.0 %collective-permute-start.11 = (f32[6,8,1024]{2,1,0:T(8,128)S(1)}, f32[6,8,1024]{2,1,0:T(8,128)S(1)}, u32[]{:S(2)}, u32[]{:S(2)}) collective-permute-start(f32[6,8,1024]{2,1,0:T(8,128)S(1)} %finish_0.1.rest_0_.refs_0_), channel_id=1, source_target_pairs={{0,4},{1,5},{2,6},{3,7},{4,0},{5,1},{6,2},{7,3},{8,12},{9,13},{10,... | collective-permute-start | bytes 589832 | tf_op jit(solution)/shard_map/ppermute | solution.py:430
  26.9 5.0 %collective-permute-start.21 = (f32[2,8,2048]{2,1,0:T(8,128)S(1)}, f32[2,8,2048]{2,1,0:T(8,128)S(1)}, u32[]{:S(2)}, u32[]{:S(2)}) collective-permute-start(f32[2,8,2048]{2,1,0:T(8,128)S(1)} %pass_2.1.rest_0_), channel_id=1, source_target_pairs={{0,16},{1,17},{2,18},{3,19},{4,12},{5,13},{6,14},{7,15},{8,24},{9,... | collective-permute-start | bytes 393224 | tf_op jit(solution)/shard_map/ppermute | solution.py:430
  31.8 13.7 %copy-start.3 = (f32[512,128]{1,0:T(8,128)S(1)}, f32[512,128]{1,0:T(8,128)}, u32[]{:S(2)}) copy-start(f32[512,128]{1,0:T(8,128)} %constant.30.clone.refs_11_) | copy-start | bytes 786436
  31.8 13.7 %copy-start.4 = (bf16[256,256]{1,0:T(8,128)(2,1)S(1)}, bf16[256,256]{1,0:T(8,128)(2,1)}, u32[]{:S(2)}) copy-start(bf16[256,256]{1,0:T(8,128)(2,1)} %constant.38.clone.refs_10_) | copy-start | bytes 393220
  31.8 13.7 %copy-start.5 = (bf16[256,256]{1,0:T(8,128)(2,1)S(1)}, bf16[256,256]{1,0:T(8,128)(2,1)}, u32[]{:S(2)}) copy-start(bf16[256,256]{1,0:T(8,128)(2,1)} %constant.37.clone.refs_9_) | copy-start | bytes 393220
  31.8 13.7 %copy-start.8 = (f32[3,64,128]{2,1,0:T(8,128)S(1)}, f32[3,64,128]{2,1,0:T(8,128)}, u32[]{:S(2)}) copy-start(f32[3,64,128]{2,1,0:T(8,128)} %constant.32.clone.refs_14_) | copy-start | bytes 294916
  31.9 13.7 %copy-start.11 = (f32[2,8,128]{2,1,0:T(8,128)S(1)}, f32[2,8,128]{2,1,0:T(8,128)}, u32[]{:S(2)}) copy-start(f32[2,8,128]{2,1,0:T(8,128)} %constant.31.clone.refs_12_) | copy-start | bytes 24580
  31.9 3.6 %collective-permute-start.22 = (f32[2,8,2048]{2,1,0:T(8,128)S(1)}, f32[2,8,2048]{2,1,0:T(8,128)S(1)}, u32[]{:S(2)}, u32[]{:S(2)}) collective-permute-start(f32[2,8,2048]{2,1,0:T(8,128)S(1)} %finish_2.1.refs_4_), channel_id=1, source_target_pairs={{0,4},{1,5},{2,6},{3,7},{4,0},{5,1},{6,2},{7,3},{8,12},{9,13},{10,... | collective-permute-start | bytes 393224 | tf_op jit(solution)/shard_map/ppermute | solution.py:430
  32.0 7.3 %collective-permute-start.13 = (f32[64,256]{1,0:T(8,128)S(1)}, f32[64,256]{1,0:T(8,128)S(1)}, u32[]{:S(2)}, u32[]{:S(2)}) collective-permute-start(f32[64,256]{1,0:T(8,128)S(1)} %get-tuple-element.128), channel_id=1, source_target_pairs={{0,1},{1,0},{2,3},{3,2},{4,5},{5,4},{6,7},{7,6},{8,9},{9,8},{10,11... | collective-permute-start | bytes 196616 | tf_op jit(solution)/shard_map/ppermute | solution.py:434
  33.6 7.2 %collective-permute-start.14 = (f32[64,256]{1,0:T(8,128)S(1)}, f32[64,256]{1,0:T(8,128)S(1)}, u32[]{:S(2)}, u32[]{:S(2)}) collective-permute-start(f32[64,256]{1,0:T(8,128)S(1)} %get-tuple-element.129), channel_id=1, source_target_pairs={{0,2},{1,3},{2,0},{3,1},{4,6},{5,7},{6,4},{7,5},{8,10},{9,11},{10,... | collective-permute-start | bytes 196616 | tf_op jit(solution)/shard_map/ppermute | solution.py:434
  34.0 11.5 %collective-permute-start.15 = (f32[64,256]{1,0:T(8,128)S(1)}, f32[64,256]{1,0:T(8,128)S(1)}, u32[]{:S(2)}, u32[]{:S(2)}) collective-permute-start(f32[64,256]{1,0:T(8,128)S(1)} %get-tuple-element.130), channel_id=1, source_target_pairs={{0,3},{1,2},{2,1},{3,0},{4,7},{5,6},{6,5},{7,4},{8,11},{9,10},{10,... | collective-permute-start | bytes 196616 | tf_op jit(solution)/shard_map/ppermute | solution.py:434
  36.7 12.8 %collective-permute-start.23 = (f32[64,256]{1,0:T(8,128)S(1)}, f32[64,256]{1,0:T(8,128)S(1)}, u32[]{:S(2)}, u32[]{:S(2)}) collective-permute-start(f32[64,256]{1,0:T(8,128)S(1)} %get-tuple-element.134), channel_id=1, source_target_pairs={{0,1},{1,0},{2,3},{3,2},{4,5},{5,4},{6,7},{7,6},{8,9},{9,8},{10,11... | collective-permute-start | bytes 196616 | tf_op jit(solution)/shard_map/ppermute | solution.py:434
  39.2 11.7 %collective-permute-start.24 = (f32[64,256]{1,0:T(8,128)S(1)}, f32[64,256]{1,0:T(8,128)S(1)}, u32[]{:S(2)}, u32[]{:S(2)}) collective-permute-start(f32[64,256]{1,0:T(8,128)S(1)} %get-tuple-element.135), channel_id=1, source_target_pairs={{0,2},{1,3},{2,0},{3,1},{4,6},{5,7},{6,4},{7,5},{8,10},{9,11},{10,... | collective-permute-start | bytes 196616 | tf_op jit(solution)/shard_map/ppermute | solution.py:434
  39.3 11.7 %collective-permute-start.25 = (f32[64,256]{1,0:T(8,128)S(1)}, f32[64,256]{1,0:T(8,128)S(1)}, u32[]{:S(2)}, u32[]{:S(2)}) collective-permute-start(f32[64,256]{1,0:T(8,128)S(1)} %get-tuple-element.136), channel_id=1, source_target_pairs={{0,3},{1,2},{2,1},{3,0},{4,7},{5,6},{6,5},{7,4},{8,11},{9,10},{10,... | collective-permute-start | bytes 196616 | tf_op jit(solution)/shard_map/ppermute | solution.py:434
  47.8 6.5 %collective-permute-start.18 = (f32[8,4096]{1,0:T(8,128)S(1)}, f32[8,4096]{1,0:T(8,128)S(1)}, u32[]{:S(2)}, u32[]{:S(2)}) collective-permute-start(f32[8,4096]{1,0:T(8,128)S(1)} %backward_0.1.refs_18_), channel_id=1, source_target_pairs={{0,4},{1,5},{2,6},{3,7},{4,0},{5,1},{6,2},{7,3},{8,12},{9,13},{10,... | collective-permute-start | bytes 393224 | tf_op jit(solution)/shard_map/ppermute | solution.py:430
  47.9 6.5 %collective-permute-start.17 = (f32[8,4096]{1,0:T(8,128)S(1)}, f32[8,4096]{1,0:T(8,128)S(1)}, u32[]{:S(2)}, u32[]{:S(2)}) collective-permute-start(f32[8,4096]{1,0:T(8,128)S(1)} %backward_0.1.refs_18_), channel_id=1, source_target_pairs={{0,16},{1,17},{2,18},{3,19},{4,12},{5,13},{6,14},{7,15},{8,24},{9,... | collective-permute-start | bytes 393224 | tf_op jit(solution)/shard_map/ppermute | solution.py:430
  49.5 5.4 %collective-permute-start.16 = (f32[8,4096]{1,0:T(8,128)S(1)}, f32[8,4096]{1,0:T(8,128)S(1)}, u32[]{:S(2)}, u32[]{:S(2)}) collective-permute-start(f32[8,4096]{1,0:T(8,128)S(1)} %backward_0.1.refs_18_), channel_id=1, source_target_pairs={{0,8},{1,9},{2,10},{3,11},{4,20},{5,21},{6,22},{7,23},{8,0},{9,1},... | collective-permute-start | bytes 393224 | tf_op jit(solution)/shard_map/ppermute | solution.py:430
  53.2 5.6 %collective-permute-start.27 = (f32[8,4096]{1,0:T(8,128)S(1)}, f32[8,4096]{1,0:T(8,128)S(1)}, u32[]{:S(2)}, u32[]{:S(2)}) collective-permute-start(f32[8,4096]{1,0:T(8,128)S(1)} %backward_1.1), channel_id=1, source_target_pairs={{0,16},{1,17},{2,18},{3,19},{4,12},{5,13},{6,14},{7,15},{8,24},{9,... | collective-permute-start | bytes 393224 | tf_op jit(solution)/shard_map/ppermute | solution.py:430
  53.8 5.0 %collective-permute-start.26 = (f32[8,4096]{1,0:T(8,128)S(1)}, f32[8,4096]{1,0:T(8,128)S(1)}, u32[]{:S(2)}, u32[]{:S(2)}) collective-permute-start(f32[8,4096]{1,0:T(8,128)S(1)} %backward_1.1), channel_id=1, source_target_pairs={{0,8},{1,9},{2,10},{3,11},{4,20},{5,21},{6,22},{7,23},{8,0},{9,1},... | collective-permute-start | bytes 393224 | tf_op jit(solution)/shard_map/ppermute | solution.py:430
  54.3 5.7 %collective-permute-start.28 = (f32[8,4096]{1,0:T(8,128)S(1)}, f32[8,4096]{1,0:T(8,128)S(1)}, u32[]{:S(2)}, u32[]{:S(2)}) collective-permute-start(f32[8,4096]{1,0:T(8,128)S(1)} %backward_1.1), channel_id=1, source_target_pairs={{0,4},{1,5},{2,6},{3,7},{4,0},{5,1},{6,2},{7,3},{8,12},{9,13},{10,... | collective-permute-start | bytes 393224 | tf_op jit(solution)/shard_map/ppermute | solution.py:430
  54.4 5.7 %collective-permute-start.20 = (f32[8,4096]{1,0:T(8,128)S(1)}, f32[8,4096]{1,0:T(8,128)S(1)}, u32[]{:S(2)}, u32[]{:S(2)}) collective-permute-start(f32[8,4096]{1,0:T(8,128)S(1)} %collective-permute-done.17), channel_id=1, source_target_pairs={{0,4},{1,5},{2,6},{3,7},{4,0},{5,1},{6,2},{7,3},{8,12},{9,13},{10,... | collective-permute-start | bytes 393224 | tf_op jit(solution)/shard_map/ppermute | solution.py:430
  54.9 5.2 %collective-permute-start.19 = (f32[8,4096]{1,0:T(8,128)S(1)}, f32[8,4096]{1,0:T(8,128)S(1)}, u32[]{:S(2)}, u32[]{:S(2)}) collective-permute-start(f32[8,4096]{1,0:T(8,128)S(1)} %collective-permute-done.16), channel_id=1, source_target_pairs={{0,4},{1,5},{2,6},{3,7},{4,0},{5,1},{6,2},{7,3},{8,12},{9,13},{10,... | collective-permute-start | bytes 393224 | tf_op jit(solution)/shard_map/ppermute | solution.py:430
  58.8 1.3 %collective-permute-start.30 = (f32[8,4096]{1,0:T(8,128)S(1)}, f32[8,4096]{1,0:T(8,128)S(1)}, u32[]{:S(2)}, u32[]{:S(2)}) collective-permute-start(f32[8,4096]{1,0:T(8,128)S(1)} %collective-permute-done.27), channel_id=1, source_target_pairs={{0,4},{1,5},{2,6},{3,7},{4,0},{5,1},{6,2},{7,3},{8,12},{9,13},{10,... | collective-permute-start | bytes 393224 | tf_op jit(solution)/shard_map/ppermute | solution.py:430
  58.8 1.5 %collective-permute-start.29 = (f32[8,4096]{1,0:T(8,128)S(1)}, f32[8,4096]{1,0:T(8,128)S(1)}, u32[]{:S(2)}, u32[]{:S(2)}) collective-permute-start(f32[8,4096]{1,0:T(8,128)S(1)} %collective-permute-done.26), channel_id=1, source_target_pairs={{0,4},{1,5},{2,6},{3,7},{4,0},{5,1},{6,2},{7,3},{8,12},{9,13},{10,... | collective-permute-start | bytes 393224 | tf_op jit(solution)/shard_map/ppermute | solution.py:430

commit v2 on v1

--- a/solution.py
+++ b/solution.py
@@ -8,6 +8,7 @@
 from jax.experimental import pallas as pl
 from jax.experimental.pallas import tpu as pltpu
 from jax.sharding import PartitionSpec as P
+
 
 BLK = 4
 NY = 64
@@ -110,47 +111,60 @@
     return o, lax.rem(o, 2), lax.div(o, 2)
 
 
-def take_kernel(flip, start, source, *rest):
+def fetch(source, out, sem, side, start, number):
+    at = pl.multiple_of(side * (source.shape[2] // 2) + start, LANES)
+    step = out.shape[0] // number
+    return [
+        pltpu.make_async_copy(
+            source.at[pl.ds(n * step, step), :, pl.ds(at, out.shape[2])], out.at[pl.ds(n * step, step)], sem.at[n]
+        )
+        for n in range(number)
+    ]
+
+
+def take_kernel(start, source, *rest):
     out, sem = rest[-2:]
+    copies = fetch(source, out, sem, 1 - my_core(), start, sem.shape[0])
+    for copy in copies:
+        copy.start()
+    for copy in copies:
+        copy.wait()
+
+
+class Place:
+    def __init__(self, per_device, tiles, host):
+        self.o, self.core, self.chip = my_place()
+        self.tiles, self.host = tiles, host
+        self.chips = tiles.shape[0]
+        owners = [lax.div(tiles[t, 0] * BLK, 2 * per_device) for t in range(self.chips)]
+        key, same = 0, True
+        for t in range(self.chips):
+            key = key + owners[t] * self.chips**t
+            same = same & (owners[t] == owners[0])
+        self.key, self.same = key, same
+        self.bit_1 = jnp.where(self.core == 0, 1, 2)
+        self.bit_2 = 3 - self.bit_1
+
+    def tile(self, chip):
+        return self.host[self.key * self.chips + chip]
+
+    def heads(self, chip):
+        tile = self.tile(chip)
+        return BLK * self.tiles[tile, 0], BLK * self.tiles[tile, 1]
+
+
+def setup_kernel(per_device, tiles, host, rotation, source, after, *rest):
+    count = len(rest) - 3
+    mine, (high, low, sem) = rest[:count], rest[count:]
     core = my_core()
-    side = 1 - core if flip else core
-    at = pl.multiple_of(side * (source.shape[2] // 2) + start, LANES)
-    copy = pltpu.make_async_copy(source.at[:, :, pl.ds(at, out.shape[2])], out, sem)
-    copy.start()
-    copy.wait()
-
-
-def setup_kernel(per_device, n_grid, tiles, host, rotation, mask, log_r, high, low, powers, flags, match, alone):
-    o, core, chip = my_place()
-    at, size_x = SUB * lax.axis_index("grid"), SUB * n_grid
-    exponents = (
-        2 * at + SUB + 1,
-        2 * size_x + 1 - SUB - 2 * at,
-        2 * size_x + 2 - 2 * at,
-        2 * at,
-        2 * at + 2 * SUB + 2,
-        2 * size_x - 2 * SUB - 2 * at,
-    )
-    for n, exponent in enumerate(exponents):
-        power = jnp.exp(exponent.astype(f32) * log_r[...])
-        powers[n] = power if n < 2 else 1.0 - power
-    chips = tiles.shape[0]
-    owners = [lax.div(tiles[t, 0] * BLK, 2 * per_device) for t in range(chips)]
-    key = 0
-    for t in range(chips):
-        key = key + owners[t] * chips**t
-    same = owners[0] == owners[1]
-    for t in range(2, chips):
-        same = same & (owners[t] == owners[0])
-    alone[0] = same.astype(jnp.int32)
-    bit_1 = jnp.where(core == 0, 1, 2)
-    bit_2 = 3 - bit_1
+    copies = []
+    for n, out in enumerate(mine):
+        copies += fetch(source, out, sem.at[n], core, n * out.shape[2], sem.shape[1])
+    for copy in copies:
+        copy.start()
+    at = Place(per_device, tiles, host)
     pair = BLK // 2
-    order = [chip ^ 3, chip ^ bit_1, chip ^ bit_2, chip]
-    heads = []
-    for where in order:
-        tile = host[key * chips + where]
-        heads.append((BLK * tiles[tile, 0], BLK * tiles[tile, 1]))
+    heads = [at.heads(chip) for chip in (at.chip ^ 3, at.chip ^ at.bit_1, at.chip ^ at.bit_2, at.chip)]
     wanted = []
     for a, b in heads:
         wanted += [a + (1 - core) * pair] + [b + w for w in range(BLK)] + [a + core * pair]
@@ -159,35 +173,72 @@
             wanted += [a + (1 - core) * pair + u, a + core * pair + u]
     lane = lax.broadcasted_iota(jnp.int32, (SUB, LANES), 1)
     chosen = jnp.concatenate([jnp.where(lane == n, 1.0, 0.0) for n in wanted]).astype(bf16)
-    count = chosen.shape[0]
+    rows = chosen.shape[0]
     row = lax.broadcasted_iota(jnp.int32, (LANES, LANES), 0)
     column = lax.broadcasted_iota(jnp.int32, (LANES, LANES), 1)
     columns = [
-        jnp.where(row - (o ^ e) * per_device == jnp.right_shift(column, 3), 1.0, 0.0).astype(bf16)
+        jnp.where(row - (at.o ^ e) * per_device == jnp.right_shift(column, 3), 1.0, 0.0).astype(bf16)
         for e in range(2)
     ]
-    keep = (lax.broadcasted_iota(jnp.int32, (count, LANES), 0) & (SUB - 1)) == (
-        lax.broadcasted_iota(jnp.int32, (count, LANES), 1) & (SUB - 1)
+    keep = (lax.broadcasted_iota(jnp.int32, (rows, LANES), 0) & (SUB - 1)) == (
+        lax.broadcasted_iota(jnp.int32, (rows, LANES), 1) & (SUB - 1)
     )
     for out, values in zip((high, low), split(rotation[...])):
         picked = lax.dot_general(chosen, values, (((1,), (1,)), ((), ())), preferred_element_type=f32).astype(bf16)
         for e in range(2):
             out[:, e * LANES:(e + 1) * LANES] = jnp.where(keep, dot(picked, columns[e]), 0.0).astype(bf16)
-    a, b = heads[-1]
+    for copy in copies:
+        copy.wait()
+
+
+def ready_kernel(per_device, n_grid, tiles, host, mask, log_r, *rest):
+    out, powers, flags, match, alone, zeros, sem = rest[-7:]
+    zeros[...] = jnp.zeros(zeros.shape, f32)
+    step = zeros.shape[0]
+    copies = [
+        pltpu.make_async_copy(zeros, out.at[pl.ds(n * step, step)], sem.at[n]) for n in range(out.shape[0] // step)
+    ]
+    for copy in copies:
+        copy.start()
+    begin, size_x = SUB * lax.axis_index("grid"), SUB * n_grid
+    exponents = (
+        2 * begin + SUB + 1,
+        2 * size_x + 1 - SUB - 2 * begin,
+        2 * size_x + 2 - 2 * begin,
+        2 * begin,
+        2 * begin + 2 * SUB + 2,
+        2 * size_x - 2 * SUB - 2 * begin,
+    )
+    for n, exponent in enumerate(exponents):
+        power = jnp.exp(exponent.astype(f32) * log_r[...])
+        powers[n] = power if n < 2 else 1.0 - power
+    at = Place(per_device, tiles, host)
+    alone[0] = at.same.astype(jnp.int32)
+    a, b = at.heads(at.chip)
+    pair = BLK // 2
     live = mask[...].astype(f32)
+    row = lax.broadcasted_iota(jnp.int32, live.shape, 0)
+    column = lax.broadcasted_iota(jnp.int32, (1, live.shape[1]), 1)
     for u in range(pair):
-        line = jnp.sum(jnp.where(row == a + core * pair + u, live, 0.0), axis=0, keepdims=True)
+        line = jnp.sum(jnp.where(row == a + at.core * pair + u, live, 0.0), axis=0, keepdims=True)
         for w in range(BLK):
-            flags[u * BLK + w] = jnp.sum(jnp.where(column[:1] == b + w, line, 0.0))
+            flags[u * BLK + w] = jnp.sum(jnp.where(column == b + w, line, 0.0))
     blocks = per_device // BLK
-    parts = [chip, chip ^ bit_1, chip ^ bit_2, chip ^ 3, chip, chip ^ bit_2, chip ^ bit_1, chip ^ 3]
-    for n, where in enumerate(parts):
-        home = tiles[host[key * chips + where], 0]
+    parts = [0, at.bit_1, at.bit_2, 3, 0, at.bit_2, at.bit_1, 3]
+    for n, flip in enumerate(parts):
+        home = tiles[at.tile(at.chip ^ flip), 0]
         for block in range(blocks):
-            hit = home == o * blocks + block
+            hit = home == at.o * blocks + block
             if n % 4 == 3:
-                hit = hit & same
+                hit = hit & at.same
             match[block * len(parts) + n] = hit.astype(jnp.int32)
+    for copy in copies:
+        copy.wait()
+
+
+def join_kernel(x, y, out):
+    out[0] = x[...]
+    out[1] = y[...]
 
 
 def rotate_kernel(first, high, low, *rest):
@@ -221,19 +272,6 @@
     out = rest[-1]
     count = out.shape[0]
     out[...] = keep[count:] + got[count:] + passed[...]
-
-
-def clear_kernel(*refs):
-    out, zeros, sem = refs[-3:]
-    zeros[...] = jnp.zeros(zeros.shape, f32)
-    step = zeros.shape[0]
-    copies = [
-        pltpu.make_async_copy(zeros, out.at[pl.ds(n * step, step)], sem.at[n]) for n in range(out.shape[0] // step)
-    ]
-    for copy in copies:
-        copy.start()
-    for copy in copies:
-        copy.wait()
 
 
 def sub_sums(values):
@@ -375,8 +413,12 @@
 def place_kernel(stride, match, *refs):
     parts, (out, rows, sem) = refs[:-4], refs[-3:]
     pair = BLK // 2
-    blocks, count = out.shape[0] // BLK, len(parts) // pair
+    blocks = out.shape[0] // BLK
     core = my_core()
+    values = []
+    for part in parts:
+        values += [part] if len(part.shape) == 2 else [part.at[n] for n in range(part.shape[0])]
+    parts, count = values, len(values) // pair
 
     def hits(b, side):
         return [(match[b * stride + side * stride // 2 + n], side * count // 2 + n) for n in range(count // 2)]
@@ -419,8 +461,6 @@
     half = width // 2
     chips = n_orb // 2
     axes = ("orb", "grid")
-    o, g = lax.axis_index("orb"), lax.axis_index("grid")
-    core, chip = o % 2, o // 2
 
     def swap(x, even, odd):
         moves = []
@@ -436,21 +476,16 @@
     chunk = half // CHUNKS
     orbitals = pltpu.with_memory_space_constraint(orbitals, pltpu.HBM)
 
-    def take(flip, start, lanes, *after):
-        return pl.pallas_call(
-            functools.partial(take_kernel, flip, start),
-            out_shape=jax.ShapeDtypeStruct((per_device, planes, lanes), f32),
-            in_specs=[HBM] + [ANY] * len(after), out_specs=VM, scratch_shapes=[DMA], name=f"take_{int(flip)}_{start}",
-            compiler_params=grant(4),
-        )(orbitals, *after)
-
-    theirs, mine, last = [], [], ()
+    part = jax.ShapeDtypeStruct((per_device, planes, chunk), f32)
+    copies = per_device // 2
+    theirs, last = [], ()
     for n in range(CHUNKS):
-        taken = take(True, n * chunk, chunk, *last)
+        taken = pl.pallas_call(
+            functools.partial(take_kernel, n * chunk), out_shape=part, in_specs=[HBM] + [ANY] * len(last), out_specs=VM,
+            scratch_shapes=[DMA((copies,))], compiler_params=grant(4),
+        )(orbitals, *last)
         theirs.append(swap(taken, 1, 1))
         last = (taken,)
-    for n in range(CHUNKS):
-        mine.append(take(False, n * chunk, chunk, *last))
 
     pair = BLK // 2
     firsts = (BLK + 2) * chips
@@ -458,41 +493,47 @@
     wide_table = jax.ShapeDtypeStruct((rows, 2 * LANES), bf16)
     blocks = per_device // BLK
     c, r = line_np()
-    high, low, powers, flags, match, alone = pl.pallas_call(
-        functools.partial(setup_kernel, per_device, n_grid),
-        out_shape=(wide_table, wide_table, jax.ShapeDtypeStruct((6, NY, LANES), f32), jax.ShapeDtypeStruct((pair * BLK,), f32),
-                   jax.ShapeDtypeStruct((blocks * 8,), jnp.int32), jax.ShapeDtypeStruct((1,), jnp.int32)),
-        in_specs=[SM, SM, VM, VM, VM], out_specs=(VM, VM, VM, SM, SM, SM), name="setup", compiler_params=grant(4),
-    )(tile_list, jnp.asarray(host_np(chips).reshape(-1)), rotation, pair_mask, jnp.asarray(np.log(r), f32))
-
-    def rotate(first, count, fields, name, *after):
+    c, r = line_np()
+    host = jnp.asarray(host_np(chips).reshape(-1))
+    *mine, high, low = pl.pallas_call(
+        functools.partial(setup_kernel, per_device),
+        out_shape=[part] * CHUNKS + [wide_table] * 2,
+        in_specs=[SM, SM, VM, HBM, ANY], out_specs=[VM] * (CHUNKS + 2),
+        scratch_shapes=[DMA((CHUNKS, copies))], name="setup", compiler_params=grant(6),
+    )(tile_list, host, rotation, orbitals, *last)
+
+    def rotate(first, count, fields, *after):
         part = jax.ShapeDtypeStruct((count, planes, chunk * (len(fields) // 2)), f32)
         send, keep = pl.pallas_call(
             functools.partial(rotate_kernel, first * SUB), out_shape=(part, part),
             in_specs=[VM] * (2 + len(fields)) + [ANY] * len(after),
-            out_specs=(VM, VM), name=name, compiler_params=grant(8),
+            out_specs=(VM, VM), compiler_params=grant(8),
         )(high, low, *fields, *after)
         return send, keep, swap(send, 2, 4)
 
     sums, last = [], ()
     for n in range(CHUNKS):
-        sums.append(rotate(0, firsts // 2, [mine[n], theirs[n]], f"rotate_{n}", *last))
+        sums.append(rotate(0, firsts // 2, [mine[n], theirs[n]], *last))
         last = (sums[-1][0],)
     both = [x for n in range(CHUNKS) for x in (mine[n], theirs[n])]
-    sums.append(rotate(firsts, (pair - 1) * chips, both, "rotate_rest", *last))
-    empty = pl.pallas_call(
-        clear_kernel, out_shape=pltpu.HBM(shape, f32), in_specs=[ANY], out_specs=HBM,
-        scratch_shapes=[pltpu.VMEM((pair, planes, width), f32), DMA((per_device // pair,))], name="clear",
+    sums.append(rotate(firsts, (pair - 1) * chips, both, *last))
+    empty, powers, flags, match, alone = pl.pallas_call(
+        functools.partial(ready_kernel, per_device, n_grid),
+        out_shape=(pltpu.HBM(shape, f32), jax.ShapeDtypeStruct((6, NY, LANES), f32),
+                   jax.ShapeDtypeStruct((pair * BLK,), f32), jax.ShapeDtypeStruct((blocks * 8,), jnp.int32),
+                   jax.ShapeDtypeStruct((1,), jnp.int32)),
+        in_specs=[SM, SM, VM, VM, ANY], out_specs=(HBM, VM, SM, SM, SM),
+        scratch_shapes=[pltpu.VMEM((pair, planes, width), f32), DMA((per_device // pair,))], name="ready",
         compiler_params=grant(4),
-    )(sums[-1][0])
+    )(tile_list, host, pair_mask, jnp.asarray(np.log(r), f32), sums[-1][0])
     passing, own, other = [], [], []
 
     def pass_on(n, *after, spec=ANY):
-        send, keep, got = sums[n]
+        _, keep, got = sums[n]
         count = keep.shape[0] // 2
         value = pl.pallas_call(
             pass_kernel, out_shape=jax.ShapeDtypeStruct((count,) + keep.shape[1:], f32),
-            in_specs=[VM] * 2 + [spec] * len(after), out_specs=VM, name=f"pass_{n}", compiler_params=grant(4),
+            in_specs=[VM] * 2 + [spec] * len(after), out_specs=VM, compiler_params=grant(4),
         )(keep, got, *after)
         passing.append((keep, got, swap(value, 4, 2)))
         return value
@@ -501,7 +542,7 @@
         keep, got, passed = passing[n]
         own.append(pl.pallas_call(
             finish_kernel, out_shape=jax.ShapeDtypeStruct(passed.shape, f32), in_specs=[VM] * 3 + [ANY] * len(after),
-            out_specs=VM, name=f"finish_{n}", compiler_params=grant(4),
+            out_specs=VM, compiler_params=grant(4),
         )(keep, got, passed, *after))
         other.append(swap(own[-1], 1, 1))
         return own[-1]
@@ -542,7 +583,6 @@
             in_specs=[VM] * len(inputs) + [ANY] * len(last),
             out_specs=[VM] * (n_grid + 2),
             scratch_shapes=[wide],
-            name=f"forward_{u}",
             compiler_params=grant(16),
         )(*inputs, *last)
         last = (spectrum,)
@@ -558,7 +598,6 @@
             in_specs=[SM] + [VM] * len(inputs) + [ANY] * len(last),
             out_specs=VM,
             scratch_shapes=[pltpu.VMEM(cube, f32), wide],
-            name=f"backward_{u}",
             compiler_params=grant(16),
         )(flags, *inputs, *last))
         last = (terms[-1],)
@@ -566,7 +605,13 @@
     near_1 = [swap(term, 2, 4) for term in terms]
     near_2 = [swap(term, 4, 2) for term in terms]
     own_parts = [[term, x, y] for term, x, y in zip(terms, near_1, near_2)]
-    sib_parts = [[swap(v, 1, 1) for v in group] for group in own_parts]
+    sib_parts = []
+    for term, x, y in own_parts:
+        joined = pl.pallas_call(
+            join_kernel, out_shape=jax.ShapeDtypeStruct((2,) + term.shape, f32), in_specs=[VM] * 2, out_specs=VM,
+            compiler_params=grant(4),
+        )(x, y)
+        sib_parts.append([swap(term, 1, 1), swap(joined, 1, 1)])
 
     def place(target, groups):
         parts = [part for group in groups for part in group]
@@ -649,7 +694,7 @@
 
 
 def any_device(orbitals, rotation, tile_list, pair_mask):
-    n_orb, n_grid = lax.axis_size("orb"), lax.axis_size("grid")
+    n_grid = lax.axis_size("grid")
     number_orbitals, size_x = rotation.shape[0], orbitals.shape[1] * n_grid
     rotated = jnp.einsum(
         "ij,ixc->jxc",
@@ -689,8 +734,9 @@
         fits = n_orb == 8 and 2 * tile_list.shape[0] == n_orb and planes == SUB and per_device % BLK == 0
         fits = fits and width == NY * NZ and 2 * NZ == LANES and n_grid in (2, 4, 8)
         fits = fits and per_device * SUB == LANES and rotation.shape == (LANES, LANES)
-        body = tile_device if fits else any_device
-        return body(orbitals, rotation, tile_list, pair_mask)
+        if not fits:
+            return any_device(orbitals, rotation, tile_list, pair_mask)
+        return tile_device(orbitals, rotation, tile_list, pair_mask)
 
     in_specs = (P("orb", "grid", None), P(), P(), P())
     out_specs = P("orb", "grid", None)

time: 62.4 us -> 62.2 us (level)
  the two profiles are of different devices: /device:TPU:16 before, /device:TPU:20 now
where the time goes in v2:
time: 62.2 us; the launch traced here: 61.9 us
  waiting for transfers between devices  24.3 us (39%)
  starting transfers between devices  19.2 us (31%)
  Pallas kernels  17.4 us (28%)
  between operations  0.84 us (1%)
    ppermute x19, waiting for transfers between devices, swap(): return lax.ppermute(x, axes, moves)  19.6 us
    ppermute x19, starting transfers between devices, swap(): return lax.ppermute(x, axes, moves)  11.5 us
    ppermute x6, starting transfers between devices, cross(): return lax.ppermute(x, axes, moves)  7.64 us
    ppermute x6, waiting for transfers between devices, cross(): return lax.ppermute(x, axes, moves)  4.71 us
    pallas_call x2, Pallas kernels, tile_device(): pl.pallas_call(functools.partial(backward_kernel, u, (CHUNKS, CHUNKS, len...  4.55 us
    pallas_call x1, Pallas kernels, tile_device(): pl.pallas_call(functools.partial(ready_kernel, per_device, n_grid), out_s...  2.7 us
    pallas_call x2, Pallas kernels, tile_device(): pl.pallas_call(functools.partial(forward_kernel, u, counts + (n_grid - 1,...  2.33 us
    pallas_call x2, Pallas kernels, tile_device(): pl.pallas_call(functools.partial(take_kernel, n * chunk), out_shape=part,...  2.28 us
  transfers between devices with their start and end apart: 25, of which 13 were waited for; matrix products, arithmetic and copies ran while one was open for 0% of the time, Pallas kernels for 24%

profile of v2, /device:TPU:20, one launch (start us, length us, event | category | flops | bytes accessed | tf_op | source)
XLA Modules:
  0.0 61.9 jit_solution(10282160798142260173)
XLA Ops:
  0.0 1.1 %shard_map.156.rest_0_ = f32[16,8,1024]{2,1,0:T(8,128)S(1)} custom-call(f32[16,8,4096]{2,1,0:T(8,128)} %source.5), custom_call_target="tpu_custom_call" | custom-call | tf_op jit(solution)/shard_map/pallas_call | solution.py:483
  1.2 0.1 collective-permute-start.4
  1.3 1.1 %shard_map.157.after = f32[16,8,1024]{2,1,0:T(8,128)S(1)} custom-call(f32[16,8,4096]{2,1,0:T(8,128)} %source.5, f32[16,8,1024]{2,1,0:T(8,128)S(1)} %shard_map.156.rest_0_), custom_call_target="tpu_custom_call" | custom-call | tf_op jit(solution)/shard_map/pallas_call | solution.py:483
  2.4 0.5 collective-permute-start.5
  3.0 0.1 copy.22.tiles
  3.1 2.1 %setup.1 = (f32[16,8,1024]{2,1,0:T(8,128)S(1)}, f32[16,8,1024]{2,1,0:T(8,128)S(1)}, bf16[256,256]{1,0:T(8,128)(2,1)S(1)}, bf16[256,256]{1,0:T(8,128)(2,1)S(1)}) custom-call(s32[4,2]{1,0:T(4,128)S(1)} %copy.22.tiles, s32[1024]{0:T(1024)S(1)} %copy-done.13, f32[128,128]{1,0:T(8,128)S(1)} %copy-done.9, f32[16,8,4096]{2,1,0:T(8,128)} %source.5, ...), custom_call_target="tpu_custom_call" | custom-call | tf_op jit(solution)/shard_map/setup/pallas_call | solution.py:498
  5.1 0.5 shard_map.158
  5.6 1.6 %collective-permute-start.6 = (f32[12,8,1024]{2,1,0:T(8,128)S(1)}, f32[12,8,1024]{2,1,0:T(8,128)S(1)}, u32[]{:S(2)}, u32[]{:S(2)}) collective-permute-start(f32[12,8,1024]{2,1,0:T(8,128)S(1)} %get-tuple-element.111.rest_2_), channel_id=1, source_target_pairs={{0,8},{1,9},{2,10},{3,11},{4,20},{5,21},{6,22},{7,23},{8,0},{9,1},... | collective-permute-start | bytes 1179656 | tf_op jit(solution)/shard_map/ppermute | solution.py:470
  7.2 0.5 shard_map.159
  7.7 0.6 collective-permute-start.8
  8.3 0.7 %shard_map.160 = (f32[4,8,2048]{2,1,0:T(8,128)S(1)}, f32[4,8,2048]{2,1,0:T(8,128)S(1)}) custom-call(bf16[256,256]{1,0:T(8,128)(2,1)S(1)} %get-tuple-element.107.high, bf16[256,256]{1,0:T(8,128)(2,1)S(1)} %get-tuple-element.108.low, f32[16,8,1024]{2,1,0:T(8,128)S(1)} %get-tuple-element.109.rest_0_, f32[16,8,1024]{2,1,0:T(8,128)S(1)} %collective-permute-done.4.rest_1_, ...), custom_call_target="tpu_custom_call" | custom-call | tf_op jit(solution)/shard_map/pallas_call | solution.py:507
  9.0 1.6 %collective-permute-start.10 = (f32[4,8,2048]{2,1,0:T(8,128)S(1)}, f32[4,8,2048]{2,1,0:T(8,128)S(1)}, u32[]{:S(2)}, u32[]{:S(2)}) collective-permute-start(f32[4,8,2048]{2,1,0:T(8,128)S(1)} %get-tuple-element.113.rest_0_), channel_id=1, source_target_pairs={{0,8},{1,9},{2,10},{3,11},{4,20},{5,21},{6,22},{7,23},{8,0},{9,1},... | collective-permute-start | bytes 786440 | tf_op jit(solution)/shard_map/ppermute | solution.py:470
  10.6 2.7 %ready.1 = (f32[16,8,4096]{2,1,0:T(8,128)}, f32[6,64,128]{2,1,0:T(8,128)S(1)}, f32[8]{0:T(128)S(1)}, s32[32]{0:T(128)S(1)}, s32[1]{0:T(128)}) custom-call(s32[4,2]{1,0:T(4,128)S(1)} %copy.22.tiles, s32[1024]{0:T(1024)S(1)} %copy-done.13, s32[128,128]{1,0:T(8,128)S(1)} %copy-done.10, f32[64,128]{1,0:T(8,128)S(1)} %copy-done.12, ...), custom_call_target="tpu_custom_call" | custom-call | tf_op jit(solution)/shard_map/ready/pallas_call | solution.py:520
  13.3 0.2 collective-permute-done.6.got
  13.5 0.6 collective-permute-start.7
  14.1 5.9 %collective-permute-done.8.got = f32[12,8,1024]{2,1,0:T(8,128)S(1)} collective-permute-done((f32[12,8,1024]{2,1,0:T(8,128)S(1)}, f32[12,8,1024]{2,1,0:T(8,128)S(1)}, u32[]{:S(2)}, u32[]{:S(2)}) %collective-permute-start.8) | collective-permute-done | bytes 393248 | tf_op jit(solution)/shard_map/ppermute | solution.py:470
  20.1 0.6 collective-permute-start.9
  20.6 0.7 %collective-permute-done.7.passed = f32[6,8,1024]{2,1,0:T(8,128)S(1)} collective-permute-done((f32[6,8,1024]{2,1,0:T(8,128)S(1)}, f32[6,8,1024]{2,1,0:T(8,128)S(1)}, u32[]{:S(2)}, u32[]{:S(2)}) %collective-permute-start.7) | collective-permute-done | bytes 196640 | tf_op jit(solution)/shard_map/ppermute | solution.py:470
  21.4 3.3 %collective-permute-done.10.got = f32[4,8,2048]{2,1,0:T(8,128)S(1)} collective-permute-done((f32[4,8,2048]{2,1,0:T(8,128)S(1)}, f32[4,8,2048]{2,1,0:T(8,128)S(1)}, u32[]{:S(2)}, u32[]{:S(2)}) %collective-permute-start.10) | collective-permute-done | bytes 262176 | tf_op jit(solution)/shard_map/ppermute | solution.py:470
  24.7 1.1 %collective-permute-done.9.passed = f32[6,8,1024]{2,1,0:T(8,128)S(1)} collective-permute-done((f32[6,8,1024]{2,1,0:T(8,128)S(1)}, f32[6,8,1024]{2,1,0:T(8,128)S(1)}, u32[]{:S(2)}, u32[]{:S(2)}) %collective-permute-start.9) | collective-permute-done | bytes 196640 | tf_op jit(solution)/shard_map/ppermute | solution.py:470
  25.8 0.1 collective-permute-start.12
  25.9 0.5 collective-permute-start.11
  26.4 0.5 collective-permute-start.20
  26.9 0.4 collective-permute-done.12.refs_3_
  27.3 0.3 collective-permute-done.11.refs_2_
  27.7 1.2 %shard_map.166 = (f32[64,256]{1,0:T(8,128)S(1)}, f32[64,256]{1,0:T(8,128)S(1)}, f32[64,256]{1,0:T(8,128)S(1)}, f32[512,256]{1,0:T(8,128)S(1)}, f32[64,256]{1,0:T(8,128)S(1)}, /*index=5*/f32[64,256]{1,0:T(8,128)S(1)}) custom-call(f32[6,8,1024]{2,1,0:T(8,128)S(1)} %shard_map.163.rest_0_.refs_0_, f32[6,8,1024]{2,1,0:T(8,128)S(1)} %shard_map.165.refs_1_, ...), custom_call_target="tpu_custom_call" | custom-call | tf_op jit(solution)/shard_map/pallas_call | solution.py:580
  28.8 2.6 %collective-permute-done.20.passed = f32[2,8,2048]{2,1,0:T(8,128)S(1)} collective-permute-done((f32[2,8,2048]{2,1,0:T(8,128)S(1)}, f32[2,8,2048]{2,1,0:T(8,128)S(1)}, u32[]{:S(2)}, u32[]{:S(2)}) %collective-permute-start.20) | collective-permute-done | bytes 131104 | tf_op jit(solution)/shard_map/ppermute | solution.py:470
  31.5 1.6 %collective-permute-start.13 = (f32[64,256]{1,0:T(8,128)S(1)}, f32[64,256]{1,0:T(8,128)S(1)}, u32[]{:S(2)}, u32[]{:S(2)}) collective-permute-start(f32[64,256]{1,0:T(8,128)S(1)} %get-tuple-element.122), channel_id=1, source_target_pairs={{0,1},{1,0},{2,3},{3,2},{4,5},{5,4},{6,7},{7,6},{8,9},{9,8},{10,11... | collective-permute-start | bytes 196616 | tf_op jit(solution)/shard_map/ppermute | solution.py:474
  33.2 0.3 collective-permute-start.14
  33.5 1.6 %collective-permute-start.15 = (f32[64,256]{1,0:T(8,128)S(1)}, f32[64,256]{1,0:T(8,128)S(1)}, u32[]{:S(2)}, u32[]{:S(2)}) collective-permute-start(f32[64,256]{1,0:T(8,128)S(1)} %get-tuple-element.124), channel_id=1, source_target_pairs={{0,3},{1,2},{2,1},{3,0},{4,7},{5,6},{6,5},{7,4},{8,11},{9,10},{10,... | collective-permute-start | bytes 196616 | tf_op jit(solution)/shard_map/ppermute | solution.py:474
  35.1 1.2 %shard_map.170 = (f32[64,256]{1,0:T(8,128)S(1)}, f32[64,256]{1,0:T(8,128)S(1)}, f32[64,256]{1,0:T(8,128)S(1)}, f32[512,256]{1,0:T(8,128)S(1)}, f32[64,256]{1,0:T(8,128)S(1)}, /*index=5*/f32[64,256]{1,0:T(8,128)S(1)}) custom-call(f32[6,8,1024]{2,1,0:T(8,128)S(1)} %shard_map.163.rest_0_.refs_0_, f32[6,8,1024]{2,1,0:T(8,128)S(1)} %shard_map.165.refs_1_, ...), custom_call_target="tpu_custom_call" | custom-call | tf_op jit(solution)/shard_map/pallas_call | solution.py:580
  36.2 2.5 %collective-permute-start.22 = (f32[64,256]{1,0:T(8,128)S(1)}, f32[64,256]{1,0:T(8,128)S(1)}, u32[]{:S(2)}, u32[]{:S(2)}) collective-permute-start(f32[64,256]{1,0:T(8,128)S(1)} %get-tuple-element.128), channel_id=1, source_target_pairs={{0,1},{1,0},{2,3},{3,2},{4,5},{5,4},{6,7},{7,6},{8,9},{9,8},{10,11... | collective-permute-start | bytes 196616 | tf_op jit(solution)/shard_map/ppermute | solution.py:474
  38.8 1.5 %collective-permute-start.24 = (f32[64,256]{1,0:T(8,128)S(1)}, f32[64,256]{1,0:T(8,128)S(1)}, u32[]{:S(2)}, u32[]{:S(2)}) collective-permute-start(f32[64,256]{1,0:T(8,128)S(1)} %get-tuple-element.130), channel_id=1, source_target_pairs={{0,3},{1,2},{2,1},{3,0},{4,7},{5,6},{6,5},{7,4},{8,11},{9,10},{10,... | collective-permute-start | bytes 196616 | tf_op jit(solution)/shard_map/ppermute | solution.py:474
  40.3 4.7 %collective-permute-done.15.refs_6_ = f32[64,256]{1,0:T(8,128)S(1)} collective-permute-done((f32[64,256]{1,0:T(8,128)S(1)}, f32[64,256]{1,0:T(8,128)S(1)}, u32[]{:S(2)}, u32[]{:S(2)}) %collective-permute-start.15) | collective-permute-done | bytes 65568 | tf_op jit(solution)/shard_map/ppermute | solution.py:474
  45.1 2.3 %shard_map.167.refs_18_ = f32[8,4096]{1,0:T(8,128)S(1)} custom-call(f32[8]{0:T(128)S(1)} %get-tuple-element.116.flags, f32[6,8,1024]{2,1,0:T(8,128)S(1)} %shard_map.163.rest_0_.refs_0_, f32[6,8,1024]{2,1,0:T(8,128)S(1)} %shard_map.165.refs_1_, f32[6,8,1024]{2,1,0:T(8,128)S(1)} %collective-permute-done.11.refs_2_, ...), custom_call_target="tpu_custom_call" | custom-call | tf_op jit(solution)/shard_map/pallas_call | solution.py:595
  47.3 0.6 collective-permute-start.17
  47.9 1.5 %collective-permute-start.16 = (f32[8,4096]{1,0:T(8,128)S(1)}, f32[8,4096]{1,0:T(8,128)S(1)}, u32[]{:S(2)}, u32[]{:S(2)}) collective-permute-start(f32[8,4096]{1,0:T(8,128)S(1)} %shard_map.167.refs_18_), channel_id=1, source_target_pairs={{0,8},{1,9},{2,10},{3,11},{4,20},{5,21},{6,22},{7,23},{8,0},{9,1},... | collective-permute-start | bytes 393224 | tf_op jit(solution)/shard_map/ppermute | solution.py:470
  49.4 2.3 %shard_map.171 = f32[8,4096]{1,0:T(8,128)S(1)} custom-call(f32[8]{0:T(128)S(1)} %get-tuple-element.116.flags, f32[6,8,1024]{2,1,0:T(8,128)S(1)} %shard_map.163.rest_0_.refs_0_, f32[6,8,1024]{2,1,0:T(8,128)S(1)} %shard_map.165.refs_1_, f32[6,8,1024]{2,1,0:T(8,128)S(1)} %collective-permute-done.11.refs_2_, f32[6,8,1024]{2,1,0:T(8,128)S(1)} %collective-permute-done.12.refs_3_, ...), custom_call_target="tpu_custom_call" | custom-call | tf_op jit(solution)/shard_map/pallas_call | solution.py:595
  51.7 1.6 %collective-permute-start.26 = (f32[8,4096]{1,0:T(8,128)S(1)}, f32[8,4096]{1,0:T(8,128)S(1)}, u32[]{:S(2)}, u32[]{:S(2)}) collective-permute-start(f32[8,4096]{1,0:T(8,128)S(1)} %shard_map.171), channel_id=1, source_target_pairs={{0,16},{1,17},{2,18},{3,19},{4,12},{5,13},{6,14},{7,15},{8,24},{9,... | collective-permute-start | bytes 393224 | tf_op jit(solution)/shard_map/ppermute | solution.py:470
  53.3 0.5 collective-permute-start.25
  53.9 2.8 %collective-permute-done.26.y = f32[8,4096]{1,0:T(8,128)S(1)} collective-permute-done((f32[8,4096]{1,0:T(8,128)S(1)}, f32[8,4096]{1,0:T(8,128)S(1)}, u32[]{:S(2)}, u32[]{:S(2)}) %collective-permute-start.26) | collective-permute-done | bytes 131104 | tf_op jit(solution)/shard_map/ppermute | solution.py:470
  56.7 1.5 %collective-permute-done.25.x = f32[8,4096]{1,0:T(8,128)S(1)} collective-permute-done((f32[8,4096]{1,0:T(8,128)S(1)}, f32[8,4096]{1,0:T(8,128)S(1)}, u32[]{:S(2)}, u32[]{:S(2)}) %collective-permute-start.25) | collective-permute-done | bytes 131104 | tf_op jit(solution)/shard_map/ppermute | solution.py:470
  58.3 0.5 collective-permute-start.18
  58.8 0.1 collective-permute-start.27
  59.5 0.6 collective-permute-done.18
  60.1 0.2 collective-permute-done.27
  60.3 1.6 %conditional.1 = (f32[16,8,4096]{2,1,0:T(8,128)}) conditional(s32[]{:T(128)} %bitcast, (s32[32]{0:T(128)S(1)}, f32[8,4096]{1,0:T(8,128)S(1)}, f32[8,4096]{1,0:T(8,128)S(1)}, f32[8,4096]{1,0:T(8,128)S(1)}, f32[8,4096]{1,0:T(8,128)S(1)}, /*index=5*/f32[2,8,4096]{2,1,0:T(8,128)S(1)}, f32[8,4096]{1,0:T(8,128)S(1)}, f32[8,4096]{1,0:T(8,128)S(1)}, ...), branch_computations={%region_0.0_spmd, %region_1.0_spmd} | conditional | bytes 2097320 | solution.py:636
  60.3 1.6 %place.2 = f32[16,8,4096]{2,1,0:T(8,128)} custom-call(s32[32]{0:T(128)S(1)} %get-tuple-element.56.match, f32[8,4096]{1,0:T(8,128)S(1)} %get-tuple-element.57.refs_0_, f32[8,4096]{1,0:T(8,128)S(1)} %get-tuple-element.58.refs_1_, f32[8,4096]{1,0:T(8,128)S(1)} %get-tuple-element.59.refs_2_, ...), custom_call_target="tpu_custom_call", output_to_operand_aliasing={{}: (11, {})} | custom-call | tf_op jit(solution)/shard_map/cond/branch_0_fun/place/pallas_call | solution.py:618
  (54 shorter events, 0.5 us)
Async XLA Ops:
  1.1 1.8 %copy-start.14 = (s32[4,2]{0,1:T(2,128)S(1)}, s32[4,2]{0,1:T(2,128)}, u32[]{:S(2)}) copy-start(s32[4,2]{0,1:T(2,128)} %param.20) | copy-start | bytes 100
  1.2 1.9 %copy-start.9 = (f32[128,128]{1,0:T(8,128)S(1)}, f32[128,128]{1,0:T(8,128)}, u32[]{:S(2)}) copy-start(f32[128,128]{1,0:T(8,128)} %rotation.1) | copy-start | bytes 196612
  1.2 1.9 %copy-start.13 = (s32[1024]{0:T(1024)S(1)}, s32[1024]{0:T(1024)}, u32[]{:S(2)}) copy-start(s32[1024]{0:T(1024)} %constant.27.clone.host) | copy-start | bytes 12292
  1.2 3.9 %collective-permute-start.4 = (f32[16,8,1024]{2,1,0:T(8,128)S(1)}, f32[16,8,1024]{2,1,0:T(8,128)S(1)}, u32[]{:S(2)}, u32[]{:S(2)}) collective-permute-start(f32[16,8,1024]{2,1,0:T(8,128)S(1)} %shard_map.156.rest_0_), channel_id=1, source_target_pairs={{0,4},{1,5},{2,6},{3,7},{4,0},{5,1},{6,2},{7,3},{8,12},{9,13},{10,... | collective-permute-start | bytes 1572872 | tf_op jit(solution)/shard_map/ppermute | solution.py:470
  2.4 4.8 %collective-permute-start.5 = (f32[16,8,1024]{2,1,0:T(8,128)S(1)}, f32[16,8,1024]{2,1,0:T(8,128)S(1)}, u32[]{:S(2)}, u32[]{:S(2)}) collective-permute-start(f32[16,8,1024]{2,1,0:T(8,128)S(1)} %shard_map.157.after), channel_id=1, source_target_pairs={{0,4},{1,5},{2,6},{3,7},{4,0},{5,1},{6,2},{7,3},{8,12},{9,13},{10,... | collective-permute-start | bytes 1572872 | tf_op jit(solution)/shard_map/ppermute | solution.py:470
  5.6 7.8 %collective-permute-start.6 = (f32[12,8,1024]{2,1,0:T(8,128)S(1)}, f32[12,8,1024]{2,1,0:T(8,128)S(1)}, u32[]{:S(2)}, u32[]{:S(2)}) collective-permute-start(f32[12,8,1024]{2,1,0:T(8,128)S(1)} %get-tuple-element.111.rest_2_), channel_id=1, source_target_pairs={{0,8},{1,9},{2,10},{3,11},{4,20},{5,21},{6,22},{7,23},{8,0},{9,1},... | collective-permute-start | bytes 1179656 | tf_op jit(solution)/shard_map/ppermute | solution.py:470
  7.2 3.4 %copy-start.10 = (s32[128,128]{1,0:T(8,128)S(1)}, s32[128,128]{1,0:T(8,128)}, u32[]{:S(2)}) copy-start(s32[128,128]{1,0:T(8,128)} %mask.1) | copy-start | bytes 196612
  7.2 3.4 %copy-start.12 = (f32[64,128]{1,0:T(8,128)S(1)}, f32[64,128]{1,0:T(8,128)}, u32[]{:S(2)}) copy-start(f32[64,128]{1,0:T(8,128)} %constant.28.clone.log_r) | copy-start | bytes 98308
  7.7 12.3 %collective-permute-start.8 = (f32[12,8,1024]{2,1,0:T(8,128)S(1)}, f32[12,8,1024]{2,1,0:T(8,128)S(1)}, u32[]{:S(2)}, u32[]{:S(2)}) collective-permute-start(f32[12,8,1024]{2,1,0:T(8,128)S(1)} %get-tuple-element.112.rest_4_), channel_id=1, source_target_pairs={{0,8},{1,9},{2,10},{3,11},{4,20},{5,21},{6,22},{7,23},{8,0},{9,1},... | collective-permute-start | bytes 1179656 | tf_op jit(solution)/shard_map/ppermute | solution.py:470
  9.0 15.7 %collective-permute-start.10 = (f32[4,8,2048]{2,1,0:T(8,128)S(1)}, f32[4,8,2048]{2,1,0:T(8,128)S(1)}, u32[]{:S(2)}, u32[]{:S(2)}) collective-permute-start(f32[4,8,2048]{2,1,0:T(8,128)S(1)} %get-tuple-element.113.rest_0_), channel_id=1, source_target_pairs={{0,8},{1,9},{2,10},{3,11},{4,20},{5,21},{6,22},{7,23},{8,0},{9,1},... | collective-permute-start | bytes 786440 | tf_op jit(solution)/shard_map/ppermute | solution.py:470
  13.5 7.8 %collective-permute-start.7 = (f32[6,8,1024]{2,1,0:T(8,128)S(1)}, f32[6,8,1024]{2,1,0:T(8,128)S(1)}, u32[]{:S(2)}, u32[]{:S(2)}) collective-permute-start(f32[6,8,1024]{2,1,0:T(8,128)S(1)} %shard_map.161.rest_0_), channel_id=1, source_target_pairs={{0,16},{1,17},{2,18},{3,19},{4,12},{5,13},{6,14},{7,15},{8,24},{9,... | collective-permute-start | bytes 589832 | tf_op jit(solution)/shard_map/ppermute | solution.py:470
  20.0 7.6 %copy-start = (bf16[512,512]{1,0:T(8,128)(2,1)S(1)}, bf16[512,512]{1,0:T(8,128)(2,1)}, u32[]{:S(2)}) copy-start(bf16[512,512]{1,0:T(8,128)(2,1)} %constant.34.clone.refs_5_.refs_8_.refs_7_) | copy-start | bytes 1572868
  20.0 7.6 %copy-start.1 = (bf16[512,512]{1,0:T(8,128)(2,1)S(1)}, bf16[512,512]{1,0:T(8,128)(2,1)}, u32[]{:S(2)}) copy-start(bf16[512,512]{1,0:T(8,128)(2,1)} %constant.33.clone.refs_4_.refs_7_.refs_6_) | copy-start | bytes 1572868
  20.0 7.6 %copy-start.2 = (f32[512,128]{1,0:T(8,128)S(1)}, f32[512,128]{1,0:T(8,128)}, u32[]{:S(2)}) copy-start(f32[512,128]{1,0:T(8,128)} %constant.29.clone.refs_8_.refs_10_) | copy-start | bytes 786436
  20.0 7.6 %copy-start.6 = (bf16[256,256]{1,0:T(8,128)(2,1)S(1)}, bf16[256,256]{1,0:T(8,128)(2,1)}, u32[]{:S(2)}) copy-start(bf16[256,256]{1,0:T(8,128)(2,1)} %constant.36.clone.refs_7_.refs_9_) | copy-start | bytes 393220
  20.0 7.6 %copy-start.7 = (bf16[256,256]{1,0:T(8,128)(2,1)S(1)}, bf16[256,256]{1,0:T(8,128)(2,1)}, u32[]{:S(2)}) copy-start(bf16[256,256]{1,0:T(8,128)(2,1)} %constant.35.clone.refs_6_.refs_8_) | copy-start | bytes 393220
  20.1 5.7 %collective-permute-start.9 = (f32[6,8,1024]{2,1,0:T(8,128)S(1)}, f32[6,8,1024]{2,1,0:T(8,128)S(1)}, u32[]{:S(2)}, u32[]{:S(2)}) collective-permute-start(f32[6,8,1024]{2,1,0:T(8,128)S(1)} %shard_map.162.rest_0_), channel_id=1, source_target_pairs={{0,16},{1,17},{2,18},{3,19},{4,12},{5,13},{6,14},{7,15},{8,24},{9,... | collective-permute-start | bytes 589832 | tf_op jit(solution)/shard_map/ppermute | solution.py:470
  25.8 1.5 %collective-permute-start.12 = (f32[6,8,1024]{2,1,0:T(8,128)S(1)}, f32[6,8,1024]{2,1,0:T(8,128)S(1)}, u32[]{:S(2)}, u32[]{:S(2)}) collective-permute-start(f32[6,8,1024]{2,1,0:T(8,128)S(1)} %shard_map.165.refs_1_), channel_id=1, source_target_pairs={{0,4},{1,5},{2,6},{3,7},{4,0},{5,1},{6,2},{7,3},{8,12},{9,13},{10,... | collective-permute-start | bytes 589832 | tf_op jit(solution)/shard_map/ppermute | solution.py:470
  25.9 1.7 %collective-permute-start.11 = (f32[6,8,1024]{2,1,0:T(8,128)S(1)}, f32[6,8,1024]{2,1,0:T(8,128)S(1)}, u32[]{:S(2)}, u32[]{:S(2)}) collective-permute-start(f32[6,8,1024]{2,1,0:T(8,128)S(1)} %shard_map.163.rest_0_.refs_0_), channel_id=1, source_target_pairs={{0,4},{1,5},{2,6},{3,7},{4,0},{5,1},{6,2},{7,3},{8,12},{9,13},{10,... | collective-permute-start | bytes 589832 | tf_op jit(solution)/shard_map/ppermute | solution.py:470
  26.4 5.0 %collective-permute-start.20 = (f32[2,8,2048]{2,1,0:T(8,128)S(1)}, f32[2,8,2048]{2,1,0:T(8,128)S(1)}, u32[]{:S(2)}, u32[]{:S(2)}) collective-permute-start(f32[2,8,2048]{2,1,0:T(8,128)S(1)} %shard_map.164.rest_0_), channel_id=1, source_target_pairs={{0,16},{1,17},{2,18},{3,19},{4,12},{5,13},{6,14},{7,15},{8,24},{9,... | collective-permute-start | bytes 393224 | tf_op jit(solution)/shard_map/ppermute | solution.py:470
  31.4 13.7 %copy-start.3 = (f32[512,128]{1,0:T(8,128)S(1)}, f32[512,128]{1,0:T(8,128)}, u32[]{:S(2)}) copy-start(f32[512,128]{1,0:T(8,128)} %constant.30.clone.refs_11_) | copy-start | bytes 786436
  31.4 13.7 %copy-start.4 = (bf16[256,256]{1,0:T(8,128)(2,1)S(1)}, bf16[256,256]{1,0:T(8,128)(2,1)}, u32[]{:S(2)}) copy-start(bf16[256,256]{1,0:T(8,128)(2,1)} %constant.38.clone.refs_10_) | copy-start | bytes 393220
  31.4 13.7 %copy-start.5 = (bf16[256,256]{1,0:T(8,128)(2,1)S(1)}, bf16[256,256]{1,0:T(8,128)(2,1)}, u32[]{:S(2)}) copy-start(bf16[256,256]{1,0:T(8,128)(2,1)} %constant.37.clone.refs_9_) | copy-start | bytes 393220
  31.4 13.7 %copy-start.8 = (f32[3,64,128]{2,1,0:T(8,128)S(1)}, f32[3,64,128]{2,1,0:T(8,128)}, u32[]{:S(2)}) copy-start(f32[3,64,128]{2,1,0:T(8,128)} %constant.32.clone.refs_14_) | copy-start | bytes 294916
  31.4 13.7 %copy-start.11 = (f32[2,8,128]{2,1,0:T(8,128)S(1)}, f32[2,8,128]{2,1,0:T(8,128)}, u32[]{:S(2)}) copy-start(f32[2,8,128]{2,1,0:T(8,128)} %constant.31.clone.refs_12_) | copy-start | bytes 24580
  31.4 3.6 %collective-permute-start.21 = (f32[2,8,2048]{2,1,0:T(8,128)S(1)}, f32[2,8,2048]{2,1,0:T(8,128)S(1)}, u32[]{:S(2)}, u32[]{:S(2)}) collective-permute-start(f32[2,8,2048]{2,1,0:T(8,128)S(1)} %shard_map.169.refs_4_), channel_id=1, source_target_pairs={{0,4},{1,5},{2,6},{3,7},{4,0},{5,1},{6,2},{7,3},{8,12},{9,13},{10,... | collective-permute-start | bytes 393224 | tf_op jit(solution)/shard_map/ppermute | solution.py:470
  31.5 7.3 %collective-permute-start.13 = (f32[64,256]{1,0:T(8,128)S(1)}, f32[64,256]{1,0:T(8,128)S(1)}, u32[]{:S(2)}, u32[]{:S(2)}) collective-permute-start(f32[64,256]{1,0:T(8,128)S(1)} %get-tuple-element.122), channel_id=1, source_target_pairs={{0,1},{1,0},{2,3},{3,2},{4,5},{5,4},{6,7},{7,6},{8,9},{9,8},{10,11... | collective-permute-start | bytes 196616 | tf_op jit(solution)/shard_map/ppermute | solution.py:474
  33.2 7.2 %collective-permute-start.14 = (f32[64,256]{1,0:T(8,128)S(1)}, f32[64,256]{1,0:T(8,128)S(1)}, u32[]{:S(2)}, u32[]{:S(2)}) collective-permute-start(f32[64,256]{1,0:T(8,128)S(1)} %get-tuple-element.123), channel_id=1, source_target_pairs={{0,2},{1,3},{2,0},{3,1},{4,6},{5,7},{6,4},{7,5},{8,10},{9,11},{10,... | collective-permute-start | bytes 196616 | tf_op jit(solution)/shard_map/ppermute | solution.py:474
  33.5 11.5 %collective-permute-start.15 = (f32[64,256]{1,0:T(8,128)S(1)}, f32[64,256]{1,0:T(8,128)S(1)}, u32[]{:S(2)}, u32[]{:S(2)}) collective-permute-start(f32[64,256]{1,0:T(8,128)S(1)} %get-tuple-element.124), channel_id=1, source_target_pairs={{0,3},{1,2},{2,1},{3,0},{4,7},{5,6},{6,5},{7,4},{8,11},{9,10},{10,... | collective-permute-start | bytes 196616 | tf_op jit(solution)/shard_map/ppermute | solution.py:474
  36.2 13.2 %collective-permute-start.22 = (f32[64,256]{1,0:T(8,128)S(1)}, f32[64,256]{1,0:T(8,128)S(1)}, u32[]{:S(2)}, u32[]{:S(2)}) collective-permute-start(f32[64,256]{1,0:T(8,128)S(1)} %get-tuple-element.128), channel_id=1, source_target_pairs={{0,1},{1,0},{2,3},{3,2},{4,5},{5,4},{6,7},{7,6},{8,9},{9,8},{10,11... | collective-permute-start | bytes 196616 | tf_op jit(solution)/shard_map/ppermute | solution.py:474
  38.8 10.6 %collective-permute-start.23 = (f32[64,256]{1,0:T(8,128)S(1)}, f32[64,256]{1,0:T(8,128)S(1)}, u32[]{:S(2)}, u32[]{:S(2)}) collective-permute-start(f32[64,256]{1,0:T(8,128)S(1)} %get-tuple-element.129), channel_id=1, source_target_pairs={{0,2},{1,3},{2,0},{3,1},{4,6},{5,7},{6,4},{7,5},{8,10},{9,11},{10,... | collective-permute-start | bytes 196616 | tf_op jit(solution)/shard_map/ppermute | solution.py:474
  38.8 10.6 %collective-permute-start.24 = (f32[64,256]{1,0:T(8,128)S(1)}, f32[64,256]{1,0:T(8,128)S(1)}, u32[]{:S(2)}, u32[]{:S(2)}) collective-permute-start(f32[64,256]{1,0:T(8,128)S(1)} %get-tuple-element.130), channel_id=1, source_target_pairs={{0,3},{1,2},{2,1},{3,0},{4,7},{5,6},{6,5},{7,4},{8,11},{9,10},{10,... | collective-permute-start | bytes 196616 | tf_op jit(solution)/shard_map/ppermute | solution.py:474
  47.3 6.5 %collective-permute-start.17 = (f32[8,4096]{1,0:T(8,128)S(1)}, f32[8,4096]{1,0:T(8,128)S(1)}, u32[]{:S(2)}, u32[]{:S(2)}) collective-permute-start(f32[8,4096]{1,0:T(8,128)S(1)} %shard_map.167.refs_18_), channel_id=1, source_target_pairs={{0,16},{1,17},{2,18},{3,19},{4,12},{5,13},{6,14},{7,15},{8,24},{9,... | collective-permute-start | bytes 393224 | tf_op jit(solution)/shard_map/ppermute | solution.py:470
  47.9 5.9 %collective-permute-start.16 = (f32[8,4096]{1,0:T(8,128)S(1)}, f32[8,4096]{1,0:T(8,128)S(1)}, u32[]{:S(2)}, u32[]{:S(2)}) collective-permute-start(f32[8,4096]{1,0:T(8,128)S(1)} %shard_map.167.refs_18_), channel_id=1, source_target_pairs={{0,8},{1,9},{2,10},{3,11},{4,20},{5,21},{6,22},{7,23},{8,0},{9,1},... | collective-permute-start | bytes 393224 | tf_op jit(solution)/shard_map/ppermute | solution.py:470
  51.7 5.0 %collective-permute-start.26 = (f32[8,4096]{1,0:T(8,128)S(1)}, f32[8,4096]{1,0:T(8,128)S(1)}, u32[]{:S(2)}, u32[]{:S(2)}) collective-permute-start(f32[8,4096]{1,0:T(8,128)S(1)} %shard_map.171), channel_id=1, source_target_pairs={{0,16},{1,17},{2,18},{3,19},{4,12},{5,13},{6,14},{7,15},{8,24},{9,... | collective-permute-start | bytes 393224 | tf_op jit(solution)/shard_map/ppermute | solution.py:470
  53.3 5.0 %collective-permute-start.25 = (f32[8,4096]{1,0:T(8,128)S(1)}, f32[8,4096]{1,0:T(8,128)S(1)}, u32[]{:S(2)}, u32[]{:S(2)}) collective-permute-start(f32[8,4096]{1,0:T(8,128)S(1)} %shard_map.171), channel_id=1, source_target_pairs={{0,8},{1,9},{2,10},{3,11},{4,20},{5,21},{6,22},{7,23},{8,0},{9,1},... | collective-permute-start | bytes 393224 | tf_op jit(solution)/shard_map/ppermute | solution.py:470
  53.8 6.4 %collective-permute-start.19 = (f32[2,8,4096]{2,1,0:T(8,128)S(1)}, f32[2,8,4096]{2,1,0:T(8,128)S(1)}, u32[]{:S(2)}, u32[]{:S(2)}) collective-permute-start(f32[2,8,4096]{2,1,0:T(8,128)S(1)} %shard_map.168), channel_id=1, source_target_pairs={{0,4},{1,5},{2,6},{3,7},{4,0},{5,1},{6,2},{7,3},{8,12},{9,13},{10,... | collective-permute-start | bytes 786440 | tf_op jit(solution)/shard_map/ppermute | solution.py:470
  58.3 2.0 %collective-permute-start.28 = (f32[2,8,4096]{2,1,0:T(8,128)S(1)}, f32[2,8,4096]{2,1,0:T(8,128)S(1)}, u32[]{:S(2)}, u32[]{:S(2)}) collective-permute-start(f32[2,8,4096]{2,1,0:T(8,128)S(1)} %shard_map.172), channel_id=1, source_target_pairs={{0,4},{1,5},{2,6},{3,7},{4,0},{5,1},{6,2},{7,3},{8,12},{9,13},{10,... | collective-permute-start | bytes 786440 | tf_op jit(solution)/shard_map/ppermute | solution.py:470
  58.3 1.7 %collective-permute-start.18 = (f32[8,4096]{1,0:T(8,128)S(1)}, f32[8,4096]{1,0:T(8,128)S(1)}, u32[]{:S(2)}, u32[]{:S(2)}) collective-permute-start(f32[8,4096]{1,0:T(8,128)S(1)} %shard_map.167.refs_18_), channel_id=1, source_target_pairs={{0,4},{1,5},{2,6},{3,7},{4,0},{5,1},{6,2},{7,3},{8,12},{9,13},{10,... | collective-permute-start | bytes 393224 | tf_op jit(solution)/shard_map/ppermute | solution.py:470
  58.8 1.4 %collective-permute-start.27 = (f32[8,4096]{1,0:T(8,128)S(1)}, f32[8,4096]{1,0:T(8,128)S(1)}, u32[]{:S(2)}, u32[]{:S(2)}) collective-permute-start(f32[8,4096]{1,0:T(8,128)S(1)} %shard_map.171), channel_id=1, source_target_pairs={{0,4},{1,5},{2,6},{3,7},{4,0},{5,1},{6,2},{7,3},{8,12},{9,13},{10,... | collective-permute-start | bytes 393224 | tf_op jit(solution)/shard_map/ppermute | solution.py:470

commit v3 on v2

--- a/solution.py
+++ b/solution.py
@@ -154,12 +154,12 @@
 
 
 def setup_kernel(per_device, tiles, host, rotation, source, after, *rest):
-    count = len(rest) - 3
-    mine, (high, low, sem) = rest[:count], rest[count:]
+    fetched, (high, low, sem) = rest[:-3], rest[-3:]
     core = my_core()
     copies = []
-    for n, out in enumerate(mine):
-        copies += fetch(source, out, sem.at[n], core, n * out.shape[2], sem.shape[1])
+    for n, out in enumerate(fetched):
+        side, chunk = (1 - core, n + 1) if n < CHUNKS - 1 else (core, n - CHUNKS + 1)
+        copies += fetch(source, out, sem.at[n], side, chunk * out.shape[2], sem.shape[1])
     for copy in copies:
         copy.start()
     at = Place(per_device, tiles, host)
@@ -301,12 +301,12 @@
 
 def forward_kernel(u, counts, *refs):
     groups = []
-    for count in counts[:-1]:
+    for count in counts:
         groups.append(refs[:count])
         refs = refs[count:]
     first_own, first_other, own, other = groups[:4]
     y_hi, y_lo, z_hi, z_lo, ends, powers = refs[:6]
-    messages, (spectrum, a_out, b_out, dens) = refs[-4 - counts[-1]:-4], refs[-4:]
+    message, spectrum, a_out, b_out, dens = refs[-5:]
     if u == 0:
         own, other = first_own, first_other
     core, g = my_core(), lax.axis_index("grid")
@@ -341,8 +341,7 @@
             leftward = (even - odd) - far * (even + odd)
             a_out[lines, lanes] = rightward
             b_out[lines, lanes] = leftward
-            for k, out in enumerate(messages, 1):
-                out[lines, lanes] = jnp.where((g ^ k) > g, rightward, leftward)
+            message[lines, lanes] = jnp.where((g & 1) == 0, rightward, leftward)
         return carry
 
     lax.fori_loop(0, NY // SUB, reduce, 0)
@@ -359,25 +358,17 @@
     core, g = my_core(), lax.axis_index("grid")
     tiles = own[0].shape[2] // LANES
     first, last = basis[0], basis[1]
+    odd, inner = (g & 1) == 1, (g == 1) | (g == 2)
 
     def ends(group, carry):
         lines = pl.ds(pl.multiple_of(group * SUB, SUB), SUB)
         scale, r, slab = steady[0, lines, :], steady[1, lines, :], steady[2, lines, :]
-        decays = [None, jnp.ones((SUB, LANES), f32), slab]
-        while len(decays) <= len(received):
-            decays.append(decays[-1] * slab)
         for q in range(BLK // 2):
             lanes = slice(q * LANES, (q + 1) * LANES)
-            from_left = from_right = jnp.zeros((SUB, LANES), f32)
-            for n, ref in enumerate(received, 1):
-                distance = jnp.abs((g ^ n) - g)
-                factor = decays[n]
-                for d in range(1, n):
-                    factor = jnp.where(distance == d, decays[d], factor)
-                value = factor * ref[lines, lanes]
-                is_left = (g ^ n) < g
-                from_left = from_left + jnp.where(is_left, value, 0.0)
-                from_right = from_right + jnp.where(is_left, 0.0, value)
+            same = received[0][lines, lanes] + jnp.where(inner, 0.0, slab * received[2][lines, lanes])
+            across = jnp.where(inner, received[1][lines, lanes], 0.0)
+            from_left = jnp.where(odd, same, across)
+            from_right = jnp.where(odd, across, same)
             before = scale * (powers[2, lines, :] * from_left
                               + r * powers[3, lines, :] * (b_in[lines, lanes] + slab * from_right))
             after = scale * (powers[4, lines, :] * from_right
@@ -410,6 +401,13 @@
                 out[:, pl.ds(pl.multiple_of(at * LANES, LANES), LANES)] = -total
 
 
+def relay_kernel(got, a, b, steady, out):
+    g = lax.axis_index("grid")
+    for q in range(BLK // 2):
+        lanes = slice(q * LANES, (q + 1) * LANES)
+        out[:, lanes] = jnp.where((g & 1) == 1, a[:, lanes], b[:, lanes]) + steady[2] * got[:, lanes]
+
+
 def place_kernel(stride, match, *refs):
     parts, (out, rows, sem) = refs[:-4], refs[-3:]
     pair = BLK // 2
@@ -469,23 +467,19 @@
             moves += [(a * n_grid + b, (a ^ flip) * n_grid + b) for b in range(n_grid)]
         return lax.ppermute(x, axes, moves)
 
-    def cross(x, k):
-        moves = [(a * n_grid + b, a * n_grid + (b ^ k)) for a in range(n_orb) for b in range(n_grid)]
-        return lax.ppermute(x, axes, moves)
+    def along(x, target):
+        return lax.ppermute(x, axes, [(a * n_grid + b, a * n_grid + t) for a in range(n_orb) for b, t in enumerate(target)])
 
     chunk = half // CHUNKS
     orbitals = pltpu.with_memory_space_constraint(orbitals, pltpu.HBM)
 
     part = jax.ShapeDtypeStruct((per_device, planes, chunk), f32)
     copies = per_device // 2
-    theirs, last = [], ()
-    for n in range(CHUNKS):
-        taken = pl.pallas_call(
-            functools.partial(take_kernel, n * chunk), out_shape=part, in_specs=[HBM] + [ANY] * len(last), out_specs=VM,
-            scratch_shapes=[DMA((copies,))], compiler_params=grant(4),
-        )(orbitals, *last)
-        theirs.append(swap(taken, 1, 1))
-        last = (taken,)
+    taken = pl.pallas_call(
+        functools.partial(take_kernel, 0), out_shape=part, in_specs=[HBM], out_specs=VM,
+        scratch_shapes=[DMA((copies,))], name="take", compiler_params=grant(4),
+    )(orbitals)
+    theirs = [swap(taken, 1, 1)]
 
     pair = BLK // 2
     firsts = (BLK + 2) * chips
@@ -495,12 +489,15 @@
     c, r = line_np()
     c, r = line_np()
     host = jnp.asarray(host_np(chips).reshape(-1))
-    *mine, high, low = pl.pallas_call(
+    *fetched, high, low = pl.pallas_call(
         functools.partial(setup_kernel, per_device),
-        out_shape=[part] * CHUNKS + [wide_table] * 2,
-        in_specs=[SM, SM, VM, HBM, ANY], out_specs=[VM] * (CHUNKS + 2),
-        scratch_shapes=[DMA((CHUNKS, copies))], name="setup", compiler_params=grant(6),
-    )(tile_list, host, rotation, orbitals, *last)
+        out_shape=[part] * (2 * CHUNKS - 1) + [wide_table] * 2,
+        in_specs=[SM, SM, VM, HBM, ANY], out_specs=[VM] * (2 * CHUNKS + 1),
+        scratch_shapes=[DMA((2 * CHUNKS - 1, copies))], name="setup", compiler_params=grant(8),
+    )(tile_list, host, rotation, orbitals, taken)
+    mine = fetched[CHUNKS - 1:]
+    for n, taken in enumerate(fetched[:CHUNKS - 1], 1):
+        theirs.append(swap(taken, 1, 1))
 
     def rotate(first, count, fields, *after):
         part = jax.ShapeDtypeStruct((count, planes, chunk * (len(fields) // 2)), f32)
@@ -516,7 +513,6 @@
         sums.append(rotate(0, firsts // 2, [mine[n], theirs[n]], *last))
         last = (sums[-1][0],)
     both = [x for n in range(CHUNKS) for x in (mine[n], theirs[n])]
-    sums.append(rotate(firsts, (pair - 1) * chips, both, *last))
     empty, powers, flags, match, alone = pl.pallas_call(
         functools.partial(ready_kernel, per_device, n_grid),
         out_shape=(pltpu.HBM(shape, f32), jax.ShapeDtypeStruct((6, NY, LANES), f32),
@@ -550,10 +546,11 @@
     step = pass_on(0, empty, spec=HBM)
     for n in range(1, CHUNKS):
         step = pass_on(n, step)
-    step = finish(0, step)
-    step = pass_on(CHUNKS, step)
-    for n in range(1, CHUNKS):
+    sums.append(rotate(firsts, (pair - 1) * chips, both, step))
+    step = sums[-1][0]
+    for n in range(CHUNKS):
         step = finish(n, step)
+    last = (pass_on(CHUNKS, step),)
 
     sine_x, eigen_x = sine_np(planes), eigen_np(planes)
     ends = jnp.asarray(np.einsum("jp,pkl->kjl", sine_x, r[None] ** np.arange(planes - 1, -1, -1)[:, None, None])
@@ -570,23 +567,28 @@
     cube = (NY * SUB, 2 * LANES)
     wide = pltpu.VMEM((width // LANES * SUB, BLK * LANES), f32)
     base_own, base_other = own[:CHUNKS], other[:CHUNKS]
-    last = ()
     for u in range(pair):
         if u:
             finish(CHUNKS, *last)
         more_own, more_other = own[CHUNKS:][:u], other[CHUNKS:][:u]
         counts = (CHUNKS, CHUNKS, len(more_own), len(more_other))
         inputs = [*base_own, *base_other, *more_own, *more_other, y_hi, y_lo, z_hi, z_lo, ends, powers]
-        *messages, spectrum, a, b = pl.pallas_call(
-            functools.partial(forward_kernel, u, counts + (n_grid - 1,)),
-            out_shape=[lines] * (n_grid - 1) + [jax.ShapeDtypeStruct(cube, f32), lines, lines],
+        message, spectrum, a, b = pl.pallas_call(
+            functools.partial(forward_kernel, u, counts),
+            out_shape=[lines, jax.ShapeDtypeStruct(cube, f32), lines, lines],
             in_specs=[VM] * len(inputs) + [ANY] * len(last),
-            out_specs=[VM] * (n_grid + 2),
+            out_specs=[VM] * 4,
             scratch_shapes=[wide],
             compiler_params=grant(16),
         )(*inputs, *last)
+        near = along(message, (1, 0, 3, 2))
+        relayed = pl.pallas_call(
+            relay_kernel, out_shape=lines, in_specs=[VM] * 4, out_specs=VM, compiler_params=grant(4),
+        )(near, a, b, steady)
+        far_pair = along(relayed, (0, 2, 1, 3))
+        handed = along(far_pair, (1, 0, 3, 2))
         last = (spectrum,)
-        solved.append((spectrum, a, b, [cross(m, k) for k, m in enumerate(messages, 1)]))
+        solved.append((spectrum, a, b, [near, far_pair, handed]))
 
     terms, last = [], ()
     for u, (spectrum, a, b, received) in enumerate(solved):
@@ -732,7 +734,7 @@
     def on_device(orbitals, rotation, tile_list, pair_mask):
         per_device, planes, width = orbitals.shape
         fits = n_orb == 8 and 2 * tile_list.shape[0] == n_orb and planes == SUB and per_device % BLK == 0
-        fits = fits and width == NY * NZ and 2 * NZ == LANES and n_grid in (2, 4, 8)
+        fits = fits and width == NY * NZ and 2 * NZ == LANES and n_grid == 4
         fits = fits and per_device * SUB == LANES and rotation.shape == (LANES, LANES)
         if not fits:
             return any_device(orbitals, rotation, tile_list, pair_mask)

time: 62.2 us -> 66.5 us (1.069)
  the two profiles are of different devices: /device:TPU:20 before, /device:TPU:0 now
where the time goes in v3:
time: 66.5 us; the launch traced here: 66.3 us
  starting transfers between devices  28.7 us (43%)
  waiting for transfers between devices  21 us (32%)
  Pallas kernels  15.5 us (23%)
  between operations  0.91 us (1%)
    ppermute x19, waiting for transfers between devices, swap(): return lax.ppermute(x, axes, moves)  18.7 us
    ppermute x19, starting transfers between devices, swap(): return lax.ppermute(x, axes, moves)  16.4 us
    ppermute x6, starting transfers between devices, along(): lax.ppermute(x, axes, [(a * n_grid + b, a * n_grid + t) for a in range(n_...  12.3 us
    pallas_call x2, Pallas kernels, tile_device(): pl.pallas_call(functools.partial(backward_kernel, u, (CHUNKS, CHUNKS, len...  4.42 us
    pallas_call x1, Pallas kernels, tile_device(): pl.pallas_call(functools.partial(ready_kernel, per_device, n_grid), out_s...  2.7 us
    ppermute x6, waiting for transfers between devices, along(): lax.ppermute(x, axes, [(a * n_grid + b, a * n_grid + t) for a in range(n_...  2.31 us
    pallas_call x1, Pallas kernels, tile_device(): pl.pallas_call(functools.partial(setup_kernel, per_device), out_shape=[pa...  2.29 us
    pallas_call x2, Pallas kernels, tile_device(): pl.pallas_call(functools.partial(forward_kernel, u, counts), out_shape=[l...  2.28 us
  transfers between devices with their start and end apart: 25, of which 12 were waited for; matrix products, arithmetic and copies ran while one was open for 0% of the time, Pallas kernels for 20%

profile of v3, /device:TPU:0, one launch (start us, length us, event | category | flops | bytes accessed | tf_op | source)
XLA Modules:
  0.0 66.3 jit_solution(11833812547864347186)
XLA Ops:
  0.0 1.2 %take.1.after = f32[16,8,1024]{2,1,0:T(8,128)S(1)} custom-call(f32[16,8,4096]{2,1,0:T(8,128)} %source.3), custom_call_target="tpu_custom_call" | custom-call | tf_op jit(solution)/shard_map/take/pallas_call | solution.py:478
  1.2 0.6 collective-permute-start.5
  1.8 0.1 copy.22.tiles
  1.9 2.3 %setup.1 = (f32[16,8,1024]{2,1,0:T(8,128)S(1)}, f32[16,8,1024]{2,1,0:T(8,128)S(1)}, f32[16,8,1024]{2,1,0:T(8,128)S(1)}, bf16[256,256]{1,0:T(8,128)(2,1)S(1)}, bf16[256,256]{1,0:T(8,128)(2,1)S(1)}) custom-call(s32[4,2]{1,0:T(4,128)S(1)} %copy.22.tiles, s32[1024]{0:T(1024)S(1)} %copy-done.13, f32[128,128]{1,0:T(8,128)S(1)} %copy-done.9, ...), custom_call_target="tpu_custom_call" | custom-call | tf_op jit(solution)/shard_map/setup/pallas_call | solution.py:492
  4.2 0.1 collective-permute-start.4
  4.3 0.5 shard_map.156
  4.8 3.0 %collective-permute-start.6 = (f32[12,8,1024]{2,1,0:T(8,128)S(1)}, f32[12,8,1024]{2,1,0:T(8,128)S(1)}, u32[]{:S(2)}, u32[]{:S(2)}) collective-permute-start(f32[12,8,1024]{2,1,0:T(8,128)S(1)} %get-tuple-element.109.rest_2_), channel_id=1, source_target_pairs={{0,8},{1,9},{2,10},{3,11},{4,20},{5,21},{6,22},{7,23},{8,0},{9,1},... | collective-permute-start | bytes 1179656 | tf_op jit(solution)/shard_map/ppermute | solution.py:468
  7.8 0.5 shard_map.157
  8.3 1.0 %collective-permute-start.8 = (f32[12,8,1024]{2,1,0:T(8,128)S(1)}, f32[12,8,1024]{2,1,0:T(8,128)S(1)}, u32[]{:S(2)}, u32[]{:S(2)}) collective-permute-start(f32[12,8,1024]{2,1,0:T(8,128)S(1)} %get-tuple-element.110.rest_0_), channel_id=1, source_target_pairs={{0,8},{1,9},{2,10},{3,11},{4,20},{5,21},{6,22},{7,23},{8,0},{9,1},... | collective-permute-start | bytes 1179656 | tf_op jit(solution)/shard_map/ppermute | solution.py:468
  9.3 2.7 %ready.1 = (f32[16,8,4096]{2,1,0:T(8,128)}, f32[6,64,128]{2,1,0:T(8,128)S(1)}, f32[8]{0:T(128)S(1)}, s32[32]{0:T(128)S(1)}, s32[1]{0:T(128)}) custom-call(s32[4,2]{1,0:T(4,128)S(1)} %copy.22.tiles, s32[1024]{0:T(1024)S(1)} %copy-done.13, s32[128,128]{1,0:T(8,128)S(1)} %copy-done.10, f32[64,128]{1,0:T(8,128)S(1)} %copy-done.12, ...), custom_call_target="tpu_custom_call" | custom-call | tf_op jit(solution)/shard_map/ready/pallas_call | solution.py:516
  12.0 1.5 %collective-permute-done.6.got = f32[12,8,1024]{2,1,0:T(8,128)S(1)} collective-permute-done((f32[12,8,1024]{2,1,0:T(8,128)S(1)}, f32[12,8,1024]{2,1,0:T(8,128)S(1)}, u32[]{:S(2)}, u32[]{:S(2)}) %collective-permute-start.6) | collective-permute-done | bytes 393248 | tf_op jit(solution)/shard_map/ppermute | solution.py:468
  13.6 2.1 %collective-permute-start.7 = (f32[6,8,1024]{2,1,0:T(8,128)S(1)}, f32[6,8,1024]{2,1,0:T(8,128)S(1)}, u32[]{:S(2)}, u32[]{:S(2)}) collective-permute-start(f32[6,8,1024]{2,1,0:T(8,128)S(1)} %shard_map.158.rest_0_), channel_id=1, source_target_pairs={{0,16},{1,17},{2,18},{3,19},{4,12},{5,13},{6,14},{7,15},{8,24},{9,... | collective-permute-start | bytes 589832 | tf_op jit(solution)/shard_map/ppermute | solution.py:468
  15.7 4.1 %collective-permute-done.8.got = f32[12,8,1024]{2,1,0:T(8,128)S(1)} collective-permute-done((f32[12,8,1024]{2,1,0:T(8,128)S(1)}, f32[12,8,1024]{2,1,0:T(8,128)S(1)}, u32[]{:S(2)}, u32[]{:S(2)}) %collective-permute-start.8) | collective-permute-done | bytes 393248 | tf_op jit(solution)/shard_map/ppermute | solution.py:468
  19.8 2.4 %collective-permute-start.9 = (f32[6,8,1024]{2,1,0:T(8,128)S(1)}, f32[6,8,1024]{2,1,0:T(8,128)S(1)}, u32[]{:S(2)}, u32[]{:S(2)}) collective-permute-start(f32[6,8,1024]{2,1,0:T(8,128)S(1)} %shard_map.159.rest_4_), channel_id=1, source_target_pairs={{0,16},{1,17},{2,18},{3,19},{4,12},{5,13},{6,14},{7,15},{8,24},{9,... | collective-permute-start | bytes 589832 | tf_op jit(solution)/shard_map/ppermute | solution.py:468
  22.3 0.7 %shard_map.160 = (f32[4,8,2048]{2,1,0:T(8,128)S(1)}, f32[4,8,2048]{2,1,0:T(8,128)S(1)}) custom-call(bf16[256,256]{1,0:T(8,128)(2,1)S(1)} %get-tuple-element.104.high, bf16[256,256]{1,0:T(8,128)(2,1)S(1)} %get-tuple-element.105.low, f32[16,8,1024]{2,1,0:T(8,128)S(1)} %get-tuple-element.108.rest_0_, f32[16,8,1024]{2,1,0:T(8,128)S(1)} %collective-permute-done.5.rest_1_, ...), custom_call_target="tpu_custom_call" | custom-call | tf_op jit(solution)/shard_map/pallas_call | solution.py:504
  23.0 1.6 %collective-permute-start.12 = (f32[4,8,2048]{2,1,0:T(8,128)S(1)}, f32[4,8,2048]{2,1,0:T(8,128)S(1)}, u32[]{:S(2)}, u32[]{:S(2)}) collective-permute-start(f32[4,8,2048]{2,1,0:T(8,128)S(1)} %get-tuple-element.117.rest_0_), channel_id=1, source_target_pairs={{0,8},{1,9},{2,10},{3,11},{4,20},{5,21},{6,22},{7,23},{8,0},{9,1},... | collective-permute-start | bytes 786440 | tf_op jit(solution)/shard_map/ppermute | solution.py:468
  24.6 2.5 %collective-permute-done.9.passed = f32[6,8,1024]{2,1,0:T(8,128)S(1)} collective-permute-done((f32[6,8,1024]{2,1,0:T(8,128)S(1)}, f32[6,8,1024]{2,1,0:T(8,128)S(1)}, u32[]{:S(2)}, u32[]{:S(2)}) %collective-permute-start.9) | collective-permute-done | bytes 196640 | tf_op jit(solution)/shard_map/ppermute | solution.py:468
  27.1 0.1 collective-permute-start.11
  27.2 0.5 collective-permute-start.10
  27.7 1.7 %collective-permute-done.12.got = f32[4,8,2048]{2,1,0:T(8,128)S(1)} collective-permute-done((f32[4,8,2048]{2,1,0:T(8,128)S(1)}, f32[4,8,2048]{2,1,0:T(8,128)S(1)}, u32[]{:S(2)}, u32[]{:S(2)}) %collective-permute-start.12) | collective-permute-done | bytes 262176 | tf_op jit(solution)/shard_map/ppermute | solution.py:468
  29.5 0.1 collective-permute-start.20
  29.6 1.1 %shard_map.164 = (f32[64,256]{1,0:T(8,128)S(1)}, f32[512,256]{1,0:T(8,128)S(1)}, f32[64,256]{1,0:T(8,128)S(1)}, f32[64,256]{1,0:T(8,128)S(1)}) custom-call(f32[6,8,1024]{2,1,0:T(8,128)S(1)} %shard_map.161.rest_0_.refs_0_, f32[6,8,1024]{2,1,0:T(8,128)S(1)} %shard_map.162.rest_0_.refs_1_, f32[6,8,1024]{2,1,0:T(8,128)S(1)} %collective-permute-done.10.refs_2_, ...), custom_call_target="tpu_custom_call" | custom-call | tf_op jit(solution)/shard_map/pallas_call | solution.py:576
  30.8 3.7 %collective-permute-done.20.passed = f32[2,8,2048]{2,1,0:T(8,128)S(1)} collective-permute-done((f32[2,8,2048]{2,1,0:T(8,128)S(1)}, f32[2,8,2048]{2,1,0:T(8,128)S(1)}, u32[]{:S(2)}, u32[]{:S(2)}) %collective-permute-start.20) | collective-permute-done | bytes 131104 | tf_op jit(solution)/shard_map/ppermute | solution.py:468
  34.6 0.1 collective-permute-start.21
  34.7 1.6 %collective-permute-start.13 = (f32[64,256]{1,0:T(8,128)S(1)}, f32[64,256]{1,0:T(8,128)S(1)}, u32[]{:S(2)}, u32[]{:S(2)}) collective-permute-start(f32[64,256]{1,0:T(8,128)S(1)} %get-tuple-element.120), channel_id=1, source_target_pairs={{0,1},{1,0},{2,3},{3,2},{4,5},{5,4},{6,7},{7,6},{8,9},{9,8},{10,11... | collective-permute-start | bytes 196616 | tf_op jit(solution)/shard_map/ppermute | solution.py:471
  36.3 1.1 %shard_map.169 = (f32[64,256]{1,0:T(8,128)S(1)}, f32[512,256]{1,0:T(8,128)S(1)}, f32[64,256]{1,0:T(8,128)S(1)}, f32[64,256]{1,0:T(8,128)S(1)}) custom-call(f32[6,8,1024]{2,1,0:T(8,128)S(1)} %shard_map.161.rest_0_.refs_0_, f32[6,8,1024]{2,1,0:T(8,128)S(1)} %shard_map.162.rest_0_.refs_1_, f32[6,8,1024]{2,1,0:T(8,128)S(1)} %collective-permute-done.10.refs_2_, ...), custom_call_target="tpu_custom_call" | custom-call | tf_op jit(solution)/shard_map/pallas_call | solution.py:576
  37.5 1.3 %collective-permute-start.22 = (f32[64,256]{1,0:T(8,128)S(1)}, f32[64,256]{1,0:T(8,128)S(1)}, u32[]{:S(2)}, u32[]{:S(2)}) collective-permute-start(f32[64,256]{1,0:T(8,128)S(1)} %get-tuple-element.124), channel_id=1, source_target_pairs={{0,1},{1,0},{2,3},{3,2},{4,5},{5,4},{6,7},{7,6},{8,9},{9,8},{10,11... | collective-permute-start | bytes 196616 | tf_op jit(solution)/shard_map/ppermute | solution.py:471
  38.8 0.4 collective-permute-done.13.got.refs_4_
  39.2 0.7 %collective-permute-start.14 = (f32[64,256]{1,0:T(8,128)S(1)}, f32[64,256]{1,0:T(8,128)S(1)}, u32[]{:S(2)}, u32[]{:S(2)}) collective-permute-start(f32[64,256]{1,0:T(8,128)S(1)} %shard_map.165), channel_id=1, source_target_pairs={{0,0},{1,2},{2,1},{3,3},{4,4},{5,6},{6,5},{7,7},{8,8},{9,10},{10,9... | collective-permute-start | bytes 196616 | tf_op jit(solution)/shard_map/ppermute | solution.py:471
  39.9 1.9 %collective-permute-done.22.got.refs_4_ = f32[64,256]{1,0:T(8,128)S(1)} collective-permute-done((f32[64,256]{1,0:T(8,128)S(1)}, f32[64,256]{1,0:T(8,128)S(1)}, u32[]{:S(2)}, u32[]{:S(2)}) %collective-permute-start.22) | collective-permute-done | bytes 65568 | tf_op jit(solution)/shard_map/ppermute | solution.py:471
  41.8 0.7 %collective-permute-start.23 = (f32[64,256]{1,0:T(8,128)S(1)}, f32[64,256]{1,0:T(8,128)S(1)}, u32[]{:S(2)}, u32[]{:S(2)}) collective-permute-start(f32[64,256]{1,0:T(8,128)S(1)} %shard_map.170), channel_id=1, source_target_pairs={{0,0},{1,2},{2,1},{3,3},{4,4},{5,6},{6,5},{7,7},{8,8},{9,10},{10,9... | collective-permute-start | bytes 196616 | tf_op jit(solution)/shard_map/ppermute | solution.py:471
  42.5 4.5 %collective-permute-start.15 = (f32[64,256]{1,0:T(8,128)S(1)}, f32[64,256]{1,0:T(8,128)S(1)}, u32[]{:S(2)}, u32[]{:S(2)}) collective-permute-start(f32[64,256]{1,0:T(8,128)S(1)} %collective-permute-done.14.refs_5_), channel_id=1, source_target_pairs={{0,1},{1,0},{2,3},{3,2},{4,5},{5,4},{6,7},{7,6},{8,9},{9,8},{10,11... | collective-permute-start | bytes 196616 | tf_op jit(solution)/shard_map/ppermute | solution.py:471
  47.0 3.5 %collective-permute-start.24 = (f32[64,256]{1,0:T(8,128)S(1)}, f32[64,256]{1,0:T(8,128)S(1)}, u32[]{:S(2)}, u32[]{:S(2)}) collective-permute-start(f32[64,256]{1,0:T(8,128)S(1)} %collective-permute-done.23.refs_5_), channel_id=1, source_target_pairs={{0,1},{1,0},{2,3},{3,2},{4,5},{5,4},{6,7},{7,6},{8,9},{9,8},{10,11... | collective-permute-start | bytes 196616 | tf_op jit(solution)/shard_map/ppermute | solution.py:471
  50.5 2.2 %shard_map.166.refs_18_ = f32[8,4096]{1,0:T(8,128)S(1)} custom-call(f32[8]{0:T(128)S(1)} %get-tuple-element.113.flags, f32[6,8,1024]{2,1,0:T(8,128)S(1)} %shard_map.161.rest_0_.refs_0_, f32[6,8,1024]{2,1,0:T(8,128)S(1)} %shard_map.162.rest_0_.refs_1_, f32[6,8,1024]{2,1,0:T(8,128)S(1)} %collective-permute-done.10.refs_2_, ...), custom_call_target="tpu_custom_call" | custom-call | tf_op jit(solution)/shard_map/pallas_call | solution.py:597
  52.7 0.6 collective-permute-start.17
  53.3 1.5 %collective-permute-start.16 = (f32[8,4096]{1,0:T(8,128)S(1)}, f32[8,4096]{1,0:T(8,128)S(1)}, u32[]{:S(2)}, u32[]{:S(2)}) collective-permute-start(f32[8,4096]{1,0:T(8,128)S(1)} %shard_map.166.refs_18_), channel_id=1, source_target_pairs={{0,8},{1,9},{2,10},{3,11},{4,20},{5,21},{6,22},{7,23},{8,0},{9,1},... | collective-permute-start | bytes 393224 | tf_op jit(solution)/shard_map/ppermute | solution.py:468
  54.8 2.2 %shard_map.171 = f32[8,4096]{1,0:T(8,128)S(1)} custom-call(f32[8]{0:T(128)S(1)} %get-tuple-element.113.flags, f32[6,8,1024]{2,1,0:T(8,128)S(1)} %shard_map.161.rest_0_.refs_0_, f32[6,8,1024]{2,1,0:T(8,128)S(1)} %shard_map.162.rest_0_.refs_1_, f32[6,8,1024]{2,1,0:T(8,128)S(1)} %collective-permute-done.10.refs_2_, ...), custom_call_target="tpu_custom_call" | custom-call | tf_op jit(solution)/shard_map/pallas_call | solution.py:597
  57.0 1.6 %collective-permute-start.26 = (f32[8,4096]{1,0:T(8,128)S(1)}, f32[8,4096]{1,0:T(8,128)S(1)}, u32[]{:S(2)}, u32[]{:S(2)}) collective-permute-start(f32[8,4096]{1,0:T(8,128)S(1)} %shard_map.171), channel_id=1, source_target_pairs={{0,16},{1,17},{2,18},{3,19},{4,12},{5,13},{6,14},{7,15},{8,24},{9,... | collective-permute-start | bytes 393224 | tf_op jit(solution)/shard_map/ppermute | solution.py:468
  58.6 0.5 collective-permute-start.25
  59.1 0.5 collective-permute-done.16.x
  59.6 2.4 %collective-permute-done.26.y = f32[8,4096]{1,0:T(8,128)S(1)} collective-permute-done((f32[8,4096]{1,0:T(8,128)S(1)}, f32[8,4096]{1,0:T(8,128)S(1)}, u32[]{:S(2)}, u32[]{:S(2)}) %collective-permute-start.26) | collective-permute-done | bytes 131104 | tf_op jit(solution)/shard_map/ppermute | solution.py:468
  62.0 1.5 %collective-permute-done.25.x = f32[8,4096]{1,0:T(8,128)S(1)} collective-permute-done((f32[8,4096]{1,0:T(8,128)S(1)}, f32[8,4096]{1,0:T(8,128)S(1)}, u32[]{:S(2)}, u32[]{:S(2)}) %collective-permute-start.25) | collective-permute-done | bytes 131104 | tf_op jit(solution)/shard_map/ppermute | solution.py:468
  63.6 0.5 collective-permute-start.18
  64.1 0.1 collective-permute-start.27
  64.8 0.6 collective-permute-done.18
  65.3 0.2 collective-permute-done.27
  65.5 0.7 %conditional.1 = (f32[16,8,4096]{2,1,0:T(8,128)}) conditional(s32[]{:T(128)} %bitcast, (s32[32]{0:T(128)S(1)}, f32[8,4096]{1,0:T(8,128)S(1)}, f32[8,4096]{1,0:T(8,128)S(1)}, f32[8,4096]{1,0:T(8,128)S(1)}, f32[8,4096]{1,0:T(8,128)S(1)}, /*index=5*/f32[2,8,4096]{2,1,0:T(8,128)S(1)}, f32[8,4096]{1,0:T(8,128)S(1)}, f32[8,4096]{1,0:T(8,128)S(1)}, ...), branch_computations={%region_0.0_spmd, %region_1.0_spmd} | conditional | bytes 2097320 | solution.py:638
  65.5 0.7 %place.2 = f32[16,8,4096]{2,1,0:T(8,128)} custom-call(s32[32]{0:T(128)S(1)} %get-tuple-element.56.match, f32[8,4096]{1,0:T(8,128)S(1)} %get-tuple-element.57.refs_0_, f32[8,4096]{1,0:T(8,128)S(1)} %get-tuple-element.58.refs_1_, f32[8,4096]{1,0:T(8,128)S(1)} %get-tuple-element.59.refs_2_, ...), custom_call_target="tpu_custom_call", output_to_operand_aliasing={{}: (11, {})} | custom-call | tf_op jit(solution)/shard_map/cond/branch_0_fun/place/pallas_call | solution.py:620
  (55 shorter events, 0.5 us)
Async XLA Ops:
  0.0 1.9 %copy-start.13 = (s32[1024]{0:T(1024)S(1)}, s32[1024]{0:T(1024)}, u32[]{:S(2)}) copy-start(s32[1024]{0:T(1024)} %constant.27.clone.host) | copy-start | bytes 12292
  0.0 1.8 %copy-start.14 = (s32[4,2]{0,1:T(2,128)S(1)}, s32[4,2]{0,1:T(2,128)}, u32[]{:S(2)}) copy-start(s32[4,2]{0,1:T(2,128)} %param.20) | copy-start | bytes 100
  0.0 1.8 %copy-start.9 = (f32[128,128]{1,0:T(8,128)S(1)}, f32[128,128]{1,0:T(8,128)}, u32[]{:S(2)}) copy-start(f32[128,128]{1,0:T(8,128)} %rotation.1) | copy-start | bytes 196612
  1.2 3.1 %collective-permute-start.5 = (f32[16,8,1024]{2,1,0:T(8,128)S(1)}, f32[16,8,1024]{2,1,0:T(8,128)S(1)}, u32[]{:S(2)}, u32[]{:S(2)}) collective-permute-start(f32[16,8,1024]{2,1,0:T(8,128)S(1)} %take.1.after), channel_id=1, source_target_pairs={{0,4},{1,5},{2,6},{3,7},{4,0},{5,1},{6,2},{7,3},{8,12},{9,13},{10,... | collective-permute-start | bytes 1572872 | tf_op jit(solution)/shard_map/ppermute | solution.py:468
  4.2 5.2 %copy-start.10 = (s32[128,128]{1,0:T(8,128)S(1)}, s32[128,128]{1,0:T(8,128)}, u32[]{:S(2)}) copy-start(s32[128,128]{1,0:T(8,128)} %mask.1) | copy-start | bytes 196612
  4.2 5.2 %copy-start.12 = (f32[64,128]{1,0:T(8,128)S(1)}, f32[64,128]{1,0:T(8,128)}, u32[]{:S(2)}) copy-start(f32[64,128]{1,0:T(8,128)} %constant.28.clone.log_r) | copy-start | bytes 98308
  4.2 3.6 %collective-permute-start.4 = (f32[16,8,1024]{2,1,0:T(8,128)S(1)}, f32[16,8,1024]{2,1,0:T(8,128)S(1)}, u32[]{:S(2)}, u32[]{:S(2)}) collective-permute-start(f32[16,8,1024]{2,1,0:T(8,128)S(1)} %get-tuple-element.107), channel_id=1, source_target_pairs={{0,4},{1,5},{2,6},{3,7},{4,0},{5,1},{6,2},{7,3},{8,12},{9,13},{10,... | collective-permute-start | bytes 1572872 | tf_op jit(solution)/shard_map/ppermute | solution.py:468
  4.8 8.8 %collective-permute-start.6 = (f32[12,8,1024]{2,1,0:T(8,128)S(1)}, f32[12,8,1024]{2,1,0:T(8,128)S(1)}, u32[]{:S(2)}, u32[]{:S(2)}) collective-permute-start(f32[12,8,1024]{2,1,0:T(8,128)S(1)} %get-tuple-element.109.rest_2_), channel_id=1, source_target_pairs={{0,8},{1,9},{2,10},{3,11},{4,20},{5,21},{6,22},{7,23},{8,0},{9,1},... | collective-permute-start | bytes 1179656 | tf_op jit(solution)/shard_map/ppermute | solution.py:468
  8.3 11.5 %collective-permute-start.8 = (f32[12,8,1024]{2,1,0:T(8,128)S(1)}, f32[12,8,1024]{2,1,0:T(8,128)S(1)}, u32[]{:S(2)}, u32[]{:S(2)}) collective-permute-start(f32[12,8,1024]{2,1,0:T(8,128)S(1)} %get-tuple-element.110.rest_0_), channel_id=1, source_target_pairs={{0,8},{1,9},{2,10},{3,11},{4,20},{5,21},{6,22},{7,23},{8,0},{9,1},... | collective-permute-start | bytes 1179656 | tf_op jit(solution)/shard_map/ppermute | solution.py:468
  13.6 11.0 %collective-permute-start.7 = (f32[6,8,1024]{2,1,0:T(8,128)S(1)}, f32[6,8,1024]{2,1,0:T(8,128)S(1)}, u32[]{:S(2)}, u32[]{:S(2)}) collective-permute-start(f32[6,8,1024]{2,1,0:T(8,128)S(1)} %shard_map.158.rest_0_), channel_id=1, source_target_pairs={{0,16},{1,17},{2,18},{3,19},{4,12},{5,13},{6,14},{7,15},{8,24},{9,... | collective-permute-start | bytes 589832 | tf_op jit(solution)/shard_map/ppermute | solution.py:468
  19.8 7.3 %collective-permute-start.9 = (f32[6,8,1024]{2,1,0:T(8,128)S(1)}, f32[6,8,1024]{2,1,0:T(8,128)S(1)}, u32[]{:S(2)}, u32[]{:S(2)}) collective-permute-start(f32[6,8,1024]{2,1,0:T(8,128)S(1)} %shard_map.159.rest_4_), channel_id=1, source_target_pairs={{0,16},{1,17},{2,18},{3,19},{4,12},{5,13},{6,14},{7,15},{8,24},{9,... | collective-permute-start | bytes 589832 | tf_op jit(solution)/shard_map/ppermute | solution.py:468
  23.0 6.6 %copy-start = (bf16[512,512]{1,0:T(8,128)(2,1)S(1)}, bf16[512,512]{1,0:T(8,128)(2,1)}, u32[]{:S(2)}) copy-start(bf16[512,512]{1,0:T(8,128)(2,1)} %constant.34.clone.refs_5_.refs_8_.refs_7_) | copy-start | bytes 1572868
  23.0 6.6 %copy-start.1 = (bf16[512,512]{1,0:T(8,128)(2,1)S(1)}, bf16[512,512]{1,0:T(8,128)(2,1)}, u32[]{:S(2)}) copy-start(bf16[512,512]{1,0:T(8,128)(2,1)} %constant.33.clone.refs_4_.refs_7_.refs_6_) | copy-start | bytes 1572868
  23.0 6.6 %copy-start.4 = (f32[512,128]{1,0:T(8,128)S(1)}, f32[512,128]{1,0:T(8,128)}, u32[]{:S(2)}) copy-start(f32[512,128]{1,0:T(8,128)} %constant.29.clone.refs_8_.refs_10_) | copy-start | bytes 786436
  23.0 6.6 %copy-start.7 = (bf16[256,256]{1,0:T(8,128)(2,1)S(1)}, bf16[256,256]{1,0:T(8,128)(2,1)}, u32[]{:S(2)}) copy-start(bf16[256,256]{1,0:T(8,128)(2,1)} %constant.36.clone.refs_7_.refs_9_) | copy-start | bytes 393220
  23.0 6.6 %copy-start.8 = (bf16[256,256]{1,0:T(8,128)(2,1)S(1)}, bf16[256,256]{1,0:T(8,128)(2,1)}, u32[]{:S(2)}) copy-start(bf16[256,256]{1,0:T(8,128)(2,1)} %constant.35.clone.refs_6_.refs_8_) | copy-start | bytes 393220
  23.0 6.4 %collective-permute-start.12 = (f32[4,8,2048]{2,1,0:T(8,128)S(1)}, f32[4,8,2048]{2,1,0:T(8,128)S(1)}, u32[]{:S(2)}, u32[]{:S(2)}) collective-permute-start(f32[4,8,2048]{2,1,0:T(8,128)S(1)} %get-tuple-element.117.rest_0_), channel_id=1, source_target_pairs={{0,8},{1,9},{2,10},{3,11},{4,20},{5,21},{6,22},{7,23},{8,0},{9,1},... | collective-permute-start | bytes 786440 | tf_op jit(solution)/shard_map/ppermute | solution.py:468
  27.1 2.4 %collective-permute-start.11 = (f32[6,8,1024]{2,1,0:T(8,128)S(1)}, f32[6,8,1024]{2,1,0:T(8,128)S(1)}, u32[]{:S(2)}, u32[]{:S(2)}) collective-permute-start(f32[6,8,1024]{2,1,0:T(8,128)S(1)} %shard_map.162.rest_0_.refs_1_), channel_id=1, source_target_pairs={{0,4},{1,5},{2,6},{3,7},{4,0},{5,1},{6,2},{7,3},{8,12},{9,13},{10,... | collective-permute-start | bytes 589832 | tf_op jit(solution)/shard_map/ppermute | solution.py:468
  27.2 2.4 %collective-permute-start.10 = (f32[6,8,1024]{2,1,0:T(8,128)S(1)}, f32[6,8,1024]{2,1,0:T(8,128)S(1)}, u32[]{:S(2)}, u32[]{:S(2)}) collective-permute-start(f32[6,8,1024]{2,1,0:T(8,128)S(1)} %shard_map.161.rest_0_.refs_0_), channel_id=1, source_target_pairs={{0,4},{1,5},{2,6},{3,7},{4,0},{5,1},{6,2},{7,3},{8,12},{9,13},{10,... | collective-permute-start | bytes 589832 | tf_op jit(solution)/shard_map/ppermute | solution.py:468
  29.5 5.0 %collective-permute-start.20 = (f32[2,8,2048]{2,1,0:T(8,128)S(1)}, f32[2,8,2048]{2,1,0:T(8,128)S(1)}, u32[]{:S(2)}, u32[]{:S(2)}) collective-permute-start(f32[2,8,2048]{2,1,0:T(8,128)S(1)} %shard_map.163.refs_10_), channel_id=1, source_target_pairs={{0,16},{1,17},{2,18},{3,19},{4,12},{5,13},{6,14},{7,15},{8,24},{9,... | collective-permute-start | bytes 393224 | tf_op jit(solution)/shard_map/ppermute | solution.py:468
  34.5 4.7 %copy-start.2 = (f32[3,64,128]{2,1,0:T(8,128)S(1)}, f32[3,64,128]{2,1,0:T(8,128)}, u32[]{:S(2)}) copy-start(f32[3,64,128]{2,1,0:T(8,128)} %constant.32.clone.steady.refs_14_) | copy-start | bytes 294916
  34.5 15.9 %copy-start.3 = (f32[512,128]{1,0:T(8,128)S(1)}, f32[512,128]{1,0:T(8,128)}, u32[]{:S(2)}) copy-start(f32[512,128]{1,0:T(8,128)} %constant.30.clone.refs_11_) | copy-start | bytes 786436
  34.5 15.9 %copy-start.5 = (bf16[256,256]{1,0:T(8,128)(2,1)S(1)}, bf16[256,256]{1,0:T(8,128)(2,1)}, u32[]{:S(2)}) copy-start(bf16[256,256]{1,0:T(8,128)(2,1)} %constant.38.clone.refs_10_) | copy-start | bytes 393220
  34.6 15.9 %copy-start.6 = (bf16[256,256]{1,0:T(8,128)(2,1)S(1)}, bf16[256,256]{1,0:T(8,128)(2,1)}, u32[]{:S(2)}) copy-start(bf16[256,256]{1,0:T(8,128)(2,1)} %constant.37.clone.refs_9_) | copy-start | bytes 393220
  34.6 15.9 %copy-start.11 = (f32[2,8,128]{2,1,0:T(8,128)S(1)}, f32[2,8,128]{2,1,0:T(8,128)}, u32[]{:S(2)}) copy-start(f32[2,8,128]{2,1,0:T(8,128)} %constant.31.clone.refs_12_) | copy-start | bytes 24580
  34.6 1.7 %collective-permute-start.21 = (f32[2,8,2048]{2,1,0:T(8,128)S(1)}, f32[2,8,2048]{2,1,0:T(8,128)S(1)}, u32[]{:S(2)}, u32[]{:S(2)}) collective-permute-start(f32[2,8,2048]{2,1,0:T(8,128)S(1)} %shard_map.168.refs_4_), channel_id=1, source_target_pairs={{0,4},{1,5},{2,6},{3,7},{4,0},{5,1},{6,2},{7,3},{8,12},{9,13},{10,... | collective-permute-start | bytes 393224 | tf_op jit(solution)/shard_map/ppermute | solution.py:468
  34.7 4.5 %collective-permute-start.13 = (f32[64,256]{1,0:T(8,128)S(1)}, f32[64,256]{1,0:T(8,128)S(1)}, u32[]{:S(2)}, u32[]{:S(2)}) collective-permute-start(f32[64,256]{1,0:T(8,128)S(1)} %get-tuple-element.120), channel_id=1, source_target_pairs={{0,1},{1,0},{2,3},{3,2},{4,5},{5,4},{6,7},{7,6},{8,9},{9,8},{10,11... | collective-permute-start | bytes 196616 | tf_op jit(solution)/shard_map/ppermute | solution.py:471
  37.5 4.3 %collective-permute-start.22 = (f32[64,256]{1,0:T(8,128)S(1)}, f32[64,256]{1,0:T(8,128)S(1)}, u32[]{:S(2)}, u32[]{:S(2)}) collective-permute-start(f32[64,256]{1,0:T(8,128)S(1)} %get-tuple-element.124), channel_id=1, source_target_pairs={{0,1},{1,0},{2,3},{3,2},{4,5},{5,4},{6,7},{7,6},{8,9},{9,8},{10,11... | collective-permute-start | bytes 196616 | tf_op jit(solution)/shard_map/ppermute | solution.py:471
  39.2 3.3 %collective-permute-start.14 = (f32[64,256]{1,0:T(8,128)S(1)}, f32[64,256]{1,0:T(8,128)S(1)}, u32[]{:S(2)}, u32[]{:S(2)}) collective-permute-start(f32[64,256]{1,0:T(8,128)S(1)} %shard_map.165), channel_id=1, source_target_pairs={{0,0},{1,2},{2,1},{3,3},{4,4},{5,6},{6,5},{7,7},{8,8},{9,10},{10,9... | collective-permute-start | bytes 196616 | tf_op jit(solution)/shard_map/ppermute | solution.py:471
  41.8 5.2 %collective-permute-start.23 = (f32[64,256]{1,0:T(8,128)S(1)}, f32[64,256]{1,0:T(8,128)S(1)}, u32[]{:S(2)}, u32[]{:S(2)}) collective-permute-start(f32[64,256]{1,0:T(8,128)S(1)} %shard_map.170), channel_id=1, source_target_pairs={{0,0},{1,2},{2,1},{3,3},{4,4},{5,6},{6,5},{7,7},{8,8},{9,10},{10,9... | collective-permute-start | bytes 196616 | tf_op jit(solution)/shard_map/ppermute | solution.py:471
  42.5 8.0 %collective-permute-start.15 = (f32[64,256]{1,0:T(8,128)S(1)}, f32[64,256]{1,0:T(8,128)S(1)}, u32[]{:S(2)}, u32[]{:S(2)}) collective-permute-start(f32[64,256]{1,0:T(8,128)S(1)} %collective-permute-done.14.refs_5_), channel_id=1, source_target_pairs={{0,1},{1,0},{2,3},{3,2},{4,5},{5,4},{6,7},{7,6},{8,9},{9,8},{10,11... | collective-permute-start | bytes 196616 | tf_op jit(solution)/shard_map/ppermute | solution.py:471
  47.0 7.8 %collective-permute-start.24 = (f32[64,256]{1,0:T(8,128)S(1)}, f32[64,256]{1,0:T(8,128)S(1)}, u32[]{:S(2)}, u32[]{:S(2)}) collective-permute-start(f32[64,256]{1,0:T(8,128)S(1)} %collective-permute-done.23.refs_5_), channel_id=1, source_target_pairs={{0,1},{1,0},{2,3},{3,2},{4,5},{5,4},{6,7},{7,6},{8,9},{9,8},{10,11... | collective-permute-start | bytes 196616 | tf_op jit(solution)/shard_map/ppermute | solution.py:471
  52.7 6.4 %collective-permute-start.17 = (f32[8,4096]{1,0:T(8,128)S(1)}, f32[8,4096]{1,0:T(8,128)S(1)}, u32[]{:S(2)}, u32[]{:S(2)}) collective-permute-start(f32[8,4096]{1,0:T(8,128)S(1)} %shard_map.166.refs_18_), channel_id=1, source_target_pairs={{0,16},{1,17},{2,18},{3,19},{4,12},{5,13},{6,14},{7,15},{8,24},{9,... | collective-permute-start | bytes 393224 | tf_op jit(solution)/shard_map/ppermute | solution.py:468
  53.3 6.3 %collective-permute-start.16 = (f32[8,4096]{1,0:T(8,128)S(1)}, f32[8,4096]{1,0:T(8,128)S(1)}, u32[]{:S(2)}, u32[]{:S(2)}) collective-permute-start(f32[8,4096]{1,0:T(8,128)S(1)} %shard_map.166.refs_18_), channel_id=1, source_target_pairs={{0,8},{1,9},{2,10},{3,11},{4,20},{5,21},{6,22},{7,23},{8,0},{9,1},... | collective-permute-start | bytes 393224 | tf_op jit(solution)/shard_map/ppermute | solution.py:468
  57.0 5.0 %collective-permute-start.26 = (f32[8,4096]{1,0:T(8,128)S(1)}, f32[8,4096]{1,0:T(8,128)S(1)}, u32[]{:S(2)}, u32[]{:S(2)}) collective-permute-start(f32[8,4096]{1,0:T(8,128)S(1)} %shard_map.171), channel_id=1, source_target_pairs={{0,16},{1,17},{2,18},{3,19},{4,12},{5,13},{6,14},{7,15},{8,24},{9,... | collective-permute-start | bytes 393224 | tf_op jit(solution)/shard_map/ppermute | solution.py:468
  58.6 5.0 %collective-permute-start.25 = (f32[8,4096]{1,0:T(8,128)S(1)}, f32[8,4096]{1,0:T(8,128)S(1)}, u32[]{:S(2)}, u32[]{:S(2)}) collective-permute-start(f32[8,4096]{1,0:T(8,128)S(1)} %shard_map.171), channel_id=1, source_target_pairs={{0,8},{1,9},{2,10},{3,11},{4,20},{5,21},{6,22},{7,23},{8,0},{9,1},... | collective-permute-start | bytes 393224 | tf_op jit(solution)/shard_map/ppermute | solution.py:468
  59.6 6.0 %collective-permute-start.19 = (f32[2,8,4096]{2,1,0:T(8,128)S(1)}, f32[2,8,4096]{2,1,0:T(8,128)S(1)}, u32[]{:S(2)}, u32[]{:S(2)}) collective-permute-start(f32[2,8,4096]{2,1,0:T(8,128)S(1)} %shard_map.167), channel_id=1, source_target_pairs={{0,4},{1,5},{2,6},{3,7},{4,0},{5,1},{6,2},{7,3},{8,12},{9,13},{10,... | collective-permute-start | bytes 786440 | tf_op jit(solution)/shard_map/ppermute | solution.py:468
  63.5 2.0 %collective-permute-start.28 = (f32[2,8,4096]{2,1,0:T(8,128)S(1)}, f32[2,8,4096]{2,1,0:T(8,128)S(1)}, u32[]{:S(2)}, u32[]{:S(2)}) collective-permute-start(f32[2,8,4096]{2,1,0:T(8,128)S(1)} %shard_map.172), channel_id=1, source_target_pairs={{0,4},{1,5},{2,6},{3,7},{4,0},{5,1},{6,2},{7,3},{8,12},{9,13},{10,... | collective-permute-start | bytes 786440 | tf_op jit(solution)/shard_map/ppermute | solution.py:468
  63.6 1.7 %collective-permute-start.18 = (f32[8,4096]{1,0:T(8,128)S(1)}, f32[8,4096]{1,0:T(8,128)S(1)}, u32[]{:S(2)}, u32[]{:S(2)}) collective-permute-start(f32[8,4096]{1,0:T(8,128)S(1)} %shard_map.166.refs_18_), channel_id=1, source_target_pairs={{0,4},{1,5},{2,6},{3,7},{4,0},{5,1},{6,2},{7,3},{8,12},{9,13},{10,... | collective-permute-start | bytes 393224 | tf_op jit(solution)/shard_map/ppermute | solution.py:468
  64.1 1.4 %collective-permute-start.27 = (f32[8,4096]{1,0:T(8,128)S(1)}, f32[8,4096]{1,0:T(8,128)S(1)}, u32[]{:S(2)}, u32[]{:S(2)}) collective-permute-start(f32[8,4096]{1,0:T(8,128)S(1)} %shard_map.171), channel_id=1, source_target_pairs={{0,4},{1,5},{2,6},{3,7},{4,0},{5,1},{6,2},{7,3},{8,12},{9,13},{10,... | collective-permute-start | bytes 393224 | tf_op jit(solution)/shard_map/ppermute | solution.py:468
